TPU v7x, 256 devices: a whole 4x4x8 slice. The times are simulated.
256 devices in a mesh: expert: 4 (over z_lo), etp: 16 (over y, x), tp: 4 (over z_hi, core).
Axes of the slice: x: 4, y: 4, z: 8 (z_hi: 2, z_lo: 4; z = z_hi * 4 + z_lo), core: 2. Of those that a mesh axis runs over, the one named last changes fastest.
Arguments:
- d_out: bfloat16 [2048, 6144], P(('expert', 'tp'), 'etp'), may hold values from -6 to 6
- expert_ids: int32 [2048, 2], P(('expert', 'tp')), may hold values from 0 to 3, all different within a row; in each aligned block of 128 rows (0 to 127, 128 to 255, ...) at most 64 rows name the same one
- gate_weights: float32 [2048, 2], P(('expert', 'tp')), may hold values from 0.05 to 0.95, as said below
- saved_gate: bfloat16 [4, 1024, 16384], P('expert', None, ('etp', 'tp')), may hold values from -8 to 8
- saved_up: bfloat16 [4, 1024, 16384], P('expert', None, ('etp', 'tp')), may hold values from -6 to 6
- w_gate: bfloat16 [4, 6144, 16384], P('expert', None, ('etp', 'tp')), may hold values from -0.078125 to 0.078125
- w_up: bfloat16 [4, 6144, 16384], P('expert', None, ('etp', 'tp')), may hold values from -0.078125 to 0.078125
- w_down: bfloat16 [4, 16384, 6144], P('expert', ('etp', 'tp')), may hold values from -0.046875 to 0.046875
- w_out: bfloat16 [6144, 6144], P('tp', 'etp'), may hold values from -0.078125 to 0.078125
Outputs:
- d_hidden: bfloat16 [2048, 6144], P(('expert', 'tp'), 'etp')
- d_heads: bfloat16 [2048, 6144], P(('expert', 'etp'), 'tp')
Inputs may be any that keep to these rules, and one draw needn't show every extreme that they name: `expert_ids`: each token names two different experts; in every block of 128 tokens every expert is named by exactly 64 tokens. `gate_weights`: a token's two weights sum to one.
All inputs are finite; a program needn't handle non-finite values.
Results may differ from a plain program's by a relative error of at most 0.02.
Values may be sent and summed in bfloat16 or wider, within the bound.
No kernel may reach another device: no remote copies, remote signals or barrier semaphores. Data moves between devices by JAX's collectives and lax.ppermute only.
A program may use at most 128 MiB of HBM per device.

v0:
```python
import functools

import jax
import jax.numpy as jnp
from jax import lax
from jax.experimental import pallas as pl
from jax.experimental.pallas import tpu as pltpu
from jax.sharding import PartitionSpec as P


BF = jnp.bfloat16
F32 = jnp.float32
I32 = jnp.int32

NN = (((1,), (0,)), ((), ()))
NT = (((1,), (1,)), ((), ()))
VM = pl.BlockSpec(memory_space=pltpu.VMEM)
SM = pl.BlockSpec(memory_space=pltpu.SMEM)


CHUNKS = (0, 1, 3, 2)


def room(mib):
    return pltpu.CompilerParams(vmem_limit_bytes=mib << 20)


def shape(dims, kind=BF):
    return jax.ShapeDtypeStruct(dims, kind)


def shift_plane(value, step, first):
    pairs = []
    for y in range(4):
        for x in range(4):
            for t in range(4):
                along_x = (t % 2 == 0) == first
                to_y = y if along_x else (y + step) % 4
                to_x = (x + step) % 4 if along_x else x
                pairs.append((16 * y + 4 * x + t, 16 * to_y + 4 * to_x + t))
    return lax.ppermute(value, ("etp", "tp"), pairs)


def shift_z(value, step):
    pairs = []
    for low in range(4):
        for high in range(2):
            for core in range(2):
                to = (4 * high + low + (step if core == 0 else -step)) % 8
                pairs.append((4 * low + 2 * high + core, 4 * (to % 4) + 2 * (to // 4) + core))
    return lax.ppermute(value, ("expert", "tp"), pairs)


def swap_core(value):
    return lax.ppermute(value, "tp", [(t, t ^ 1) for t in range(4)])


def dispatch_kernel(pos, ids, gates, grads, near, far, sel_out):
    expert = (pos[0] + pos[1] * lax.broadcasted_iota(I32, (8, 128), 0)) & 3
    hit0 = ids[0:1, :] == expert
    hit1 = ids[1:2, :] == expert
    zero = jnp.zeros((8, 128), F32)
    member = jnp.where(hit0 | hit1, 1.0, zero)
    weight = jnp.where(hit0, gates[0:1, :], zero) + jnp.where(hit1, gates[1:2, :], zero)
    before = lax.broadcasted_iota(I32, (128, 128), 0) < lax.broadcasted_iota(I32, (128, 128), 1)
    before = jnp.where(before, 1.0, jnp.zeros((128, 128), F32)).astype(BF)
    slot = jnp.dot(member.astype(BF), before, preferred_element_type=F32)
    slot_iota = lax.broadcasted_iota(I32, (64, 128), 0).astype(F32)
    for s in range(4):
        sel = jnp.where(slot[s : s + 1, :] == slot_iota, member[s : s + 1, :], 0.0)
        sel_bf = sel.astype(BF)
        rows = jnp.dot(sel_bf, grads[...], preferred_element_type=F32)
        row_weight = jnp.sum(sel * weight[s : s + 1, :], axis=1, keepdims=True)
        rows = (rows * row_weight).astype(BF)
        if s == 0:
            near[...] = rows
        else:
            far[64 * (s - 1) : 64 * s, :] = rows
        sel_out[64 * s : 64 * (s + 1), :] = sel_bf


def dispatch(pos, ids, gates, grads):
    return pl.pallas_call(
        dispatch_kernel,
        in_specs=[SM, VM, VM, VM],
        out_specs=[VM] * 3,
        out_shape=[shape((64, 384)), shape((192, 384)), shape((256, 128))],
        name="dispatch",
        compiler_params=room(4),
    )(pos, ids, gates, grads)


def combine_kernel(sel, grads, from1, from2, from3, other, own, across, out):
    rows = jnp.concatenate(
        [from1[0:64], from2[0:64], from3[0:64], other[...], own[...], across[...]], axis=0
    )
    order = (1, 2, 3, 3, 2, 1, 0, 0)
    picks = jnp.concatenate([sel[64 * k : 64 * (k + 1)] for k in order], axis=0)
    moe = lax.dot_general(picks, rows, (((0,), (0,)), ((), ())), preferred_element_type=F32)
    out[...] = (grads[...].astype(F32) + moe).astype(BF)


def combine(*args):
    return pl.pallas_call(
        combine_kernel, out_shape=shape((128, 384)), name="combine", compiler_params=room(4)
    )(*args)


def factors_kernel(table, gates, ups, mine, theirs, to_gate, to_up):
    for side, out in enumerate((mine, theirs)):

        def block_step(block, carry, side=side):
            start = pl.multiple_of(table[16 + 8 * side + block] * 64, 64)
            here = pl.ds(pl.multiple_of(block * 64, 64), 64)
            gate = gates[pl.ds(start, 64), :].astype(F32)
            up = ups[pl.ds(start, 64), :].astype(F32)
            sigma = 1.0 / (1.0 + jnp.exp(-gate))
            to_gate[here, :] = up * sigma * (1.0 + gate * (1.0 - sigma))
            to_up[here, :] = gate * sigma
            return carry

        lax.fori_loop(0, 8, block_step, 0)
        out[0:256, :] = to_gate[...].T
        out[256:512, :] = to_up[...].T


def factors(table, *saved):
    return pl.pallas_call(
        factors_kernel,
        in_specs=[SM] + [VM] * 2,
        out_specs=[VM] * 2,
        out_shape=[shape((512, 512), F32)] * 2,
        scratch_shapes=[pltpu.VMEM((512, 256), F32)] * 2,
        name="factors",
        compiler_params=room(16),
    )(table, *saved)


def act_first_kernel(table, *refs):
    pieces, down_own, down_other, acc = refs[:9], refs[9], refs[10], refs[11]
    for k, group in enumerate((0, 1, 3)):
        top, bottom, far = pieces[3 * k : 3 * k + 3]
        rows = jnp.concatenate(
            [jnp.concatenate([top[...], bottom[...]], axis=0), far[...]], axis=1
        )
        for side, down in enumerate((down_own, down_other)):
            columns = [
                down[:, pl.ds(pl.multiple_of(table[4 * group + j] * 384, 384), 384)] for j in CHUNKS
            ]
            term = lax.dot_general(
                jnp.concatenate(columns, axis=1), rows, NT, preferred_element_type=F32
            )
            if k == 0:
                acc[256 * side : 256 * (side + 1), :] = term
            else:
                acc[256 * side : 256 * (side + 1), :] += term


def act_first(table, pieces, down_own, down_other):
    return pl.pallas_call(
        act_first_kernel,
        in_specs=[SM] + [VM] * 11,
        out_specs=VM,
        out_shape=shape((512, 512), F32),
        name="act_first",
        compiler_params=room(28),
    )(table, *pieces, down_own, down_other)


def act_last_kernel(table, *refs):
    rows = jnp.concatenate([refs[0][...], refs[1][...]], axis=0)
    acc, out = refs[10], refs[13]
    for side in range(2):
        columns = jnp.concatenate([refs[2 + 4 * side + j][...] for j in range(4)], axis=1)
        here = slice(256 * side, 256 * (side + 1))
        act = acc[here, :] + lax.dot_general(columns, rows, NT, preferred_element_type=F32)
        factor = refs[11 + side]
        out[256 * side : 256 * (side + 1), :] = (act * factor[0:256, :]).astype(BF)
        out[512 + 256 * side : 512 + 256 * (side + 1), :] = (act * factor[256:512, :]).astype(BF)


def act_last(table, pieces, down_own, down_other, acc, factor_own, factor_other):
    def column(j):
        return pl.BlockSpec((256, 384), lambda i, table: (0, table[8 + CHUNKS[j]]))

    def whole(dims):
        return pl.BlockSpec(dims, lambda i, table: (0, 0))

    columns = [column(j) for j in range(4)]
    return pl.pallas_call(
        act_last_kernel,
        grid_spec=pltpu.PrefetchScalarGridSpec(
            num_scalar_prefetch=1,
            grid=(1,),
            in_specs=[whole((256, 1536))] * 2 + columns * 2 + [whole((512, 512))] * 3,
            out_specs=whole((1024, 512)),
        ),
        out_shape=shape((1024, 512)),
        name="act_last",
        compiler_params=room(20),
    )(table, *pieces, *[down_own] * 4, *[down_other] * 4, acc, factor_own, factor_other)


def part_kernel(groups, per, table, *refs):
    weights, grads, outs = refs[: 4 * per], refs[4 * per], refs[4 * per + 1 :]
    step = pl.program_id(0)
    for j in range(per):
        weight = jnp.concatenate([weights[per * k + j][...] for k in range(4)], axis=1)
        total = lax.dot_general(weight, grads[...], NN, preferred_element_type=F32).astype(BF)
        for run, group in enumerate(groups):
            for piece in range(4 // per):
                chunk = per * piece + j

                @pl.when(step == 4 // per * run + piece)
                def _(total=total, run=run, group=group, chunk=chunk):
                    if chunk == 3 and group != 2:
                        outs[3 * run + 2][...] = total
                    else:
                        here = slice(384 * chunk, 384 * (chunk + 1))
                        outs[3 * run][here, :] = total[:, 0:256]
                        outs[3 * run + 1][here, :] = total[:, 256:512]


def part(table, grads, weights, groups, per):
    steps = 4 // per

    def rows(j):
        def index(i, table):
            place = per * (i % steps) + j
            chunk = jnp.where(place == 2, 3, jnp.where(place == 3, 2, place))
            group = groups[0] if len(groups) == 1 else jnp.where(i < steps, *groups)
            return (table[4 * group + chunk], 0)

        return pl.BlockSpec((384, 256), index)

    dims = []
    for group in groups:
        dims += [(1536, 256)] * 2 if group == 2 else [(1152, 256), (1152, 256), (384, 512)]
    return pl.pallas_call(
        functools.partial(part_kernel, groups, per),
        grid_spec=pltpu.PrefetchScalarGridSpec(
            num_scalar_prefetch=1,
            grid=(steps * len(groups),),
            in_specs=[rows(j) for j in range(per)] * 4
            + [pl.BlockSpec((1024, 512), lambda i, table: (0, 0))],
            out_specs=[pl.BlockSpec(d, lambda i, table: (0, 0)) for d in dims],
        ),
        out_shape=[shape(d) for d in dims],
        compiler_params=room(20),
    )(table, *[w for weight in weights for w in [weight] * per], grads)


def add(*terms):
    total = terms[0].astype(F32)
    for term in terms[1:]:
        total = total + term.astype(F32)
    return total


def pairs_kernel(near_a, far_a, got_a, near_b, far_b, got_b, out_near_a, out_far_a, out_near_b, out_far_b):
    def some_rows(k, carry):
        here = pl.ds(pl.multiple_of(k * 128, 128), 128)
        out_near_a[here, :] = add(near_a[here, :], got_a[here, :]).astype(BF)
        out_near_b[here, :] = add(near_b[here, :], got_b[here, :]).astype(BF)
        return carry

    lax.fori_loop(0, 9, some_rows, 0)
    out_far_a[:, 0:256] = add(far_a[:, 0:256], got_a[1152:1536, :]).astype(BF)
    out_far_a[:, 256:512] = far_a[:, 256:512]
    out_far_b[:, 0:256] = far_b[:, 0:256]
    out_far_b[:, 256:512] = add(far_b[:, 256:512], got_b[1152:1536, :]).astype(BF)


def add_pairs(*args):
    return pl.pallas_call(
        pairs_kernel,
        out_shape=[shape((1152, 256)), shape((384, 512))] * 2,
        name="add_pairs",
        compiler_params=room(16),
    )(*args)


def far_kernel(own, got1, got2, top, bottom):
    total = add(own[...], got1[...], got2[...]).astype(BF)
    top[...] = total[:, 0:256]
    bottom[...] = total[:, 256:512]


def middle_far(*args):
    return pl.pallas_call(
        far_kernel,
        out_shape=[shape((384, 256))] * 2,
        name="middle_far",
        compiler_params=room(6),
    )(*args)


def near_kernel(own_t, own_b, t1, t2, b1, b2, got_top, got_bottom, own, ahead, behind):
    for k, out in enumerate((own, ahead, behind)):

        def some_rows(r, carry, k=k, out=out):
            to = pl.ds(pl.multiple_of(r * 128, 128), 128)
            here = pl.ds(pl.multiple_of(384 * k + r * 128, 128), 128)
            top = add(own_t[here, :], t1[here, :], t2[here, :])
            bottom = add(own_b[here, :], b1[here, :], b2[here, :])
            if k == 1:
                top = top + got_top[to, :].astype(F32)
            if k == 2:
                bottom = bottom + got_bottom[to, :].astype(F32)
            out[to, 0:256] = top.astype(out.dtype)
            out[to, 256:512] = bottom.astype(out.dtype)
            return carry

        lax.fori_loop(0, 3, some_rows, 0)


def middle_near(*args):
    return pl.pallas_call(
        near_kernel,
        out_shape=[shape((384, 512), F32), shape((384, 512)), shape((384, 512))],
        name="middle_near",
        compiler_params=room(16),
    )(*args)


def last_kernel(own, got1, got2, back1, back2, back3, near, across):
    rows = add(own[...], got1[...], got2[...]).T.astype(BF)
    back1[...] = rows[0:128]
    back2[...] = rows[128:256]
    back3[...] = rows[256:384]
    near[...] = rows[384:448]
    across[...] = rows[448:512]


def last(*args):
    return pl.pallas_call(
        last_kernel,
        out_shape=[shape((128, 384))] * 3 + [shape((64, 384))] * 2,
        name="last",
        compiler_params=room(8),
    )(*args)


def heads_kernel(tokens, weights, out):
    def some_rows(k, carry):
        here = pl.ds(pl.multiple_of(k * 256, 256), 256)
        out[here, :] = lax.dot_general(
            tokens[here, :], weights[...], NT, preferred_element_type=F32
        ).astype(BF)
        return carry

    lax.fori_loop(0, 2, some_rows, 0)


def heads(*args):
    return pl.pallas_call(
        heads_kernel, out_shape=shape((512, 1536)), name="heads", compiler_params=room(12)
    )(*args)


def body(d_out, expert_ids, gate_weights, saved_gate, saved_up, w_gate, w_up, w_down, w_out):
    expert = lax.axis_index("expert").astype(I32)
    etp = lax.axis_index("etp").astype(I32)
    tp = lax.axis_index("tp").astype(I32)
    y, x = etp // 4, etp % 4
    core = tp % 2
    z = 4 * (tp // 2) + expert
    direction = 1 - 2 * core

    i = jnp.arange(32, dtype=I32)
    d, j, q = i // 4, i % 4, i % 8
    feature = 4 * ((y + jnp.where(core == 0, d, j)) % 4) + (x + jnp.where(core == 0, j, d)) % 4
    holder = jnp.where(i < 24, core, 1 - core)
    step = jnp.where(q >= 6, 4 * (q - 6), (1 - 2 * holder) * (q // 2 + 1))
    place = (z - step + 16) % 8
    source_core = jnp.where((q < 6) & (q % 2 == 1), 1 - holder, holder)
    table = jnp.where(i < 16, feature, 4 * (place % 4) + 2 * (place // 4) + source_core)
    pos = jnp.where(jnp.arange(2) == 0, expert, direction)

    near, far, sel = dispatch(pos, expert_ids.T, gate_weights.T, d_out)
    other = swap_core(far)
    across = shift_z(near, 4)
    received = [
        shift_z(jnp.concatenate([far[64 * k - 64 : 64 * k], other[192 - 64 * k : 256 - 64 * k]]), k)
        for k in (1, 2, 3)
    ]

    down_own, gate_own, up_own = w_down[0], w_gate[0], w_up[0]
    down_other = swap_core(down_own)
    gate_other = swap_core(gate_own)
    up_other = swap_core(up_own)
    factor_own, sent_factor = factors(table, saved_gate[0], saved_up[0])

    rows = jnp.concatenate([*received, near, across], axis=0)
    ahead = shift_plane(rows, -1, True)
    behind = shift_plane(rows, 1, True)
    top = jnp.concatenate([rows[:256], ahead[:256], behind[:256]], axis=1)
    bottom = jnp.concatenate([rows[256:], ahead[256:], behind[256:]], axis=1)
    top, bottom, sent_factor = lax.optimization_barrier((top, bottom, sent_factor))
    factor_other = swap_core(sent_factor)
    far_top = shift_plane(ahead[:256], -1, True)
    far_bottom = shift_plane(behind[256:], 1, True)
    far = jnp.concatenate([far_top, far_bottom], axis=0)

    behind_bottom = shift_plane(bottom, 1, False)
    ahead_top = shift_plane(top, -1, False)
    behind_far = shift_plane(far, 1, False)
    ahead_far = shift_plane(far, -1, False)
    behind_top = shift_plane(top, 1, False)
    ahead_bottom = shift_plane(bottom, -1, False)
    last_bottom = shift_plane(jnp.concatenate([behind_bottom, behind_far[256:]], axis=1), 1, False)
    last_top = shift_plane(jnp.concatenate([ahead_top, ahead_far[:256]], axis=1), -1, False)

    acc = act_first(
        table,
        (top, bottom, far, ahead_top, ahead_bottom, ahead_far, behind_top, behind_bottom, behind_far),
        down_own,
        down_other,
    )
    grads = act_last(table, (last_top, last_bottom), down_own, down_other, acc, factor_own, factor_other)

    weights = (gate_own, gate_other, up_own, up_other)
    far_top, far_bottom = part(table, grads, weights, (2,), 2)
    got_top = shift_plane(far_top, 1, False)
    got_bottom = shift_plane(far_bottom, -1, False)
    near_parts = part(table, grads, weights, (1, 3), 2)
    ahead_top, ahead_bottom, ahead_far, behind_top, behind_bottom, behind_far = near_parts
    from_behind_bottom = shift_plane(ahead_bottom, 1, False)
    from_ahead_top = shift_plane(behind_top, -1, False)
    own_top, own_bottom, own_far = part(table, grads, weights, (0,), 1)
    up_near, up_far, down_near, down_far = add_pairs(
        ahead_top, ahead_far, got_top, behind_bottom, behind_far, got_bottom
    )
    from_behind_far = shift_plane(up_far, 1, False)
    from_ahead_far = shift_plane(down_far, -1, False)
    from_behind_top = shift_plane(up_near, 1, False)
    from_ahead_bottom = shift_plane(down_near, -1, False)

    far_top, far_bottom = middle_far(own_far, from_behind_far, from_ahead_far)
    got_top = shift_plane(far_top, 1, True)
    got_bottom = shift_plane(far_bottom, -1, True)
    own, to_ahead, to_behind = middle_near(
        own_top,
        own_bottom,
        from_behind_top,
        from_ahead_top,
        from_behind_bottom,
        from_ahead_bottom,
        got_top,
        got_bottom,
    )
    from_behind = shift_plane(to_ahead, 1, True)
    from_ahead = shift_plane(to_behind, -1, True)
    *back, near, across = last(own, from_behind, from_ahead)

    across = shift_z(across, 4)
    back = [shift_z(rows, -k) for k, rows in zip((1, 2, 3), back)]
    other = swap_core(jnp.concatenate([rows[64:128] for rows in back], axis=0))
    d_hidden = combine(sel, d_out, *back, other, near, across)

    head_partial = heads(lax.all_gather(d_hidden, "tp", axis=0, tiled=True), w_out)
    spread = lax.all_to_all(head_partial.reshape(16, 32, 1536), "etp", 0, 0, tiled=True)
    d_heads = jnp.sum(spread.astype(F32), axis=0).astype(BF)
    return (d_hidden, d_heads)


def solution(mesh):
    in_specs = (
        P(("expert", "tp"), "etp"),
        P(("expert", "tp"), None),
        P(("expert", "tp"), None),
        P("expert", None, ("etp", "tp")),
        P("expert", None, ("etp", "tp")),
        P("expert", None, ("etp", "tp")),
        P("expert", None, ("etp", "tp")),
        P("expert", ("etp", "tp"), None),
        P("tp", "etp"),
    )
    out_specs = (P(("expert", "tp"), "etp"), P(("expert", "etp"), "tp"))

    return jax.shard_map(body, mesh=mesh, in_specs=in_specs, out_specs=out_specs, check_vma=False)
```

profile of v0, /device:TPU:2, one launch (start us, length us, event | category | flops | bytes accessed | tf_op | source)
XLA Modules:
  0.0 215.9 jit_solution(17508349106710308371)
XLA Ops:
  0.7 0.9 copy-done.6
  1.6 0.7 copy-done.8
  2.2 0.7 copy-done.9
  2.9 0.9 dispatch.1
  3.9 7.3 %collective-permute-start.6 = (bf16[64,384]{1,0:T(8,128)(2,1)S(1)}, bf16[64,384]{1,0:T(8,128)(2,1)S(1)}, u32[]{:S(2)}, u32[]{:S(2)}) collective-permute-start(bf16[64,384]{1,0:T(8,128)(2,1)S(1)} %get-tuple-element.37), channel_id=1, source_target_pairs={{0,2},{1,3},{2,0},{3,1},{64,66},{65,67},{66,64},{67,65},{128,130},... | collective-permute-start | bytes 147464 | tf_op jit(solution)/shard_map/ppermute | solution.py:51
  11.2 1.1 collective-permute-start.3
  12.4 1.6 collective-permute-start.4
  13.9 0.9 collective-permute-start.5
  14.8 2.4 %collective-permute-done.3 = bf16[128,384]{1,0:T(8,128)(2,1)S(1)} collective-permute-done((bf16[128,384]{1,0:T(8,128)(2,1)S(1)}, bf16[128,384]{1,0:T(8,128)(2,1)S(1)}, u32[]{:S(2)}, u32[]{:S(2)}) %collective-permute-start.3) | collective-permute-done | bytes 98336 | tf_op jit(solution)/shard_map/ppermute | solution.py:51
  17.8 2.4 %collective-permute-done.4 = bf16[128,384]{1,0:T(8,128)(2,1)S(1)} collective-permute-done((bf16[128,384]{1,0:T(8,128)(2,1)S(1)}, bf16[128,384]{1,0:T(8,128)(2,1)S(1)}, u32[]{:S(2)}, u32[]{:S(2)}) %collective-permute-start.4) | collective-permute-done | bytes 98336 | tf_op jit(solution)/shard_map/ppermute | solution.py:51
  20.9 1.9 collective-permute-done.5
  25.3 1.5 collective-permute-start.8
  27.3 1.0 copy-done.4
  28.3 1.0 copy-done.5
  29.4 1.9 factors.1
  31.3 1.5 collective-permute-done.7
  32.8 1.1 fusion.11
  34.1 1.1 fusion.12
  35.3 1.7 collective-permute-start.14
  37.0 3.2 %collective-permute-start.10 = (bf16[256,384]{1,0:T(8,128)(2,1)S(1)}, bf16[256,384]{1,0:T(8,128)(2,1)S(1)}, u32[]{:S(2)}, u32[]{:S(2)}) collective-permute-start(bf16[256,384]{1,0:T(8,128)(2,1)S(1)} %get-tuple-element.69), channel_id=1, source_target_pairs={{0,12},{1,49},{2,14},{3,51},{4,0},{5,53},{6,2},{7,55},{8,4},{9,57}... | collective-permute-start | bytes 589832 | tf_op jit(solution)/shard_map/ppermute | solution.py:41
  40.2 3.2 %collective-permute-done.10 = bf16[256,384]{1,0:T(8,128)(2,1)S(1)} collective-permute-done((bf16[256,384]{1,0:T(8,128)(2,1)S(1)}, bf16[256,384]{1,0:T(8,128)(2,1)S(1)}, u32[]{:S(2)}, u32[]{:S(2)}) %collective-permute-start.10) | collective-permute-done | bytes 196640 | tf_op jit(solution)/shard_map/ppermute | solution.py:41
  43.3 0.9 collective-permute-start.11
  44.3 5.2 %collective-permute-done.11 = bf16[256,384]{1,0:T(8,128)(2,1)S(1)} collective-permute-done((bf16[256,384]{1,0:T(8,128)(2,1)S(1)}, bf16[256,384]{1,0:T(8,128)(2,1)S(1)}, u32[]{:S(2)}, u32[]{:S(2)}) %collective-permute-start.11) | collective-permute-done | bytes 196640 | tf_op jit(solution)/shard_map/ppermute | solution.py:41
  49.5 1.7 collective-permute-start.18
  51.1 1.8 collective-permute-start.9
  53.0 6.3 %collective-permute-done.18.refs_4_ = bf16[256,1152]{1,0:T(8,128)(2,1)S(1)} collective-permute-done((bf16[256,1152]{1,0:T(8,128)(2,1)S(1)}, bf16[256,1152]{1,0:T(8,128)(2,1)S(1)}, u32[]{:S(2)}, u32[]{:S(2)}) %collective-permute-start.18) | collective-permute-done | bytes 589856 | tf_op jit(solution)/shard_map/ppermute | solution.py:41
  59.4 1.6 collective-permute-start.15
  60.9 4.7 %collective-permute-done.9.refs_3_ = bf16[256,1152]{1,0:T(8,128)(2,1)S(1)} collective-permute-done((bf16[256,1152]{1,0:T(8,128)(2,1)S(1)}, bf16[256,1152]{1,0:T(8,128)(2,1)S(1)}, u32[]{:S(2)}, u32[]{:S(2)}) %collective-permute-start.9) | collective-permute-done | bytes 589856 | tf_op jit(solution)/shard_map/ppermute | solution.py:41
  65.7 2.9 %collective-permute-start.12 = (bf16[512,384]{1,0:T(8,128)(2,1)S(1)}, bf16[512,384]{1,0:T(8,128)(2,1)S(1)}, u32[]{:S(2)}, u32[]{:S(2)}) collective-permute-start(bf16[512,384]{1,0:T(8,128)(2,1)S(1)} %constant_dynamic-update-slice_fusion.5.refs_2_), channel_id=1, source_target_pairs={{0,48},{1,13},{2,50},{3,15},{4,52},{5,1},{6,54},{7,3},{8,56},{9,5}... | collective-permute-start | bytes 1179656 | tf_op jit(solution)/shard_map/ppermute | solution.py:41
  68.7 5.1 %collective-permute-done.12.refs_5_ = bf16[512,384]{1,0:T(8,128)(2,1)S(1)} collective-permute-done((bf16[512,384]{1,0:T(8,128)(2,1)S(1)}, bf16[512,384]{1,0:T(8,128)(2,1)S(1)}, u32[]{:S(2)}, u32[]{:S(2)}) %collective-permute-start.12) | collective-permute-done | bytes 393248 | tf_op jit(solution)/shard_map/ppermute | solution.py:41
  74.0 5.6 %collective-permute-done.19.refs_6_ = bf16[256,1152]{1,0:T(8,128)(2,1)S(1)} collective-permute-done((bf16[256,1152]{1,0:T(8,128)(2,1)S(1)}, bf16[256,1152]{1,0:T(8,128)(2,1)S(1)}, u32[]{:S(2)}, u32[]{:S(2)}) %collective-permute-start.19) | collective-permute-done | bytes 589856 | tf_op jit(solution)/shard_map/ppermute | solution.py:41
  79.7 3.2 %collective-permute-start.13 = (bf16[256,1536]{1,0:T(8,128)(2,1)S(1)}, bf16[256,1536]{1,0:T(8,128)(2,1)S(1)}, u32[]{:S(2)}, u32[]{:S(2)}) collective-permute-start(bf16[256,1536]{1,0:T(8,128)(2,1)S(1)} %pad_maximum_fusion), channel_id=1, source_target_pairs={{0,48},{1,13},{2,50},{3,15},{4,52},{5,1},{6,54},{7,3},{8,56},{9,5}... | collective-permute-start | bytes 2359304 | tf_op jit(solution)/shard_map/ppermute | solution.py:41
  82.9 3.2 %act_first.1.refs_10_ = f32[512,512]{1,0:T(8,128)S(1)} custom-call(s32[32]{0:T(128)S(1)} %compare_select_fusion.8.table, bf16[256,1152]{1,0:T(8,128)(2,1)S(1)} %get-tuple-element.39.refs_0_, bf16[256,1152]{1,0:T(8,128)(2,1)S(1)} %get-tuple-element.40.refs_1_, bf16[512,384]{1,0:T(8,128)(2,1)S(1)} %constant_dynamic-update-slice_fusion.5.refs_2_, ...), custom_call_target="tpu_custom_call" | custom-call | tf_op jit(solution)/shard_map/act_first/pallas_call | solution.py:160
  86.1 6.8 %collective-permute-done.16.refs_1_ = bf16[256,1536]{1,0:T(8,128)(2,1)S(1)} collective-permute-done((bf16[256,1536]{1,0:T(8,128)(2,1)S(1)}, bf16[256,1536]{1,0:T(8,128)(2,1)S(1)}, u32[]{:S(2)}, u32[]{:S(2)}) %collective-permute-start.16) | collective-permute-done | bytes 786464 | tf_op jit(solution)/shard_map/ppermute | solution.py:41
  92.9 1.7 act_last.1.refs_4_.refs_8_
  94.7 1.0 copy-done.2
  95.7 4.4 %shard_map.106 = (bf16[1536,256]{1,0:T(8,128)(2,1)S(1)}, bf16[1536,256]{1,0:T(8,128)(2,1)S(1)}) custom-call(s32[32]{0:T(128)S(1)} %compare_select_fusion.8.table, bf16[6144,256]{1,0:T(8,128)(2,1)S(1)} %bitcast.15, bf16[6144,256]{1,0:T(8,128)(2,1)S(1)} %bitcast.16, bf16[6144,256]{1,0:T(8,128)(2,1)} %collective-permute-done.refs_1_.refs_2_.refs_3_, ...), custom_call_target="tpu_custom_call" | custom-call | tf_op jit(solution)/shard_map/pallas_call | solution.py:239
  100.2 3.3 %collective-permute-start.22 = (bf16[1536,256]{1,0:T(8,128)(2,1)S(1)}, bf16[1536,256]{1,0:T(8,128)(2,1)S(1)}, u32[]{:S(2)}, u32[]{:S(2)}) collective-permute-start(bf16[1536,256]{1,0:T(8,128)(2,1)S(1)} %get-tuple-element.50), channel_id=1, source_target_pairs={{0,48},{1,13},{2,50},{3,15},{4,52},{5,1},{6,54},{7,3},{8,56},{9,5}... | collective-permute-start | bytes 2359304 | tf_op jit(solution)/shard_map/ppermute | solution.py:41
  103.5 7.0 %shard_map.105 = (bf16[1152,256]{1,0:T(8,128)(2,1)S(1)}, bf16[1152,256]{1,0:T(8,128)(2,1)S(1)}, bf16[384,512]{1,0:T(8,128)(2,1)S(1)}, bf16[1152,256]{1,0:T(8,128...) custom-call(s32[32]{0:T(128)S(1)} %compare_select_fusion.8.table, ...), custom_call_target="tpu_custom_call" | custom-call | tf_op jit(solution)/shard_map/pallas_call | solution.py:239
  110.5 2.8 %collective-permute-done.21.got_a = bf16[1536,256]{1,0:T(8,128)(2,1)S(1)} collective-permute-done((bf16[1536,256]{1,0:T(8,128)(2,1)S(1)}, bf16[1536,256]{1,0:T(8,128)(2,1)S(1)}, u32[]{:S(2)}, u32[]{:S(2)}) %collective-permute-start.21) | collective-permute-done | bytes 786464 | tf_op jit(solution)/shard_map/ppermute | solution.py:41
  113.8 1.5 collective-permute-start.27
  115.3 2.0 collective-permute-start.24
  117.3 3.2 %collective-permute-start.28 = (bf16[384,512]{1,0:T(8,128)(2,1)S(1)}, bf16[384,512]{1,0:T(8,128)(2,1)S(1)}, u32[]{:S(2)}, u32[]{:S(2)}) collective-permute-start(bf16[384,512]{1,0:T(8,128)(2,1)S(1)} %get-tuple-element.57), channel_id=1, source_target_pairs={{0,48},{1,13},{2,50},{3,15},{4,52},{5,1},{6,54},{7,3},{8,56},{9,5}... | collective-permute-start | bytes 1179656 | tf_op jit(solution)/shard_map/ppermute | solution.py:41
  120.5 2.4 %collective-permute-done.27.got1 = bf16[384,512]{1,0:T(8,128)(2,1)S(1)} collective-permute-done((bf16[384,512]{1,0:T(8,128)(2,1)S(1)}, bf16[384,512]{1,0:T(8,128)(2,1)S(1)}, u32[]{:S(2)}, u32[]{:S(2)}) %collective-permute-start.27) | collective-permute-done | bytes 393248 | tf_op jit(solution)/shard_map/ppermute | solution.py:41
  122.9 2.0 collective-permute-start.26
  124.9 4.6 %shard_map.104 = (bf16[1152,256]{1,0:T(8,128)(2,1)S(1)}, bf16[1152,256]{1,0:T(8,128)(2,1)S(1)}, bf16[384,512]{1,0:T(8,128)(2,1)S(1)}) custom-call(s32[32]{0:T(128)S(1)} %compare_select_fusion.8.table, bf16[6144,256]{1,0:T(8,128)(2,1)S(1)} %bitcast.19, bf16[6144,256]{1,0:T(8,128)(2,1)} %collective-permute-done.refs_1_.refs_2_.refs_3_, ...), custom_call_target="tpu_custom_call" | custom-call | tf_op jit(solution)/shard_map/pallas_call | solution.py:239
  129.6 0.7 collective-permute-done.28.got2
  130.4 0.9 collective-permute-start.29
  131.4 3.6 %collective-permute-start.30 = (bf16[384,256]{1,0:T(8,128)(2,1)S(1)}, bf16[384,256]{1,0:T(8,128)(2,1)S(1)}, u32[]{:S(2)}, u32[]{:S(2)}) collective-permute-start(bf16[384,256]{1,0:T(8,128)(2,1)S(1)} %get-tuple-element.59), channel_id=1, source_target_pairs={{0,12},{1,49},{2,14},{3,51},{4,0},{5,53},{6,2},{7,55},{8,4},{9,57}... | collective-permute-start | bytes 589832 | tf_op jit(solution)/shard_map/ppermute | solution.py:41
  135.0 2.6 %collective-permute-done.23.t1 = bf16[1152,256]{1,0:T(8,128)(2,1)S(1)} collective-permute-done((bf16[1152,256]{1,0:T(8,128)(2,1)S(1)}, bf16[1152,256]{1,0:T(8,128)(2,1)S(1)}, u32[]{:S(2)}, u32[]{:S(2)}) %collective-permute-start.23) | collective-permute-done | bytes 589856 | tf_op jit(solution)/shard_map/ppermute | solution.py:41
  139.1 2.7 %collective-permute-start.31 = (bf16[384,512]{1,0:T(8,128)(2,1)S(1)}, bf16[384,512]{1,0:T(8,128)(2,1)S(1)}, u32[]{:S(2)}, u32[]{:S(2)}) collective-permute-start(bf16[384,512]{1,0:T(8,128)(2,1)S(1)} %get-tuple-element.61), channel_id=1, source_target_pairs={{0,4},{1,17},{2,6},{3,19},{4,8},{5,21},{6,10},{7,23},{8,12},{9,25}... | collective-permute-start | bytes 1179656 | tf_op jit(solution)/shard_map/ppermute | solution.py:41
  141.8 3.4 %collective-permute-start.32 = (bf16[384,512]{1,0:T(8,128)(2,1)S(1)}, bf16[384,512]{1,0:T(8,128)(2,1)S(1)}, u32[]{:S(2)}, u32[]{:S(2)}) collective-permute-start(bf16[384,512]{1,0:T(8,128)(2,1)S(1)} %get-tuple-element.62), channel_id=1, source_target_pairs={{0,12},{1,49},{2,14},{3,51},{4,0},{5,53},{6,2},{7,55},{8,4},{9,57}... | collective-permute-start | bytes 1179656 | tf_op jit(solution)/shard_map/ppermute | solution.py:41
  145.2 5.7 %collective-permute-done.31.got1 = bf16[384,512]{1,0:T(8,128)(2,1)S(1)} collective-permute-done((bf16[384,512]{1,0:T(8,128)(2,1)S(1)}, bf16[384,512]{1,0:T(8,128)(2,1)S(1)}, u32[]{:S(2)}, u32[]{:S(2)}) %collective-permute-start.31) | collective-permute-done | bytes 393248 | tf_op jit(solution)/shard_map/ppermute | solution.py:41
  151.7 3.2 %collective-permute-start.34 = (bf16[128,384]{1,0:T(8,128)(2,1)S(1)}, bf16[128,384]{1,0:T(8,128)(2,1)S(1)}, u32[]{:S(2)}, u32[]{:S(2)}) collective-permute-start(bf16[128,384]{1,0:T(8,128)(2,1)S(1)} %get-tuple-element.64), channel_id=1, source_target_pairs={{0,130},{1,129},{2,128},{3,131},{64,194},{65,193},{66,192},{67,195... | collective-permute-start | bytes 294920 | tf_op jit(solution)/shard_map/ppermute | solution.py:51
  154.8 1.8 collective-permute-start.35
  156.6 2.8 %collective-permute-done.34.from2 = bf16[128,384]{1,0:T(8,128)(2,1)S(1)} collective-permute-done((bf16[128,384]{1,0:T(8,128)(2,1)S(1)}, bf16[128,384]{1,0:T(8,128)(2,1)S(1)}, u32[]{:S(2)}, u32[]{:S(2)}) %collective-permute-start.34) | collective-permute-done | bytes 98336 | tf_op jit(solution)/shard_map/ppermute | solution.py:51
  159.4 2.5 %collective-permute-done.35.from3 = bf16[128,384]{1,0:T(8,128)(2,1)S(1)} collective-permute-done((bf16[128,384]{1,0:T(8,128)(2,1)S(1)}, bf16[128,384]{1,0:T(8,128)(2,1)S(1)}, u32[]{:S(2)}, u32[]{:S(2)}) %collective-permute-start.35) | collective-permute-done | bytes 98336 | tf_op jit(solution)/shard_map/ppermute | solution.py:51
  162.1 3.6 %collective-permute-start.37 = (bf16[64,384]{1,0:T(8,128)(2,1)S(1)}, bf16[64,384]{1,0:T(8,128)(2,1)S(1)}, u32[]{:S(2)}, u32[]{:S(2)}) collective-permute-start(bf16[64,384]{1,0:T(8,128)(2,1)S(1)} %get-tuple-element.67), channel_id=1, source_target_pairs={{0,2},{1,3},{2,0},{3,1},{64,66},{65,67},{66,64},{67,65},{128,130},... | collective-permute-start | bytes 147464 | tf_op jit(solution)/shard_map/ppermute | solution.py:51
  165.6 4.6 %collective-permute-done.37.across = bf16[64,384]{1,0:T(8,128)(2,1)S(1)} collective-permute-done((bf16[64,384]{1,0:T(8,128)(2,1)S(1)}, bf16[64,384]{1,0:T(8,128)(2,1)S(1)}, u32[]{:S(2)}, u32[]{:S(2)}) %collective-permute-start.37) | collective-permute-done | bytes 49184 | tf_op jit(solution)/shard_map/ppermute | solution.py:51
  170.2 0.9 combine.1
  171.2 10.3 %all_gather.3.tokens = bf16[512,384]{1,0:T(8,128)(2,1)S(1)} all-gather(bf16[128,384]{1,0:T(8,128)(2,1)} %combine.1), channel_id=1, replica_groups=mesh['expert'=4,'etp'=16,'tp'=4] {'tp'}, dimensions={0}, use_global_device_ids=true | all-gather | bytes 491520 | tf_op jit(solution)/shard_map/all_gather | solution.py:461
  181.5 1.2 heads.1
  182.7 32.3 %all_to_all.5 = bf16[16,32,1536]{2,1,0:T(8,128)(2,1)S(1)} all-to-all(bf16[16,32,1536]{2,1,0:T(8,128)(2,1)S(1)} %bitcast.26), channel_id=1, replica_groups=mesh['expert'=4,'etp'=16,'tp'=4] {'etp'}, dimensions={0} | all-to-all | bytes 3145728 | tf_op jit(solution)/shard_map/all_to_all | solution.py:462
  215.0 0.9 reduce_sum.12
  (77 shorter events, 8.5 us)
Async XLA Ops:
  0.7 0.9 copy-start.6
  1.6 0.7 copy-start.8
  2.2 0.7 copy-start.9
  3.8 7.4 %collective-permute-start.2 = (bf16[192,384]{1,0:T(8,128)(2,1)S(1)}, bf16[192,384]{1,0:T(8,128)(2,1)S(1)}, u32[]{:S(2)}, u32[]{:S(2)}) collective-permute-start(bf16[192,384]{1,0:T(8,128)(2,1)S(1)} %get-tuple-element.36), channel_id=1, source_target_pairs={{0,1},{1,0},{2,3},{3,2},{4,5},{5,4},{6,7},{7,6},{8,9},{9,8},{10,11... | collective-permute-start | bytes 442376 | tf_op jit(solution)/shard_map/ppermute | solution.py:55
  3.9 20.2 %collective-permute-start.6 = (bf16[64,384]{1,0:T(8,128)(2,1)S(1)}, bf16[64,384]{1,0:T(8,128)(2,1)S(1)}, u32[]{:S(2)}, u32[]{:S(2)}) collective-permute-start(bf16[64,384]{1,0:T(8,128)(2,1)S(1)} %get-tuple-element.37), channel_id=1, source_target_pairs={{0,2},{1,3},{2,0},{3,1},{64,66},{65,67},{66,64},{67,65},{128,130},... | collective-permute-start | bytes 147464 | tf_op jit(solution)/shard_map/ppermute | solution.py:51
  11.2 5.9 %collective-permute-start.3 = (bf16[128,384]{1,0:T(8,128)(2,1)S(1)}, bf16[128,384]{1,0:T(8,128)(2,1)S(1)}, u32[]{:S(2)}, u32[]{:S(2)}) collective-permute-start(bf16[128,384]{1,0:T(8,128)(2,1)S(1)} %pad_maximum_fusion.5), channel_id=1, source_target_pairs={{0,64},{1,195},{2,66},{3,193},{64,128},{65,1},{66,130},{67,3},{128... | collective-permute-start | bytes 294920 | tf_op jit(solution)/shard_map/ppermute | solution.py:51
  12.4 7.9 %collective-permute-start.4 = (bf16[128,384]{1,0:T(8,128)(2,1)S(1)}, bf16[128,384]{1,0:T(8,128)(2,1)S(1)}, u32[]{:S(2)}, u32[]{:S(2)}) collective-permute-start(bf16[128,384]{1,0:T(8,128)(2,1)S(1)} %pad_maximum_fusion.6), channel_id=1, source_target_pairs={{0,128},{1,131},{2,130},{3,129},{64,192},{65,195},{66,194},{67,193... | collective-permute-start | bytes 294920 | tf_op jit(solution)/shard_map/ppermute | solution.py:51
  13.9 8.9 %collective-permute-start.5 = (bf16[128,384]{1,0:T(8,128)(2,1)S(1)}, bf16[128,384]{1,0:T(8,128)(2,1)S(1)}, u32[]{:S(2)}, u32[]{:S(2)}) collective-permute-start(bf16[128,384]{1,0:T(8,128)(2,1)S(1)} %pad_maximum_fusion.7), channel_id=1, source_target_pairs={{0,192},{1,67},{2,194},{3,65},{64,2},{65,131},{66,0},{67,129},{128... | collective-permute-start | bytes 294920 | tf_op jit(solution)/shard_map/ppermute | solution.py:51
  24.1 1.2 copy-start.10
  24.7 8.1 %collective-permute-start.7 = (bf16[512,384]{1,0:T(8,128)(2,1)}, bf16[512,384]{1,0:T(8,128)(2,1)}, u32[]{:S(2)}, u32[]{:S(2)}) collective-permute-start(bf16[512,384]{1,0:T(8,128)(2,1)} %constant_dynamic-update-slice_fusion), channel_id=1, source_target_pairs={{0,12},{1,49},{2,14},{3,51},{4,0},{5,53},{6,2},{7,55},{8,4},{9,57}... | collective-permute-start | bytes 1179656 | tf_op jit(solution)/shard_map/ppermute | solution.py:41
  25.2 54.4 %collective-permute-start.17 = (bf16[256,6144]{1,0:T(8,128)(2,1)}, bf16[256,6144]{1,0:T(8,128)(2,1)S(1)}, u32[]{:S(2)}, u32[]{:S(2)}) collective-permute-start(bf16[256,6144]{1,0:T(8,128)(2,1)} %bitcast.8), channel_id=1, source_target_pairs={{0,1},{1,0},{2,3},{3,2},{4,5},{5,4},{6,7},{7,6},{8,9},{9,8},{10,11... | collective-permute-start | bytes 9437192 | tf_op jit(solution)/shard_map/ppermute | solution.py:55
  25.3 8.9 %collective-permute-start.8 = (bf16[512,384]{1,0:T(8,128)(2,1)}, bf16[512,384]{1,0:T(8,128)(2,1)}, u32[]{:S(2)}, u32[]{:S(2)}) collective-permute-start(bf16[512,384]{1,0:T(8,128)(2,1)} %constant_dynamic-update-slice_fusion), channel_id=1, source_target_pairs={{0,4},{1,17},{2,6},{3,19},{4,8},{5,21},{6,10},{7,23},{8,12},{9,25}... | collective-permute-start | bytes 1179656 | tf_op jit(solution)/shard_map/ppermute | solution.py:41
  26.7 67.8 %collective-permute-start = (bf16[6144,256]{1,0:T(8,128)(2,1)}, bf16[6144,256]{1,0:T(8,128)(2,1)}, u32[]{:S(2)}, u32[]{:S(2)}) collective-permute-start(bf16[6144,256]{1,0:T(8,128)(2,1)} %bitcast.14), channel_id=1, source_target_pairs={{0,1},{1,0},{2,3},{3,2},{4,5},{5,4},{6,7},{7,6},{8,9},{9,8},{10,11... | collective-permute-start | bytes 9437192 | tf_op jit(solution)/shard_map/ppermute | solution.py:55
  27.1 67.5 %collective-permute-start.1 = (bf16[6144,256]{1,0:T(8,128)(2,1)}, bf16[6144,256]{1,0:T(8,128)(2,1)}, u32[]{:S(2)}, u32[]{:S(2)}) collective-permute-start(bf16[6144,256]{1,0:T(8,128)(2,1)} %bitcast.20), channel_id=1, source_target_pairs={{0,1},{1,0},{2,3},{3,2},{4,5},{5,4},{6,7},{7,6},{8,9},{9,8},{10,11... | collective-permute-start | bytes 9437192 | tf_op jit(solution)/shard_map/ppermute | solution.py:55
  27.3 1.0 copy-start.4
  28.3 1.0 copy-start.5
  29.4 5.8 %copy-start.11 = (bf16[64,384]{1,0:T(8,128)(2,1)S(1)}, bf16[64,384]{1,0:T(8,128)(2,1)}, u32[]{:S(2)}) copy-start(bf16[64,384]{1,0:T(8,128)(2,1)} %copy-done.10) | copy-start | bytes 147460
  35.3 15.8 %collective-permute-start.14 = (bf16[256,1152]{1,0:T(8,128)(2,1)S(1)}, bf16[256,1152]{1,0:T(8,128)(2,1)S(1)}, u32[]{:S(2)}, u32[]{:S(2)}) collective-permute-start(bf16[256,1152]{1,0:T(8,128)(2,1)S(1)} %get-tuple-element.40.refs_1_), channel_id=1, source_target_pairs={{0,16},{1,5},{2,18},{3,7},{4,20},{5,9},{6,22},{7,11},{8,24},{9,13}... | collective-permute-start | bytes 1769480 | tf_op jit(solution)/shard_map/ppermute | solution.py:41
  37.0 6.4 %collective-permute-start.10 = (bf16[256,384]{1,0:T(8,128)(2,1)S(1)}, bf16[256,384]{1,0:T(8,128)(2,1)S(1)}, u32[]{:S(2)}, u32[]{:S(2)}) collective-permute-start(bf16[256,384]{1,0:T(8,128)(2,1)S(1)} %get-tuple-element.69), channel_id=1, source_target_pairs={{0,12},{1,49},{2,14},{3,51},{4,0},{5,53},{6,2},{7,55},{8,4},{9,57}... | collective-permute-start | bytes 589832 | tf_op jit(solution)/shard_map/ppermute | solution.py:41
  43.3 6.1 %collective-permute-start.11 = (bf16[256,384]{1,0:T(8,128)(2,1)S(1)}, bf16[256,384]{1,0:T(8,128)(2,1)S(1)}, u32[]{:S(2)}, u32[]{:S(2)}) collective-permute-start(bf16[256,384]{1,0:T(8,128)(2,1)S(1)} %get-tuple-element.71), channel_id=1, source_target_pairs={{0,4},{1,17},{2,6},{3,19},{4,8},{5,21},{6,10},{7,23},{8,12},{9,25}... | collective-permute-start | bytes 589832 | tf_op jit(solution)/shard_map/ppermute | solution.py:41
  49.5 9.9 %collective-permute-start.18 = (bf16[256,1152]{1,0:T(8,128)(2,1)S(1)}, bf16[256,1152]{1,0:T(8,128)(2,1)S(1)}, u32[]{:S(2)}, u32[]{:S(2)}) collective-permute-start(bf16[256,1152]{1,0:T(8,128)(2,1)S(1)} %get-tuple-element.40.refs_1_), channel_id=1, source_target_pairs={{0,48},{1,13},{2,50},{3,15},{4,52},{5,1},{6,54},{7,3},{8,56},{9,5}... | collective-permute-start | bytes 1769480 | tf_op jit(solution)/shard_map/ppermute | solution.py:41
  51.1 14.5 %collective-permute-start.9 = (bf16[256,1152]{1,0:T(8,128)(2,1)S(1)}, bf16[256,1152]{1,0:T(8,128)(2,1)S(1)}, u32[]{:S(2)}, u32[]{:S(2)}) collective-permute-start(bf16[256,1152]{1,0:T(8,128)(2,1)S(1)} %get-tuple-element.39.refs_0_), channel_id=1, source_target_pairs={{0,48},{1,13},{2,50},{3,15},{4,52},{5,1},{6,54},{7,3},{8,56},{9,5}... | collective-permute-start | bytes 1769480 | tf_op jit(solution)/shard_map/ppermute | solution.py:41
  59.4 9.2 %collective-permute-start.15 = (bf16[512,384]{1,0:T(8,128)(2,1)S(1)}, bf16[512,384]{1,0:T(8,128)(2,1)S(1)}, u32[]{:S(2)}, u32[]{:S(2)}) collective-permute-start(bf16[512,384]{1,0:T(8,128)(2,1)S(1)} %constant_dynamic-update-slice_fusion.5.refs_2_), channel_id=1, source_target_pairs={{0,16},{1,5},{2,18},{3,7},{4,20},{5,9},{6,22},{7,11},{8,24},{9,13}... | collective-permute-start | bytes 1179656 | tf_op jit(solution)/shard_map/ppermute | solution.py:41
  65.7 8.2 %collective-permute-start.12 = (bf16[512,384]{1,0:T(8,128)(2,1)S(1)}, bf16[512,384]{1,0:T(8,128)(2,1)S(1)}, u32[]{:S(2)}, u32[]{:S(2)}) collective-permute-start(bf16[512,384]{1,0:T(8,128)(2,1)S(1)} %constant_dynamic-update-slice_fusion.5.refs_2_), channel_id=1, source_target_pairs={{0,48},{1,13},{2,50},{3,15},{4,52},{5,1},{6,54},{7,3},{8,56},{9,5}... | collective-permute-start | bytes 1179656 | tf_op jit(solution)/shard_map/ppermute | solution.py:41
  68.6 11.1 %collective-permute-start.19 = (bf16[256,1152]{1,0:T(8,128)(2,1)S(1)}, bf16[256,1152]{1,0:T(8,128)(2,1)S(1)}, u32[]{:S(2)}, u32[]{:S(2)}) collective-permute-start(bf16[256,1152]{1,0:T(8,128)(2,1)S(1)} %get-tuple-element.39.refs_0_), channel_id=1, source_target_pairs={{0,16},{1,5},{2,18},{3,7},{4,20},{5,9},{6,22},{7,11},{8,24},{9,13}... | collective-permute-start | bytes 1769480 | tf_op jit(solution)/shard_map/ppermute | solution.py:41
  73.8 12.2 %collective-permute-start.20 = (f32[512,512]{1,0:T(8,128)S(1)}, f32[512,512]{1,0:T(8,128)S(1)}, u32[]{:S(2)}, u32[]{:S(2)}) collective-permute-start(f32[512,512]{1,0:T(8,128)S(1)} %get-tuple-element.42), channel_id=1, source_target_pairs={{0,1},{1,0},{2,3},{3,2},{4,5},{5,4},{6,7},{7,6},{8,9},{9,8},{10,11... | collective-permute-start | bytes 3145736 | tf_op jit(solution)/shard_map/ppermute | solution.py:55
  73.9 9.0 %copy-start = (bf16[1,256,6144]{2,1,0:T(8,128)(2,1)S(1)}, bf16[1,256,6144]{2,1,0:T(8,128)(2,1)}, u32[]{:S(2)}) copy-start(bf16[1,256,6144]{2,1,0:T(8,128)(2,1)} %param.16) | copy-start | bytes 9437188
  79.7 13.2 %collective-permute-start.16 = (bf16[256,1536]{1,0:T(8,128)(2,1)S(1)}, bf16[256,1536]{1,0:T(8,128)(2,1)S(1)}, u32[]{:S(2)}, u32[]{:S(2)}) collective-permute-start(bf16[256,1536]{1,0:T(8,128)(2,1)S(1)} %pad_maximum_fusion.1), channel_id=1, source_target_pairs={{0,16},{1,5},{2,18},{3,7},{4,20},{5,9},{6,22},{7,11},{8,24},{9,13}... | collective-permute-start | bytes 2359304 | tf_op jit(solution)/shard_map/ppermute | solution.py:41
  79.7 13.2 %collective-permute-start.13 = (bf16[256,1536]{1,0:T(8,128)(2,1)S(1)}, bf16[256,1536]{1,0:T(8,128)(2,1)S(1)}, u32[]{:S(2)}, u32[]{:S(2)}) collective-permute-start(bf16[256,1536]{1,0:T(8,128)(2,1)S(1)} %pad_maximum_fusion), channel_id=1, source_target_pairs={{0,48},{1,13},{2,50},{3,15},{4,52},{5,1},{6,54},{7,3},{8,56},{9,5}... | collective-permute-start | bytes 2359304 | tf_op jit(solution)/shard_map/ppermute | solution.py:41
  92.9 1.9 copy-start.1
  92.9 2.8 %copy-start.2 = (bf16[1,6144,256]{2,1,0:T(8,128)(2,1)S(1)}, bf16[1,6144,256]{2,1,0:T(8,128)(2,1)}, u32[]{:S(2)}) copy-start(bf16[1,6144,256]{2,1,0:T(8,128)(2,1)} %param.15) | copy-start | bytes 9437188
  100.1 13.3 %collective-permute-start.21 = (bf16[1536,256]{1,0:T(8,128)(2,1)S(1)}, bf16[1536,256]{1,0:T(8,128)(2,1)S(1)}, u32[]{:S(2)}, u32[]{:S(2)}) collective-permute-start(bf16[1536,256]{1,0:T(8,128)(2,1)S(1)} %get-tuple-element.47), channel_id=1, source_target_pairs={{0,16},{1,5},{2,18},{3,7},{4,20},{5,9},{6,22},{7,11},{8,24},{9,13}... | collective-permute-start | bytes 2359304 | tf_op jit(solution)/shard_map/ppermute | solution.py:41
  100.2 13.2 %collective-permute-start.22 = (bf16[1536,256]{1,0:T(8,128)(2,1)S(1)}, bf16[1536,256]{1,0:T(8,128)(2,1)S(1)}, u32[]{:S(2)}, u32[]{:S(2)}) collective-permute-start(bf16[1536,256]{1,0:T(8,128)(2,1)S(1)} %get-tuple-element.50), channel_id=1, source_target_pairs={{0,48},{1,13},{2,50},{3,15},{4,52},{5,1},{6,54},{7,3},{8,56},{9,5}... | collective-permute-start | bytes 2359304 | tf_op jit(solution)/shard_map/ppermute | solution.py:41
  113.8 9.2 %collective-permute-start.27 = (bf16[384,512]{1,0:T(8,128)(2,1)S(1)}, bf16[384,512]{1,0:T(8,128)(2,1)S(1)}, u32[]{:S(2)}, u32[]{:S(2)}) collective-permute-start(bf16[384,512]{1,0:T(8,128)(2,1)S(1)} %get-tuple-element.56), channel_id=1, source_target_pairs={{0,16},{1,5},{2,18},{3,7},{4,20},{5,9},{6,22},{7,11},{8,24},{9,13}... | collective-permute-start | bytes 1179656 | tf_op jit(solution)/shard_map/ppermute | solution.py:41
  115.3 16.1 %collective-permute-start.24 = (bf16[1152,256]{1,0:T(8,128)(2,1)S(1)}, bf16[1152,256]{1,0:T(8,128)(2,1)S(1)}, u32[]{:S(2)}, u32[]{:S(2)}) collective-permute-start(bf16[1152,256]{1,0:T(8,128)(2,1)S(1)} %get-tuple-element.52), channel_id=1, source_target_pairs={{0,48},{1,13},{2,50},{3,15},{4,52},{5,1},{6,54},{7,3},{8,56},{9,5}... | collective-permute-start | bytes 1769480 | tf_op jit(solution)/shard_map/ppermute | solution.py:41
  117.3 17.8 %collective-permute-start.25 = (bf16[1152,256]{1,0:T(8,128)(2,1)S(1)}, bf16[1152,256]{1,0:T(8,128)(2,1)S(1)}, u32[]{:S(2)}, u32[]{:S(2)}) collective-permute-start(bf16[1152,256]{1,0:T(8,128)(2,1)S(1)} %get-tuple-element.53), channel_id=1, source_target_pairs={{0,16},{1,5},{2,18},{3,7},{4,20},{5,9},{6,22},{7,11},{8,24},{9,13}... | collective-permute-start | bytes 1769480 | tf_op jit(solution)/shard_map/ppermute | solution.py:41
  117.3 13.0 %collective-permute-start.28 = (bf16[384,512]{1,0:T(8,128)(2,1)S(1)}, bf16[384,512]{1,0:T(8,128)(2,1)S(1)}, u32[]{:S(2)}, u32[]{:S(2)}) collective-permute-start(bf16[384,512]{1,0:T(8,128)(2,1)S(1)} %get-tuple-element.57), channel_id=1, source_target_pairs={{0,48},{1,13},{2,50},{3,15},{4,52},{5,1},{6,54},{7,3},{8,56},{9,5}... | collective-permute-start | bytes 1179656 | tf_op jit(solution)/shard_map/ppermute | solution.py:41
  120.5 17.2 %collective-permute-start.23 = (bf16[1152,256]{1,0:T(8,128)(2,1)S(1)}, bf16[1152,256]{1,0:T(8,128)(2,1)S(1)}, u32[]{:S(2)}, u32[]{:S(2)}) collective-permute-start(bf16[1152,256]{1,0:T(8,128)(2,1)S(1)} %get-tuple-element.51), channel_id=1, source_target_pairs={{0,16},{1,5},{2,18},{3,7},{4,20},{5,9},{6,22},{7,11},{8,24},{9,13}... | collective-permute-start | bytes 1769480 | tf_op jit(solution)/shard_map/ppermute | solution.py:41
  122.9 15.4 %collective-permute-start.26 = (bf16[1152,256]{1,0:T(8,128)(2,1)S(1)}, bf16[1152,256]{1,0:T(8,128)(2,1)S(1)}, u32[]{:S(2)}, u32[]{:S(2)}) collective-permute-start(bf16[1152,256]{1,0:T(8,128)(2,1)S(1)} %get-tuple-element.54), channel_id=1, source_target_pairs={{0,48},{1,13},{2,50},{3,15},{4,52},{5,1},{6,54},{7,3},{8,56},{9,5}... | collective-permute-start | bytes 1769480 | tf_op jit(solution)/shard_map/ppermute | solution.py:41
  130.4 8.1 %collective-permute-start.29 = (bf16[384,256]{1,0:T(8,128)(2,1)S(1)}, bf16[384,256]{1,0:T(8,128)(2,1)S(1)}, u32[]{:S(2)}, u32[]{:S(2)}) collective-permute-start(bf16[384,256]{1,0:T(8,128)(2,1)S(1)} %get-tuple-element.58), channel_id=1, source_target_pairs={{0,4},{1,17},{2,6},{3,19},{4,8},{5,21},{6,10},{7,23},{8,12},{9,25}... | collective-permute-start | bytes 589832 | tf_op jit(solution)/shard_map/ppermute | solution.py:41
  131.4 7.2 %collective-permute-start.30 = (bf16[384,256]{1,0:T(8,128)(2,1)S(1)}, bf16[384,256]{1,0:T(8,128)(2,1)S(1)}, u32[]{:S(2)}, u32[]{:S(2)}) collective-permute-start(bf16[384,256]{1,0:T(8,128)(2,1)S(1)} %get-tuple-element.59), channel_id=1, source_target_pairs={{0,12},{1,49},{2,14},{3,51},{4,0},{5,53},{6,2},{7,55},{8,4},{9,57}... | collective-permute-start | bytes 589832 | tf_op jit(solution)/shard_map/ppermute | solution.py:41
  139.1 31.2 %copy-start.7 = (bf16[128,384]{1,0:T(8,128)(2,1)S(1)}, bf16[128,384]{1,0:T(8,128)(2,1)}, u32[]{:S(2)}) copy-start(bf16[128,384]{1,0:T(8,128)(2,1)} %grads.3) | copy-start | bytes 294916
  139.1 11.7 %collective-permute-start.31 = (bf16[384,512]{1,0:T(8,128)(2,1)S(1)}, bf16[384,512]{1,0:T(8,128)(2,1)S(1)}, u32[]{:S(2)}, u32[]{:S(2)}) collective-permute-start(bf16[384,512]{1,0:T(8,128)(2,1)S(1)} %get-tuple-element.61), channel_id=1, source_target_pairs={{0,4},{1,17},{2,6},{3,19},{4,8},{5,21},{6,10},{7,23},{8,12},{9,25}... | collective-permute-start | bytes 1179656 | tf_op jit(solution)/shard_map/ppermute | solution.py:41
  141.8 9.0 %collective-permute-start.32 = (bf16[384,512]{1,0:T(8,128)(2,1)S(1)}, bf16[384,512]{1,0:T(8,128)(2,1)S(1)}, u32[]{:S(2)}, u32[]{:S(2)}) collective-permute-start(bf16[384,512]{1,0:T(8,128)(2,1)S(1)} %get-tuple-element.62), channel_id=1, source_target_pairs={{0,12},{1,49},{2,14},{3,51},{4,0},{5,53},{6,2},{7,55},{8,4},{9,57}... | collective-permute-start | bytes 1179656 | tf_op jit(solution)/shard_map/ppermute | solution.py:41
  151.0 30.5 %copy-start.3 = (bf16[1536,384]{1,0:T(8,128)(2,1)S(1)}, bf16[1536,384]{1,0:T(8,128)(2,1)}, u32[]{:S(2)}) copy-start(bf16[1536,384]{1,0:T(8,128)(2,1)} %weights.1) | copy-start | bytes 3538948
  151.0 5.6 %collective-permute-start.33 = (bf16[128,384]{1,0:T(8,128)(2,1)S(1)}, bf16[128,384]{1,0:T(8,128)(2,1)S(1)}, u32[]{:S(2)}, u32[]{:S(2)}) collective-permute-start(bf16[128,384]{1,0:T(8,128)(2,1)S(1)} %get-tuple-element.63), channel_id=1, source_target_pairs={{0,194},{1,65},{2,192},{3,67},{64,0},{65,129},{66,2},{67,131},{128... | collective-permute-start | bytes 294920 | tf_op jit(solution)/shard_map/ppermute | solution.py:51
  151.7 7.8 %collective-permute-start.34 = (bf16[128,384]{1,0:T(8,128)(2,1)S(1)}, bf16[128,384]{1,0:T(8,128)(2,1)S(1)}, u32[]{:S(2)}, u32[]{:S(2)}) collective-permute-start(bf16[128,384]{1,0:T(8,128)(2,1)S(1)} %get-tuple-element.64), channel_id=1, source_target_pairs={{0,130},{1,129},{2,128},{3,131},{64,194},{65,193},{66,192},{67,195... | collective-permute-start | bytes 294920 | tf_op jit(solution)/shard_map/ppermute | solution.py:51
  154.8 7.1 %collective-permute-start.35 = (bf16[128,384]{1,0:T(8,128)(2,1)S(1)}, bf16[128,384]{1,0:T(8,128)(2,1)S(1)}, u32[]{:S(2)}, u32[]{:S(2)}) collective-permute-start(bf16[128,384]{1,0:T(8,128)(2,1)S(1)} %get-tuple-element.65), channel_id=1, source_target_pairs={{0,66},{1,193},{2,64},{3,195},{64,130},{65,3},{66,128},{67,1},{128... | collective-permute-start | bytes 294920 | tf_op jit(solution)/shard_map/ppermute | solution.py:51
  162.0 8.2 %collective-permute-start.36 = (bf16[192,384]{1,0:T(8,128)(2,1)S(1)}, bf16[192,384]{1,0:T(8,128)(2,1)S(1)}, u32[]{:S(2)}, u32[]{:S(2)}) collective-permute-start(bf16[192,384]{1,0:T(8,128)(2,1)S(1)} %pad_maximum_fusion.4), channel_id=1, source_target_pairs={{0,1},{1,0},{2,3},{3,2},{4,5},{5,4},{6,7},{7,6},{8,9},{9,8},{10,11... | collective-permute-start | bytes 442376 | tf_op jit(solution)/shard_map/ppermute | solution.py:55
  162.1 8.1 %collective-permute-start.37 = (bf16[64,384]{1,0:T(8,128)(2,1)S(1)}, bf16[64,384]{1,0:T(8,128)(2,1)S(1)}, u32[]{:S(2)}, u32[]{:S(2)}) collective-permute-start(bf16[64,384]{1,0:T(8,128)(2,1)S(1)} %get-tuple-element.67), channel_id=1, source_target_pairs={{0,2},{1,3},{2,0},{3,1},{64,66},{65,67},{66,64},{67,65},{128,130},... | collective-permute-start | bytes 147464 | tf_op jit(solution)/shard_map/ppermute | solution.py:51
where the time goes:
time: 218 us; the launch traced here: 216 us
  waiting for transfers between devices  70.6 us (32%)
  starting transfers between devices  62.5 us (29%)
  blocking collectives  42.6 us (20%)
  Pallas kernels  27 us (12%)
  local copies, waits for them, and re-layouts  11 us (5%)
    ppermute x24, waiting for transfers between devices, shift_plane(): return lax.ppermute(value, ('etp', 'tp'), pairs)  54 us
    ppermute x24, starting transfers between devices, shift_plane(): return lax.ppermute(value, ('etp', 'tp'), pairs)  41.9 us
    all_to_all x1, blocking collectives, body(): lax.all_to_all(head_partial.reshape(16, 32, 1536), 'etp', 0, 0, tiled=True)  32.3 us
    ppermute x8, starting transfers between devices, shift_z(): return lax.ppermute(value, ('expert', 'tp'), pairs)  19.9 us
    ppermute x8, waiting for transfers between devices, shift_z(): return lax.ppermute(value, ('expert', 'tp'), pairs)  16.6 us
    pallas_call x3, Pallas kernels, part(): pl.pallas_call(functools.partial(part_kernel, groups, per), grid_spec=plt...  16 us
    all_gather x1, blocking collectives, body(): lax.all_gather(d_hidden, 'tp', axis=0, tiled=True)  10.3 us
    unnamed x29, local copies, waits for them, and re-layouts  8.09 us
  transfers between devices with their start and end apart: 38, of which 22 were waited for; matrix products, arithmetic and copies ran while one was open for 2% of the time, Pallas kernels for 9%

commit v1 on v0

--- a/solution.py
+++ b/solution.py
@@ -86,7 +86,6 @@
         out_specs=[VM] * 3,
         out_shape=[shape((64, 384)), shape((192, 384)), shape((256, 128))],
         name="dispatch",
-        compiler_params=room(4),
     )(pos, ids, gates, grads)
 
 
@@ -136,13 +135,47 @@
     )(table, *saved)
 
 
+def pack_kernel(*refs):
+    start = 0
+    for ref in refs[:-1]:
+        refs[-1][start : start + ref.shape[0], :] = ref[...]
+        start += ref.shape[0]
+
+
+def pack(*blocks):
+    return pl.pallas_call(
+        pack_kernel, out_shape=shape((512, 384)), name="pack", compiler_params=room(4)
+    )(*blocks)
+
+
+def beside_kernel(*refs):
+    for k in range(3):
+        refs[3][:, 384 * k : 384 * (k + 1)] = refs[k][...]
+
+
+def beside(*blocks):
+    return pl.pallas_call(
+        beside_kernel, out_shape=shape((512, 1152)), name="beside", compiler_params=room(6)
+    )(*blocks)
+
+
+def halves_kernel(near_a, far_a, near_b, far_b, top, bottom):
+    top[:, 0:1152] = near_a[0:256, :]
+    top[:, 1152:1536] = far_a[0:256, :]
+    bottom[:, 0:1152] = near_b[256:512, :]
+    bottom[:, 1152:1536] = far_b[256:512, :]
+
+
+def halves(*args):
+    return pl.pallas_call(
+        halves_kernel, out_shape=[shape((256, 1536))] * 2, name="halves", compiler_params=room(8)
+    )(*args)
+
+
 def act_first_kernel(table, *refs):
-    pieces, down_own, down_other, acc = refs[:9], refs[9], refs[10], refs[11]
+    pieces, down_own, down_other, acc = refs[:6], refs[6], refs[7], refs[8]
     for k, group in enumerate((0, 1, 3)):
-        top, bottom, far = pieces[3 * k : 3 * k + 3]
-        rows = jnp.concatenate(
-            [jnp.concatenate([top[...], bottom[...]], axis=0), far[...]], axis=1
-        )
+        rows = jnp.concatenate([pieces[2 * k][...], pieces[2 * k + 1][...]], axis=1)
         for side, down in enumerate((down_own, down_other)):
             columns = [
                 down[:, pl.ds(pl.multiple_of(table[4 * group + j] * 384, 384), 384)] for j in CHUNKS
@@ -159,7 +192,7 @@
 def act_first(table, pieces, down_own, down_other):
     return pl.pallas_call(
         act_first_kernel,
-        in_specs=[SM] + [VM] * 11,
+        in_specs=[SM] + [VM] * 8,
         out_specs=VM,
         out_shape=shape((512, 512), F32),
         name="act_first",
@@ -213,12 +246,14 @@
 
                 @pl.when(step == 4 // per * run + piece)
                 def _(total=total, run=run, group=group, chunk=chunk):
-                    if chunk == 3 and group != 2:
-                        outs[3 * run + 2][...] = total
+                    here = slice(384 * chunk, 384 * (chunk + 1))
+                    if group == 2:
+                        outs[0][here, :] = total[:, 0:256]
+                        outs[1][here, :] = total[:, 256:512]
+                    elif chunk == 3:
+                        outs[2 * run + 1][...] = total
                     else:
-                        here = slice(384 * chunk, 384 * (chunk + 1))
-                        outs[3 * run][here, :] = total[:, 0:256]
-                        outs[3 * run + 1][here, :] = total[:, 256:512]
+                        outs[2 * run][here, :] = total
 
 
 def part(table, grads, weights, groups, per):
@@ -235,7 +270,7 @@
 
     dims = []
     for group in groups:
-        dims += [(1536, 256)] * 2 if group == 2 else [(1152, 256), (1152, 256), (384, 512)]
+        dims += [(1536, 256)] * 2 if group == 2 else [(1152, 512), (384, 512)]
     return pl.pallas_call(
         functools.partial(part_kernel, groups, per),
         grid_spec=pltpu.PrefetchScalarGridSpec(
@@ -260,8 +295,10 @@
 def pairs_kernel(near_a, far_a, got_a, near_b, far_b, got_b, out_near_a, out_far_a, out_near_b, out_far_b):
     def some_rows(k, carry):
         here = pl.ds(pl.multiple_of(k * 128, 128), 128)
-        out_near_a[here, :] = add(near_a[here, :], got_a[here, :]).astype(BF)
-        out_near_b[here, :] = add(near_b[here, :], got_b[here, :]).astype(BF)
+        out_near_a[here, 0:256] = add(near_a[here, 0:256], got_a[here, :]).astype(BF)
+        out_near_a[here, 256:512] = near_a[here, 256:512]
+        out_near_b[here, 0:256] = near_b[here, 0:256]
+        out_near_b[here, 256:512] = add(near_b[here, 256:512], got_b[here, :]).astype(BF)
         return carry
 
     lax.fori_loop(0, 9, some_rows, 0)
@@ -274,41 +311,32 @@
 def add_pairs(*args):
     return pl.pallas_call(
         pairs_kernel,
-        out_shape=[shape((1152, 256)), shape((384, 512))] * 2,
+        out_shape=[shape((1152, 512)), shape((384, 512))] * 2,
         name="add_pairs",
         compiler_params=room(16),
     )(*args)
 
 
-def far_kernel(own, got1, got2, top, bottom):
-    total = add(own[...], got1[...], got2[...]).astype(BF)
-    top[...] = total[:, 0:256]
-    bottom[...] = total[:, 256:512]
+def far_kernel(own, got1, got2, out):
+    out[...] = add(own[...], got1[...], got2[...]).astype(BF)
 
 
 def middle_far(*args):
     return pl.pallas_call(
-        far_kernel,
-        out_shape=[shape((384, 256))] * 2,
-        name="middle_far",
-        compiler_params=room(6),
-    )(*args)
-
-
-def near_kernel(own_t, own_b, t1, t2, b1, b2, got_top, got_bottom, own, ahead, behind):
+        far_kernel, out_shape=shape((384, 512)), name="middle_far", compiler_params=room(6)
+    )(*args)
+
+
+def near_kernel(mine, got1, got2, far, own, ahead, behind):
     for k, out in enumerate((own, ahead, behind)):
 
         def some_rows(r, carry, k=k, out=out):
             to = pl.ds(pl.multiple_of(r * 128, 128), 128)
             here = pl.ds(pl.multiple_of(384 * k + r * 128, 128), 128)
-            top = add(own_t[here, :], t1[here, :], t2[here, :])
-            bottom = add(own_b[here, :], b1[here, :], b2[here, :])
+            total = add(mine[here, :], got1[here, :], got2[here, :])
             if k == 1:
-                top = top + got_top[to, :].astype(F32)
-            if k == 2:
-                bottom = bottom + got_bottom[to, :].astype(F32)
-            out[to, 0:256] = top.astype(out.dtype)
-            out[to, 256:512] = bottom.astype(out.dtype)
+                total = total + far[to, :].astype(F32)
+            out[to, :] = total.astype(out.dtype)
             return carry
 
         lax.fori_loop(0, 3, some_rows, 0)
@@ -391,29 +419,24 @@
     up_other = swap_core(up_own)
     factor_own, sent_factor = factors(table, saved_gate[0], saved_up[0])
 
-    rows = jnp.concatenate([*received, near, across], axis=0)
+    rows = pack(*received, near, across)
     ahead = shift_plane(rows, -1, True)
     behind = shift_plane(rows, 1, True)
-    top = jnp.concatenate([rows[:256], ahead[:256], behind[:256]], axis=1)
-    bottom = jnp.concatenate([rows[256:], ahead[256:], behind[256:]], axis=1)
-    top, bottom, sent_factor = lax.optimization_barrier((top, bottom, sent_factor))
+    near, sent_factor = lax.optimization_barrier((beside(rows, ahead, behind), sent_factor))
     factor_other = swap_core(sent_factor)
-    far_top = shift_plane(ahead[:256], -1, True)
-    far_bottom = shift_plane(behind[256:], 1, True)
-    far = jnp.concatenate([far_top, far_bottom], axis=0)
-
-    behind_bottom = shift_plane(bottom, 1, False)
-    ahead_top = shift_plane(top, -1, False)
+    far = shift_plane(ahead, -1, True)
+
+    behind_near = shift_plane(near, 1, False)
+    ahead_near = shift_plane(near, -1, False)
     behind_far = shift_plane(far, 1, False)
     ahead_far = shift_plane(far, -1, False)
-    behind_top = shift_plane(top, 1, False)
-    ahead_bottom = shift_plane(bottom, -1, False)
-    last_bottom = shift_plane(jnp.concatenate([behind_bottom, behind_far[256:]], axis=1), 1, False)
-    last_top = shift_plane(jnp.concatenate([ahead_top, ahead_far[:256]], axis=1), -1, False)
+    top, bottom = halves(ahead_near, ahead_far, behind_near, behind_far)
+    last_top = shift_plane(top, -1, False)
+    last_bottom = shift_plane(bottom, 1, False)
 
     acc = act_first(
         table,
-        (top, bottom, far, ahead_top, ahead_bottom, ahead_far, behind_top, behind_bottom, behind_far),
+        (near, far, ahead_near, ahead_far, behind_near, behind_far),
         down_own,
         down_other,
     )
@@ -423,32 +446,18 @@
     far_top, far_bottom = part(table, grads, weights, (2,), 2)
     got_top = shift_plane(far_top, 1, False)
     got_bottom = shift_plane(far_bottom, -1, False)
-    near_parts = part(table, grads, weights, (1, 3), 2)
-    ahead_top, ahead_bottom, ahead_far, behind_top, behind_bottom, behind_far = near_parts
-    from_behind_bottom = shift_plane(ahead_bottom, 1, False)
-    from_ahead_top = shift_plane(behind_top, -1, False)
-    own_top, own_bottom, own_far = part(table, grads, weights, (0,), 1)
+    ahead_near, ahead_far, behind_near, behind_far = part(table, grads, weights, (1, 3), 2)
+    own_near, own_far = part(table, grads, weights, (0,), 1)
     up_near, up_far, down_near, down_far = add_pairs(
-        ahead_top, ahead_far, got_top, behind_bottom, behind_far, got_bottom
+        ahead_near, ahead_far, got_top, behind_near, behind_far, got_bottom
     )
     from_behind_far = shift_plane(up_far, 1, False)
     from_ahead_far = shift_plane(down_far, -1, False)
-    from_behind_top = shift_plane(up_near, 1, False)
-    from_ahead_bottom = shift_plane(down_near, -1, False)
-
-    far_top, far_bottom = middle_far(own_far, from_behind_far, from_ahead_far)
-    got_top = shift_plane(far_top, 1, True)
-    got_bottom = shift_plane(far_bottom, -1, True)
-    own, to_ahead, to_behind = middle_near(
-        own_top,
-        own_bottom,
-        from_behind_top,
-        from_ahead_top,
-        from_behind_bottom,
-        from_ahead_bottom,
-        got_top,
-        got_bottom,
-    )
+    from_behind_near = shift_plane(up_near, 1, False)
+    from_ahead_near = shift_plane(down_near, -1, False)
+
+    got_far = shift_plane(middle_far(own_far, from_behind_far, from_ahead_far), 1, True)
+    own, to_ahead, to_behind = middle_near(own_near, from_behind_near, from_ahead_near, got_far)
     from_behind = shift_plane(to_ahead, 1, True)
     from_ahead = shift_plane(to_behind, -1, True)
     *back, near, across = last(own, from_behind, from_ahead)

time: 218 us -> 218 us (level)
  starting transfers between devices: 62.5 us -> 50.1 us
  waiting for transfers between devices: 70.6 us -> 81 us
  local copies, waits for them, and re-layouts: 11 us -> 7.48 us
  Pallas kernels: 27 us -> 29.9 us
    ppermute x24 -> x18, starting transfers between devices: 41.9 us -> 28.1 us  [shift_plane(): return lax.ppermute(value, ('etp', 'tp'), pairs)]
    ppermute x24 -> x18, waiting for transfers between devices: 54 us -> 65 us  [shift_plane(): return lax.ppermute(value, ('etp', 'tp'), pairs)]
    pallas_call x3 -> x6, Pallas kernels: 3.73 us -> 5.58 us  [the longest x1 3.77 us: act_first(): pl.pallas_call(act_first_kernel, in_specs=[SM] + [VM] * 8, out_specs=VM,...]
    unnamed x29 -> x30, local copies, waits for them, and re-layouts: 8.09 us -> 6.59 us
  transfers between devices with their start and end apart: 38 -> 32, of which waited for: 22 -> 16; matrix products, arithmetic and copies ran while one was open for 2% -> 0% of each run, Pallas kernels for 9% -> 9%
where the time goes in v1:
time: 218 us; the launch traced here: 215 us
  waiting for transfers between devices  81 us (37%)
  starting transfers between devices  50.1 us (23%)
  blocking collectives  44.1 us (20%)
  Pallas kernels  29.9 us (14%)
  local copies, waits for them, and re-layouts  7.48 us (3%)
    ppermute x18, waiting for transfers between devices, shift_plane(): return lax.ppermute(value, ('etp', 'tp'), pairs)  65 us
    all_to_all x1, blocking collectives, body(): lax.all_to_all(head_partial.reshape(16, 32, 1536), 'etp', 0, 0, tiled=True)  33.7 us
    ppermute x18, starting transfers between devices, shift_plane(): return lax.ppermute(value, ('etp', 'tp'), pairs)  28.1 us
    ppermute x8, starting transfers between devices, shift_z(): return lax.ppermute(value, ('expert', 'tp'), pairs)  20.9 us
    pallas_call x3, Pallas kernels, part(): pl.pallas_call(functools.partial(part_kernel, groups, per), grid_spec=plt...  15.9 us
    ppermute x8, waiting for transfers between devices, shift_z(): return lax.ppermute(value, ('expert', 'tp'), pairs)  15.8 us
    all_gather x1, blocking collectives, body(): lax.all_gather(d_hidden, 'tp', axis=0, tiled=True)  10.3 us
    unnamed x30, local copies, waits for them, and re-layouts  6.59 us
  transfers between devices with their start and end apart: 32, of which 16 were waited for; matrix products, arithmetic and copies ran while one was open for 0% of the time, Pallas kernels for 9%

profile of v1, /device:TPU:2, one launch (start us, length us, event | category | flops | bytes accessed | tf_op | source)
XLA Modules:
  0.0 215.0 jit_solution(13941662930910106937)
XLA Ops:
  0.6 0.5 compare_select_fusion.9.pos
  1.2 2.0 dispatch.1
  3.1 0.5 collective-permute-start.16
  3.6 0.9 fusion.11
  4.5 0.2 collective-permute-done.2
  4.7 2.0 collective-permute-start.3
  6.7 3.3 %collective-permute-start.4 = (bf16[128,384]{1,0:T(8,128)(2,1)S(1)}, bf16[128,384]{1,0:T(8,128)(2,1)S(1)}, u32[]{:S(2)}, u32[]{:S(2)}) collective-permute-start(bf16[128,384]{1,0:T(8,128)(2,1)S(1)} %pad_maximum_fusion.2), channel_id=1, source_target_pairs={{0,128},{1,131},{2,130},{3,129},{64,192},{65,195},{66,194},{67,193... | collective-permute-start | bytes 294920 | tf_op jit(solution)/shard_map/ppermute | solution.py:51
  10.1 4.1 %collective-permute-start.5 = (bf16[128,384]{1,0:T(8,128)(2,1)S(1)}, bf16[128,384]{1,0:T(8,128)(2,1)S(1)}, u32[]{:S(2)}, u32[]{:S(2)}) collective-permute-start(bf16[128,384]{1,0:T(8,128)(2,1)S(1)} %pad_maximum_fusion.3), channel_id=1, source_target_pairs={{0,192},{1,67},{2,194},{3,65},{64,2},{65,131},{66,0},{67,129},{128... | collective-permute-start | bytes 294920 | tf_op jit(solution)/shard_map/ppermute | solution.py:51
  14.2 0.6 collective-permute-start.6
  14.8 7.8 %collective-permute-done.6.refs_4_ = bf16[64,384]{1,0:T(8,128)(2,1)S(1)} collective-permute-done((bf16[64,384]{1,0:T(8,128)(2,1)S(1)}, bf16[64,384]{1,0:T(8,128)(2,1)S(1)}, u32[]{:S(2)}, u32[]{:S(2)}) %collective-permute-start.6) | collective-permute-done | bytes 49184 | tf_op jit(solution)/shard_map/ppermute | solution.py:51
  22.6 0.6 collective-permute-start.7
  23.2 0.4 collective-permute-start
  23.7 6.7 %collective-permute-done.7.refs_1_ = bf16[512,384]{1,0:T(8,128)(2,1)S(1)} collective-permute-done((bf16[512,384]{1,0:T(8,128)(2,1)S(1)}, bf16[512,384]{1,0:T(8,128)(2,1)S(1)}, u32[]{:S(2)}, u32[]{:S(2)}) %collective-permute-start.7) | collective-permute-done | bytes 393248 | tf_op jit(solution)/shard_map/ppermute | solution.py:41
  30.5 0.8 collective-permute-start.10
  31.3 0.7 copy-done.8
  32.0 1.2 collective-permute-start.8
  33.2 0.8 copy-done.3
  34.0 4.3 %collective-permute-done.10.refs_1_ = bf16[512,384]{1,0:T(8,128)(2,1)} collective-permute-done((bf16[512,384]{1,0:T(8,128)(2,1)S(1)}, bf16[512,384]{1,0:T(8,128)(2,1)}, u32[]{:S(2)}, u32[]{:S(2)}) %collective-permute-start.10) | collective-permute-done | bytes 393248 | tf_op jit(solution)/shard_map/ppermute | solution.py:41
  38.3 3.0 %collective-permute-start.11 = (bf16[512,384]{1,0:T(8,128)(2,1)}, bf16[512,384]{1,0:T(8,128)(2,1)S(1)}, u32[]{:S(2)}, u32[]{:S(2)}) collective-permute-start(bf16[512,384]{1,0:T(8,128)(2,1)} %collective-permute-done.10.refs_1_), channel_id=1, source_target_pairs={{0,48},{1,13},{2,50},{3,15},{4,52},{5,1},{6,54},{7,3},{8,56},{9,5}... | collective-permute-start | bytes 1179656 | tf_op jit(solution)/shard_map/ppermute | solution.py:41
  41.5 0.8 copy-done.10
  42.2 1.6 collective-permute-start.13
  43.9 1.1 copy-done.6
  44.9 1.0 copy-done.7
  46.0 1.9 factors.1
  48.0 1.0 copy-done.11
  49.1 3.0 %collective-permute-start.12 = (bf16[512,1152]{1,0:T(8,128)(2,1)S(1)}, bf16[512,1152]{1,0:T(8,128)(2,1)S(1)}, u32[]{:S(2)}, u32[]{:S(2)}) collective-permute-start(bf16[512,1152]{1,0:T(8,128)(2,1)S(1)} %beside.1.refs_0_), channel_id=1, source_target_pairs={{0,16},{1,5},{2,18},{3,7},{4,20},{5,9},{6,22},{7,11},{8,24},{9,13}... | collective-permute-start | bytes 3538952 | tf_op jit(solution)/shard_map/ppermute | solution.py:41
  52.1 1.3 collective-permute-start.9
  53.5 13.1 %collective-permute-done.12.near_b.refs_4_ = bf16[512,1152]{1,0:T(8,128)(2,1)S(1)} collective-permute-done((bf16[512,1152]{1,0:T(8,128)(2,1)S(1)}, bf16[512,1152]{1,0:T(8,128)(2,1)S(1)}, u32[]{:S(2)}, u32[]{:S(2)}) %collective-permute-start.12) | collective-permute-done | bytes 1179680 | tf_op jit(solution)/shard_map/ppermute | solution.py:41
  66.6 1.7 collective-permute-done.9.near_a.refs_2_
  68.3 1.1 halves.1
  69.4 2.8 %collective-permute-start.14 = (bf16[256,1536]{1,0:T(8,128)(2,1)S(1)}, bf16[256,1536]{1,0:T(8,128)(2,1)S(1)}, u32[]{:S(2)}, u32[]{:S(2)}) collective-permute-start(bf16[256,1536]{1,0:T(8,128)(2,1)S(1)} %get-tuple-element.36), channel_id=1, source_target_pairs={{0,48},{1,13},{2,50},{3,15},{4,52},{5,1},{6,54},{7,3},{8,56},{9,5}... | collective-permute-start | bytes 2359304 | tf_op jit(solution)/shard_map/ppermute | solution.py:41
  72.3 3.8 %act_first.1.refs_10_ = f32[512,512]{1,0:T(8,128)S(1)} custom-call(s32[32]{0:T(128)S(1)} %compare_select_fusion.8.table, bf16[512,1152]{1,0:T(8,128)(2,1)S(1)} %beside.1.refs_0_, bf16[512,384]{1,0:T(8,128)(2,1)} %collective-permute-done.10.refs_1_, bf16[512,1152]{1,0:T(8,128)(2,1)S(1)} %collective-permute-done.9.near_a.refs_2_, ...), custom_call_target="tpu_custom_call" | custom-call | tf_op jit(solution)/shard_map/act_first/pallas_call | solution.py:193
  76.0 5.7 %collective-permute-done.14.refs_0_ = bf16[256,1536]{1,0:T(8,128)(2,1)S(1)} collective-permute-done((bf16[256,1536]{1,0:T(8,128)(2,1)S(1)}, bf16[256,1536]{1,0:T(8,128)(2,1)S(1)}, u32[]{:S(2)}, u32[]{:S(2)}) %collective-permute-start.14) | collective-permute-done | bytes 786464 | tf_op jit(solution)/shard_map/ppermute | solution.py:41
  81.8 3.7 %collective-permute-done.15.refs_1_ = bf16[256,1536]{1,0:T(8,128)(2,1)S(1)} collective-permute-done((bf16[256,1536]{1,0:T(8,128)(2,1)S(1)}, bf16[256,1536]{1,0:T(8,128)(2,1)S(1)}, u32[]{:S(2)}, u32[]{:S(2)}) %collective-permute-start.15) | collective-permute-done | bytes 786464 | tf_op jit(solution)/shard_map/ppermute | solution.py:41
  85.5 1.7 act_last.1.refs_4_.refs_8_
  87.2 0.2 copy-done.1
  87.3 1.0 copy-done.2
  88.3 4.4 %shard_map.106 = (bf16[1536,256]{1,0:T(8,128)(2,1)S(1)}, bf16[1536,256]{1,0:T(8,128)(2,1)S(1)}) custom-call(s32[32]{0:T(128)S(1)} %compare_select_fusion.8.table, bf16[6144,256]{1,0:T(8,128)(2,1)S(1)} %bitcast.15, bf16[6144,256]{1,0:T(8,128)(2,1)S(1)} %bitcast.16, bf16[6144,256]{1,0:T(8,128)(2,1)} %collective-permute-done.refs_1_.refs_2_.refs_3_, ...), custom_call_target="tpu_custom_call" | custom-call | tf_op jit(solution)/shard_map/pallas_call | solution.py:274
  92.8 3.2 %collective-permute-start.19 = (bf16[1536,256]{1,0:T(8,128)(2,1)S(1)}, bf16[1536,256]{1,0:T(8,128)(2,1)S(1)}, u32[]{:S(2)}, u32[]{:S(2)}) collective-permute-start(bf16[1536,256]{1,0:T(8,128)(2,1)S(1)} %get-tuple-element.46), channel_id=1, source_target_pairs={{0,48},{1,13},{2,50},{3,15},{4,52},{5,1},{6,54},{7,3},{8,56},{9,5}... | collective-permute-start | bytes 2359304 | tf_op jit(solution)/shard_map/ppermute | solution.py:41
  96.0 7.0 %shard_map.105 = (bf16[1152,512]{1,0:T(8,128)(2,1)S(1)}, bf16[384,512]{1,0:T(8,128)(2,1)S(1)}, bf16[1152,512]{1,0:T(8,128)(2,1)S(1)}, bf16[384,512]{1,0:T(8,128)(2,1)S(1)}) custom-call(s32[32]{0:T(128)S(1)} %compare_select_fusion.8.table, bf16[6144,256]{1,0:T(8,128)(2,1)S(1)} %bitcast.17, bf16[6144,256]{1,0:T(8,128)(2,1)S(1)} %bitcast.18, ...), custom_call_target="tpu_custom_call" | custom-call | tf_op jit(solution)/shard_map/pallas_call | solution.py:274
  103.0 3.0 %collective-permute-done.18.got_a = bf16[1536,256]{1,0:T(8,128)(2,1)S(1)} collective-permute-done((bf16[1536,256]{1,0:T(8,128)(2,1)S(1)}, bf16[1536,256]{1,0:T(8,128)(2,1)S(1)}, u32[]{:S(2)}, u32[]{:S(2)}) %collective-permute-start.18) | collective-permute-done | bytes 786464 | tf_op jit(solution)/shard_map/ppermute | solution.py:41
  106.0 0.4 add_pairs.1
  106.5 3.3 %collective-permute-start.21 = (bf16[1152,512]{1,0:T(8,128)(2,1)S(1)}, bf16[1152,512]{1,0:T(8,128)(2,1)S(1)}, u32[]{:S(2)}, u32[]{:S(2)}) collective-permute-start(bf16[1152,512]{1,0:T(8,128)(2,1)S(1)} %get-tuple-element.48), channel_id=1, source_target_pairs={{0,48},{1,13},{2,50},{3,15},{4,52},{5,1},{6,54},{7,3},{8,56},{9,5}... | collective-permute-start | bytes 3538952 | tf_op jit(solution)/shard_map/ppermute | solution.py:41
  109.8 3.2 %collective-permute-start.23 = (bf16[384,512]{1,0:T(8,128)(2,1)S(1)}, bf16[384,512]{1,0:T(8,128)(2,1)S(1)}, u32[]{:S(2)}, u32[]{:S(2)}) collective-permute-start(bf16[384,512]{1,0:T(8,128)(2,1)S(1)} %get-tuple-element.51), channel_id=1, source_target_pairs={{0,48},{1,13},{2,50},{3,15},{4,52},{5,1},{6,54},{7,3},{8,56},{9,5}... | collective-permute-start | bytes 1179656 | tf_op jit(solution)/shard_map/ppermute | solution.py:41
  113.0 4.6 %shard_map.104 = (bf16[1152,512]{1,0:T(8,128)(2,1)S(1)}, bf16[384,512]{1,0:T(8,128)(2,1)S(1)}) custom-call(s32[32]{0:T(128)S(1)} %compare_select_fusion.8.table, bf16[6144,256]{1,0:T(8,128)(2,1)S(1)} %bitcast.19, bf16[6144,256]{1,0:T(8,128)(2,1)} %collective-permute-done.refs_1_.refs_2_.refs_3_, bf16[6144,256]{1,0:T(8,128)(2,1)S(1)} %bitcast.25, ...), custom_call_target="tpu_custom_call" | custom-call | tf_op jit(solution)/shard_map/pallas_call | solution.py:274
  117.6 10.5 %collective-permute-done.22.got1 = bf16[384,512]{1,0:T(8,128)(2,1)S(1)} collective-permute-done((bf16[384,512]{1,0:T(8,128)(2,1)S(1)}, bf16[384,512]{1,0:T(8,128)(2,1)S(1)}, u32[]{:S(2)}, u32[]{:S(2)}) %collective-permute-start.22) | collective-permute-done | bytes 393248 | tf_op jit(solution)/shard_map/ppermute | solution.py:41
  128.3 10.5 %collective-permute-done.24.far = bf16[384,512]{1,0:T(8,128)(2,1)S(1)} collective-permute-done((bf16[384,512]{1,0:T(8,128)(2,1)S(1)}, bf16[384,512]{1,0:T(8,128)(2,1)S(1)}, u32[]{:S(2)}, u32[]{:S(2)}) %collective-permute-start.24) | collective-permute-done | bytes 393248 | tf_op jit(solution)/shard_map/ppermute | solution.py:41
  138.8 0.5 middle_near.1
  139.3 0.3 collective-permute-start.25
  139.6 3.3 %collective-permute-start.26 = (bf16[384,512]{1,0:T(8,128)(2,1)S(1)}, bf16[384,512]{1,0:T(8,128)(2,1)S(1)}, u32[]{:S(2)}, u32[]{:S(2)}) collective-permute-start(bf16[384,512]{1,0:T(8,128)(2,1)S(1)} %get-tuple-element.54), channel_id=1, source_target_pairs={{0,12},{1,49},{2,14},{3,51},{4,0},{5,53},{6,2},{7,55},{8,4},{9,57}... | collective-permute-start | bytes 1179656 | tf_op jit(solution)/shard_map/ppermute | solution.py:41
  143.0 5.7 %collective-permute-done.25.got1 = bf16[384,512]{1,0:T(8,128)(2,1)S(1)} collective-permute-done((bf16[384,512]{1,0:T(8,128)(2,1)S(1)}, bf16[384,512]{1,0:T(8,128)(2,1)S(1)}, u32[]{:S(2)}, u32[]{:S(2)}) %collective-permute-start.25) | collective-permute-done | bytes 393248 | tf_op jit(solution)/shard_map/ppermute | solution.py:41
  148.6 0.2 last.1
  148.8 3.4 %collective-permute-start.27 = (bf16[128,384]{1,0:T(8,128)(2,1)S(1)}, bf16[128,384]{1,0:T(8,128)(2,1)S(1)}, u32[]{:S(2)}, u32[]{:S(2)}) collective-permute-start(bf16[128,384]{1,0:T(8,128)(2,1)S(1)} %get-tuple-element.55), channel_id=1, source_target_pairs={{0,194},{1,65},{2,192},{3,67},{64,0},{65,129},{66,2},{67,131},{128... | collective-permute-start | bytes 294920 | tf_op jit(solution)/shard_map/ppermute | solution.py:51
  152.2 0.7 collective-permute-start.28
  152.8 3.6 %collective-permute-start.29 = (bf16[128,384]{1,0:T(8,128)(2,1)S(1)}, bf16[128,384]{1,0:T(8,128)(2,1)S(1)}, u32[]{:S(2)}, u32[]{:S(2)}) collective-permute-start(bf16[128,384]{1,0:T(8,128)(2,1)S(1)} %get-tuple-element.57), channel_id=1, source_target_pairs={{0,66},{1,193},{2,64},{3,195},{64,130},{65,3},{66,128},{67,1},{128... | collective-permute-start | bytes 294920 | tf_op jit(solution)/shard_map/ppermute | solution.py:51
  156.5 2.1 collective-permute-done.28.from2
  158.6 1.1 collective-permute-done.29.from3
  159.8 3.2 %collective-permute-start.31 = (bf16[64,384]{1,0:T(8,128)(2,1)S(1)}, bf16[64,384]{1,0:T(8,128)(2,1)S(1)}, u32[]{:S(2)}, u32[]{:S(2)}) collective-permute-start(bf16[64,384]{1,0:T(8,128)(2,1)S(1)} %get-tuple-element.59), channel_id=1, source_target_pairs={{0,2},{1,3},{2,0},{3,1},{64,66},{65,67},{66,64},{67,65},{128,130},... | collective-permute-start | bytes 147464 | tf_op jit(solution)/shard_map/ppermute | solution.py:51
  163.0 4.8 %collective-permute-done.31.across = bf16[64,384]{1,0:T(8,128)(2,1)S(1)} collective-permute-done((bf16[64,384]{1,0:T(8,128)(2,1)S(1)}, bf16[64,384]{1,0:T(8,128)(2,1)S(1)}, u32[]{:S(2)}, u32[]{:S(2)}) %collective-permute-start.31) | collective-permute-done | bytes 49184 | tf_op jit(solution)/shard_map/ppermute | solution.py:51
  167.9 0.9 combine.1
  168.8 10.3 %all_gather.3.tokens = bf16[512,384]{1,0:T(8,128)(2,1)S(1)} all-gather(bf16[128,384]{1,0:T(8,128)(2,1)} %combine.1), channel_id=1, replica_groups=mesh['expert'=4,'etp'=16,'tp'=4] {'tp'}, dimensions={0}, use_global_device_ids=true | all-gather | bytes 491520 | tf_op jit(solution)/shard_map/all_gather | solution.py:470
  179.2 1.2 heads.1
  180.4 33.7 %all_to_all.5 = bf16[16,32,1536]{2,1,0:T(8,128)(2,1)S(1)} all-to-all(bf16[16,32,1536]{2,1,0:T(8,128)(2,1)S(1)} %bitcast.26), channel_id=1, replica_groups=mesh['expert'=4,'etp'=16,'tp'=4] {'etp'}, dimensions={0} | all-to-all | bytes 3145728 | tf_op jit(solution)/shard_map/all_to_all | solution.py:471
  214.1 0.9 reduce_sum.12
  (60 shorter events, 1.1 us)
Async XLA Ops:
  3.1 11.1 %copy-start.14 = (bf16[64,384]{1,0:T(8,128)(2,1)S(1)}, bf16[64,384]{1,0:T(8,128)(2,1)}, u32[]{:S(2)}) copy-start(bf16[64,384]{1,0:T(8,128)(2,1)} %get-tuple-element.33.refs_3_) | copy-start | bytes 147460
  3.1 1.6 collective-permute-start.2
  3.1 69.1 %collective-permute-start.16 = (bf16[256,6144]{1,0:T(8,128)(2,1)}, bf16[256,6144]{1,0:T(8,128)(2,1)S(1)}, u32[]{:S(2)}, u32[]{:S(2)}) collective-permute-start(bf16[256,6144]{1,0:T(8,128)(2,1)} %bitcast.8), channel_id=1, source_target_pairs={{0,1},{1,0},{2,3},{3,2},{4,5},{5,4},{6,7},{7,6},{8,9},{9,8},{10,11... | collective-permute-start | bytes 9437192 | tf_op jit(solution)/shard_map/ppermute | solution.py:55
  4.7 17.8 %collective-permute-start.3 = (bf16[128,384]{1,0:T(8,128)(2,1)S(1)}, bf16[128,384]{1,0:T(8,128)(2,1)S(1)}, u32[]{:S(2)}, u32[]{:S(2)}) collective-permute-start(bf16[128,384]{1,0:T(8,128)(2,1)S(1)} %pad_maximum_fusion.1), channel_id=1, source_target_pairs={{0,64},{1,195},{2,66},{3,193},{64,128},{65,1},{66,130},{67,3},{128... | collective-permute-start | bytes 294920 | tf_op jit(solution)/shard_map/ppermute | solution.py:51
  6.7 15.8 %collective-permute-start.4 = (bf16[128,384]{1,0:T(8,128)(2,1)S(1)}, bf16[128,384]{1,0:T(8,128)(2,1)S(1)}, u32[]{:S(2)}, u32[]{:S(2)}) collective-permute-start(bf16[128,384]{1,0:T(8,128)(2,1)S(1)} %pad_maximum_fusion.2), channel_id=1, source_target_pairs={{0,128},{1,131},{2,130},{3,129},{64,192},{65,195},{66,194},{67,193... | collective-permute-start | bytes 294920 | tf_op jit(solution)/shard_map/ppermute | solution.py:51
  10.1 12.4 %collective-permute-start.5 = (bf16[128,384]{1,0:T(8,128)(2,1)S(1)}, bf16[128,384]{1,0:T(8,128)(2,1)S(1)}, u32[]{:S(2)}, u32[]{:S(2)}) collective-permute-start(bf16[128,384]{1,0:T(8,128)(2,1)S(1)} %pad_maximum_fusion.3), channel_id=1, source_target_pairs={{0,192},{1,67},{2,194},{3,65},{64,2},{65,131},{66,0},{67,129},{128... | collective-permute-start | bytes 294920 | tf_op jit(solution)/shard_map/ppermute | solution.py:51
  14.2 8.3 %collective-permute-start.6 = (bf16[64,384]{1,0:T(8,128)(2,1)S(1)}, bf16[64,384]{1,0:T(8,128)(2,1)S(1)}, u32[]{:S(2)}, u32[]{:S(2)}) collective-permute-start(bf16[64,384]{1,0:T(8,128)(2,1)S(1)} %copy-done.14), channel_id=1, source_target_pairs={{0,2},{1,3},{2,0},{3,1},{64,66},{65,67},{66,64},{67,65},{128,130},... | collective-permute-start | bytes 147464 | tf_op jit(solution)/shard_map/ppermute | solution.py:51
  22.6 7.9 %collective-permute-start.7 = (bf16[512,384]{1,0:T(8,128)(2,1)S(1)}, bf16[512,384]{1,0:T(8,128)(2,1)S(1)}, u32[]{:S(2)}, u32[]{:S(2)}) collective-permute-start(bf16[512,384]{1,0:T(8,128)(2,1)S(1)} %pack.1.refs_0_), channel_id=1, source_target_pairs={{0,12},{1,49},{2,14},{3,51},{4,0},{5,53},{6,2},{7,55},{8,4},{9,57}... | collective-permute-start | bytes 1179656 | tf_op jit(solution)/shard_map/ppermute | solution.py:41
  23.2 63.9 %collective-permute-start = (bf16[6144,256]{1,0:T(8,128)(2,1)}, bf16[6144,256]{1,0:T(8,128)(2,1)}, u32[]{:S(2)}, u32[]{:S(2)}) collective-permute-start(bf16[6144,256]{1,0:T(8,128)(2,1)} %bitcast.14), channel_id=1, source_target_pairs={{0,1},{1,0},{2,3},{3,2},{4,5},{5,4},{6,7},{7,6},{8,9},{9,8},{10,11... | collective-permute-start | bytes 9437192 | tf_op jit(solution)/shard_map/ppermute | solution.py:55
  23.6 63.6 %collective-permute-start.1 = (bf16[6144,256]{1,0:T(8,128)(2,1)}, bf16[6144,256]{1,0:T(8,128)(2,1)}, u32[]{:S(2)}, u32[]{:S(2)}) collective-permute-start(bf16[6144,256]{1,0:T(8,128)(2,1)} %bitcast.20), channel_id=1, source_target_pairs={{0,1},{1,0},{2,3},{3,2},{4,5},{5,4},{6,7},{7,6},{8,9},{9,8},{10,11... | collective-permute-start | bytes 9437192 | tf_op jit(solution)/shard_map/ppermute | solution.py:55
  30.5 7.9 %collective-permute-start.10 = (bf16[512,384]{1,0:T(8,128)(2,1)S(1)}, bf16[512,384]{1,0:T(8,128)(2,1)}, u32[]{:S(2)}, u32[]{:S(2)}) collective-permute-start(bf16[512,384]{1,0:T(8,128)(2,1)S(1)} %collective-permute-done.7.refs_1_), channel_id=1, source_target_pairs={{0,12},{1,49},{2,14},{3,51},{4,0},{5,53},{6,2},{7,55},{8,4},{9,57}... | collective-permute-start | bytes 1179656 | tf_op jit(solution)/shard_map/ppermute | solution.py:41
  31.3 0.7 copy-start.8
  32.0 9.4 %collective-permute-start.8 = (bf16[512,384]{1,0:T(8,128)(2,1)S(1)}, bf16[512,384]{1,0:T(8,128)(2,1)S(1)}, u32[]{:S(2)}, u32[]{:S(2)}) collective-permute-start(bf16[512,384]{1,0:T(8,128)(2,1)S(1)} %pack.1.refs_0_), channel_id=1, source_target_pairs={{0,4},{1,17},{2,6},{3,19},{4,8},{5,21},{6,10},{7,23},{8,12},{9,25}... | collective-permute-start | bytes 1179656 | tf_op jit(solution)/shard_map/ppermute | solution.py:41
  33.2 0.8 copy-start.3
  38.3 10.7 %collective-permute-start.11 = (bf16[512,384]{1,0:T(8,128)(2,1)}, bf16[512,384]{1,0:T(8,128)(2,1)S(1)}, u32[]{:S(2)}, u32[]{:S(2)}) collective-permute-start(bf16[512,384]{1,0:T(8,128)(2,1)} %collective-permute-done.10.refs_1_), channel_id=1, source_target_pairs={{0,48},{1,13},{2,50},{3,15},{4,52},{5,1},{6,54},{7,3},{8,56},{9,5}... | collective-permute-start | bytes 1179656 | tf_op jit(solution)/shard_map/ppermute | solution.py:41
  41.5 0.8 copy-start.10
  42.2 9.9 %collective-permute-start.13 = (bf16[512,384]{1,0:T(8,128)(2,1)}, bf16[512,384]{1,0:T(8,128)(2,1)}, u32[]{:S(2)}, u32[]{:S(2)}) collective-permute-start(bf16[512,384]{1,0:T(8,128)(2,1)} %collective-permute-done.10.refs_1_), channel_id=1, source_target_pairs={{0,16},{1,5},{2,18},{3,7},{4,20},{5,9},{6,22},{7,11},{8,24},{9,13}... | collective-permute-start | bytes 1179656 | tf_op jit(solution)/shard_map/ppermute | solution.py:41
  43.8 4.1 %copy-start.4 = (bf16[512,384]{1,0:T(8,128)(2,1)S(1)}, bf16[512,384]{1,0:T(8,128)(2,1)}, u32[]{:S(2)}) copy-start(bf16[512,384]{1,0:T(8,128)(2,1)} %copy-done.3) | copy-start | bytes 1179652
  43.9 1.1 copy-start.6
  44.9 1.0 copy-start.7
  46.0 1.9 copy-start.9
  47.9 1.0 copy-start.11
  49.0 23.2 %copy-start = (bf16[1,256,6144]{2,1,0:T(8,128)(2,1)S(1)}, bf16[1,256,6144]{2,1,0:T(8,128)(2,1)}, u32[]{:S(2)}) copy-start(bf16[1,256,6144]{2,1,0:T(8,128)(2,1)} %param.16) | copy-start | bytes 9437188
  49.1 17.5 %collective-permute-start.12 = (bf16[512,1152]{1,0:T(8,128)(2,1)S(1)}, bf16[512,1152]{1,0:T(8,128)(2,1)S(1)}, u32[]{:S(2)}, u32[]{:S(2)}) collective-permute-start(bf16[512,1152]{1,0:T(8,128)(2,1)S(1)} %beside.1.refs_0_), channel_id=1, source_target_pairs={{0,16},{1,5},{2,18},{3,7},{4,20},{5,9},{6,22},{7,11},{8,24},{9,13}... | collective-permute-start | bytes 3538952 | tf_op jit(solution)/shard_map/ppermute | solution.py:41
  52.1 16.2 %collective-permute-start.9 = (bf16[512,1152]{1,0:T(8,128)(2,1)S(1)}, bf16[512,1152]{1,0:T(8,128)(2,1)S(1)}, u32[]{:S(2)}, u32[]{:S(2)}) collective-permute-start(bf16[512,1152]{1,0:T(8,128)(2,1)S(1)} %beside.1.refs_0_), channel_id=1, source_target_pairs={{0,48},{1,13},{2,50},{3,15},{4,52},{5,1},{6,54},{7,3},{8,56},{9,5}... | collective-permute-start | bytes 3538952 | tf_op jit(solution)/shard_map/ppermute | solution.py:41
  66.6 9.5 %collective-permute-start.17 = (f32[512,512]{1,0:T(8,128)S(1)}, f32[512,512]{1,0:T(8,128)S(1)}, u32[]{:S(2)}, u32[]{:S(2)}) collective-permute-start(f32[512,512]{1,0:T(8,128)S(1)} %get-tuple-element.39), channel_id=1, source_target_pairs={{0,1},{1,0},{2,3},{3,2},{4,5},{5,4},{6,7},{7,6},{8,9},{9,8},{10,11... | collective-permute-start | bytes 3145736 | tf_op jit(solution)/shard_map/ppermute | solution.py:55
  69.4 12.3 %collective-permute-start.14 = (bf16[256,1536]{1,0:T(8,128)(2,1)S(1)}, bf16[256,1536]{1,0:T(8,128)(2,1)S(1)}, u32[]{:S(2)}, u32[]{:S(2)}) collective-permute-start(bf16[256,1536]{1,0:T(8,128)(2,1)S(1)} %get-tuple-element.36), channel_id=1, source_target_pairs={{0,48},{1,13},{2,50},{3,15},{4,52},{5,1},{6,54},{7,3},{8,56},{9,5}... | collective-permute-start | bytes 2359304 | tf_op jit(solution)/shard_map/ppermute | solution.py:41
  72.2 13.2 %collective-permute-start.15 = (bf16[256,1536]{1,0:T(8,128)(2,1)S(1)}, bf16[256,1536]{1,0:T(8,128)(2,1)S(1)}, u32[]{:S(2)}, u32[]{:S(2)}) collective-permute-start(bf16[256,1536]{1,0:T(8,128)(2,1)S(1)} %get-tuple-element.37), channel_id=1, source_target_pairs={{0,16},{1,5},{2,18},{3,7},{4,20},{5,9},{6,22},{7,11},{8,24},{9,13}... | collective-permute-start | bytes 2359304 | tf_op jit(solution)/shard_map/ppermute | solution.py:41
  85.4 1.9 copy-start.1
  85.5 2.8 %copy-start.2 = (bf16[1,6144,256]{2,1,0:T(8,128)(2,1)S(1)}, bf16[1,6144,256]{2,1,0:T(8,128)(2,1)}, u32[]{:S(2)}) copy-start(bf16[1,6144,256]{2,1,0:T(8,128)(2,1)} %param.15) | copy-start | bytes 9437188
  92.7 13.3 %collective-permute-start.18 = (bf16[1536,256]{1,0:T(8,128)(2,1)S(1)}, bf16[1536,256]{1,0:T(8,128)(2,1)S(1)}, u32[]{:S(2)}, u32[]{:S(2)}) collective-permute-start(bf16[1536,256]{1,0:T(8,128)(2,1)S(1)} %get-tuple-element.43), channel_id=1, source_target_pairs={{0,16},{1,5},{2,18},{3,7},{4,20},{5,9},{6,22},{7,11},{8,24},{9,13}... | collective-permute-start | bytes 2359304 | tf_op jit(solution)/shard_map/ppermute | solution.py:41
  92.8 13.2 %collective-permute-start.19 = (bf16[1536,256]{1,0:T(8,128)(2,1)S(1)}, bf16[1536,256]{1,0:T(8,128)(2,1)S(1)}, u32[]{:S(2)}, u32[]{:S(2)}) collective-permute-start(bf16[1536,256]{1,0:T(8,128)(2,1)S(1)} %get-tuple-element.46), channel_id=1, source_target_pairs={{0,48},{1,13},{2,50},{3,15},{4,52},{5,1},{6,54},{7,3},{8,56},{9,5}... | collective-permute-start | bytes 2359304 | tf_op jit(solution)/shard_map/ppermute | solution.py:41
  106.4 32.4 %collective-permute-start.20 = (bf16[1152,512]{1,0:T(8,128)(2,1)S(1)}, bf16[1152,512]{1,0:T(8,128)(2,1)S(1)}, u32[]{:S(2)}, u32[]{:S(2)}) collective-permute-start(bf16[1152,512]{1,0:T(8,128)(2,1)S(1)} %get-tuple-element.47), channel_id=1, source_target_pairs={{0,16},{1,5},{2,18},{3,7},{4,20},{5,9},{6,22},{7,11},{8,24},{9,13}... | collective-permute-start | bytes 3538952 | tf_op jit(solution)/shard_map/ppermute | solution.py:41
  106.5 32.3 %collective-permute-start.21 = (bf16[1152,512]{1,0:T(8,128)(2,1)S(1)}, bf16[1152,512]{1,0:T(8,128)(2,1)S(1)}, u32[]{:S(2)}, u32[]{:S(2)}) collective-permute-start(bf16[1152,512]{1,0:T(8,128)(2,1)S(1)} %get-tuple-element.48), channel_id=1, source_target_pairs={{0,48},{1,13},{2,50},{3,15},{4,52},{5,1},{6,54},{7,3},{8,56},{9,5}... | collective-permute-start | bytes 3538952 | tf_op jit(solution)/shard_map/ppermute | solution.py:41
  109.8 18.3 %collective-permute-start.22 = (bf16[384,512]{1,0:T(8,128)(2,1)S(1)}, bf16[384,512]{1,0:T(8,128)(2,1)S(1)}, u32[]{:S(2)}, u32[]{:S(2)}) collective-permute-start(bf16[384,512]{1,0:T(8,128)(2,1)S(1)} %get-tuple-element.50), channel_id=1, source_target_pairs={{0,16},{1,5},{2,18},{3,7},{4,20},{5,9},{6,22},{7,11},{8,24},{9,13}... | collective-permute-start | bytes 1179656 | tf_op jit(solution)/shard_map/ppermute | solution.py:41
  109.8 18.3 %collective-permute-start.23 = (bf16[384,512]{1,0:T(8,128)(2,1)S(1)}, bf16[384,512]{1,0:T(8,128)(2,1)S(1)}, u32[]{:S(2)}, u32[]{:S(2)}) collective-permute-start(bf16[384,512]{1,0:T(8,128)(2,1)S(1)} %get-tuple-element.51), channel_id=1, source_target_pairs={{0,48},{1,13},{2,50},{3,15},{4,52},{5,1},{6,54},{7,3},{8,56},{9,5}... | collective-permute-start | bytes 1179656 | tf_op jit(solution)/shard_map/ppermute | solution.py:41
  128.2 10.6 %collective-permute-start.24 = (bf16[384,512]{1,0:T(8,128)(2,1)S(1)}, bf16[384,512]{1,0:T(8,128)(2,1)S(1)}, u32[]{:S(2)}, u32[]{:S(2)}) collective-permute-start(bf16[384,512]{1,0:T(8,128)(2,1)S(1)} %middle_far.1), channel_id=1, source_target_pairs={{0,4},{1,17},{2,6},{3,19},{4,8},{5,21},{6,10},{7,23},{8,12},{9,25}... | collective-permute-start | bytes 1179656 | tf_op jit(solution)/shard_map/ppermute | solution.py:41
  139.3 28.6 %copy-start.12 = (bf16[128,384]{1,0:T(8,128)(2,1)S(1)}, bf16[128,384]{1,0:T(8,128)(2,1)}, u32[]{:S(2)}) copy-start(bf16[128,384]{1,0:T(8,128)(2,1)} %grads.3) | copy-start | bytes 294916
  139.3 28.6 %copy-start.13 = (bf16[256,128]{1,0:T(8,128)(2,1)S(1)}, bf16[256,128]{1,0:T(8,128)(2,1)}, u32[]{:S(2)}) copy-start(bf16[256,128]{1,0:T(8,128)(2,1)} %get-tuple-element.31.sel) | copy-start | bytes 196612
  139.3 9.3 %collective-permute-start.25 = (bf16[384,512]{1,0:T(8,128)(2,1)S(1)}, bf16[384,512]{1,0:T(8,128)(2,1)S(1)}, u32[]{:S(2)}, u32[]{:S(2)}) collective-permute-start(bf16[384,512]{1,0:T(8,128)(2,1)S(1)} %get-tuple-element.53), channel_id=1, source_target_pairs={{0,4},{1,17},{2,6},{3,19},{4,8},{5,21},{6,10},{7,23},{8,12},{9,25}... | collective-permute-start | bytes 1179656 | tf_op jit(solution)/shard_map/ppermute | solution.py:41
  139.6 9.0 %collective-permute-start.26 = (bf16[384,512]{1,0:T(8,128)(2,1)S(1)}, bf16[384,512]{1,0:T(8,128)(2,1)S(1)}, u32[]{:S(2)}, u32[]{:S(2)}) collective-permute-start(bf16[384,512]{1,0:T(8,128)(2,1)S(1)} %get-tuple-element.54), channel_id=1, source_target_pairs={{0,12},{1,49},{2,14},{3,51},{4,0},{5,53},{6,2},{7,55},{8,4},{9,57}... | collective-permute-start | bytes 1179656 | tf_op jit(solution)/shard_map/ppermute | solution.py:41
  148.8 30.3 %copy-start.5 = (bf16[1536,384]{1,0:T(8,128)(2,1)S(1)}, bf16[1536,384]{1,0:T(8,128)(2,1)}, u32[]{:S(2)}) copy-start(bf16[1536,384]{1,0:T(8,128)(2,1)} %weights.1) | copy-start | bytes 3538948
  148.8 7.6 %collective-permute-start.27 = (bf16[128,384]{1,0:T(8,128)(2,1)S(1)}, bf16[128,384]{1,0:T(8,128)(2,1)S(1)}, u32[]{:S(2)}, u32[]{:S(2)}) collective-permute-start(bf16[128,384]{1,0:T(8,128)(2,1)S(1)} %get-tuple-element.55), channel_id=1, source_target_pairs={{0,194},{1,65},{2,192},{3,67},{64,0},{65,129},{66,2},{67,131},{128... | collective-permute-start | bytes 294920 | tf_op jit(solution)/shard_map/ppermute | solution.py:51
  152.2 6.4 %collective-permute-start.28 = (bf16[128,384]{1,0:T(8,128)(2,1)S(1)}, bf16[128,384]{1,0:T(8,128)(2,1)S(1)}, u32[]{:S(2)}, u32[]{:S(2)}) collective-permute-start(bf16[128,384]{1,0:T(8,128)(2,1)S(1)} %get-tuple-element.56), channel_id=1, source_target_pairs={{0,130},{1,129},{2,128},{3,131},{64,194},{65,193},{66,192},{67,195... | collective-permute-start | bytes 294920 | tf_op jit(solution)/shard_map/ppermute | solution.py:51
  152.8 6.8 %collective-permute-start.29 = (bf16[128,384]{1,0:T(8,128)(2,1)S(1)}, bf16[128,384]{1,0:T(8,128)(2,1)S(1)}, u32[]{:S(2)}, u32[]{:S(2)}) collective-permute-start(bf16[128,384]{1,0:T(8,128)(2,1)S(1)} %get-tuple-element.57), channel_id=1, source_target_pairs={{0,66},{1,193},{2,64},{3,195},{64,130},{65,3},{66,128},{67,1},{128... | collective-permute-start | bytes 294920 | tf_op jit(solution)/shard_map/ppermute | solution.py:51
  159.7 8.2 %collective-permute-start.30 = (bf16[192,384]{1,0:T(8,128)(2,1)S(1)}, bf16[192,384]{1,0:T(8,128)(2,1)S(1)}, u32[]{:S(2)}, u32[]{:S(2)}) collective-permute-start(bf16[192,384]{1,0:T(8,128)(2,1)S(1)} %pad_maximum_fusion), channel_id=1, source_target_pairs={{0,1},{1,0},{2,3},{3,2},{4,5},{5,4},{6,7},{7,6},{8,9},{9,8},{10,11... | collective-permute-start | bytes 442376 | tf_op jit(solution)/shard_map/ppermute | solution.py:55
  159.8 8.1 %collective-permute-start.31 = (bf16[64,384]{1,0:T(8,128)(2,1)S(1)}, bf16[64,384]{1,0:T(8,128)(2,1)S(1)}, u32[]{:S(2)}, u32[]{:S(2)}) collective-permute-start(bf16[64,384]{1,0:T(8,128)(2,1)S(1)} %get-tuple-element.59), channel_id=1, source_target_pairs={{0,2},{1,3},{2,0},{3,1},{64,66},{65,67},{66,64},{67,65},{128,130},... | collective-permute-start | bytes 147464 | tf_op jit(solution)/shard_map/ppermute | solution.py:51

commit v2 on v1

--- a/solution.py
+++ b/solution.py
@@ -55,8 +55,8 @@
     return lax.ppermute(value, "tp", [(t, t ^ 1) for t in range(4)])
 
 
-def dispatch_kernel(pos, ids, gates, grads, near, far, sel_out):
-    expert = (pos[0] + pos[1] * lax.broadcasted_iota(I32, (8, 128), 0)) & 3
+def dispatch_kernel(table, ids, gates, grads, near, far1, far2, far3, far, sel_out):
+    expert = (table[32] + table[33] * lax.broadcasted_iota(I32, (8, 128), 0)) & 3
     hit0 = ids[0:1, :] == expert
     hit1 = ids[1:2, :] == expert
     zero = jnp.zeros((8, 128), F32)
@@ -76,17 +76,18 @@
             near[...] = rows
         else:
             far[64 * (s - 1) : 64 * s, :] = rows
+            (far1, far2, far3)[s - 1][...] = rows
         sel_out[64 * s : 64 * (s + 1), :] = sel_bf
 
 
-def dispatch(pos, ids, gates, grads):
+def dispatch(table, ids, gates, grads):
     return pl.pallas_call(
         dispatch_kernel,
         in_specs=[SM, VM, VM, VM],
-        out_specs=[VM] * 3,
-        out_shape=[shape((64, 384)), shape((192, 384)), shape((256, 128))],
+        out_specs=[VM] * 6,
+        out_shape=[shape((64, 384))] * 4 + [shape((192, 384)), shape((256, 128))],
         name="dispatch",
-    )(pos, ids, gates, grads)
+    )(table, ids, gates, grads)
 
 
 def combine_kernel(sel, grads, from1, from2, from3, other, own, across, out):
@@ -395,7 +396,7 @@
     z = 4 * (tp // 2) + expert
     direction = 1 - 2 * core
 
-    i = jnp.arange(32, dtype=I32)
+    i = jnp.arange(34, dtype=I32)
     d, j, q = i // 4, i % 4, i % 8
     feature = 4 * ((y + jnp.where(core == 0, d, j)) % 4) + (x + jnp.where(core == 0, j, d)) % 4
     holder = jnp.where(i < 24, core, 1 - core)
@@ -403,15 +404,15 @@
     place = (z - step + 16) % 8
     source_core = jnp.where((q < 6) & (q % 2 == 1), 1 - holder, holder)
     table = jnp.where(i < 16, feature, 4 * (place % 4) + 2 * (place // 4) + source_core)
-    pos = jnp.where(jnp.arange(2) == 0, expert, direction)
-
-    near, far, sel = dispatch(pos, expert_ids.T, gate_weights.T, d_out)
+    table = jnp.where(i == 32, expert, jnp.where(i == 33, direction, table))
+
+    near, *mine, far, sel = dispatch(table, expert_ids.T, gate_weights.T, d_out)
     other = swap_core(far)
     across = shift_z(near, 4)
-    received = [
-        shift_z(jnp.concatenate([far[64 * k - 64 : 64 * k], other[192 - 64 * k : 256 - 64 * k]]), k)
-        for k in (1, 2, 3)
-    ]
+    received = []
+    for k in (1, 2, 3):
+        rows = jnp.concatenate([mine[k - 1], other[192 - 64 * k : 256 - 64 * k]])
+        received.append(shift_z(rows, k))
 
     down_own, gate_own, up_own = w_down[0], w_gate[0], w_up[0]
     down_other = swap_core(down_own)
@@ -463,7 +464,10 @@
     *back, near, across = last(own, from_behind, from_ahead)
 
     across = shift_z(across, 4)
-    back = [shift_z(rows, -k) for k, rows in zip((1, 2, 3), back)]
+    returned = []
+    for k, rows in zip((1, 2, 3), back):
+        returned.append(shift_z(rows, -k))
+    back = returned
     other = swap_core(jnp.concatenate([rows[64:128] for rows in back], axis=0))
     d_hidden = combine(sel, d_out, *back, other, near, across)
 

time: 218 us -> 217 us (level)
  waiting for transfers between devices: 81 us -> 90.6 us
  Pallas kernels: 29.9 us -> 23.8 us
  local copies, waits for them, and re-layouts: 7.48 us -> 2.04 us
  other arithmetic: 1.48 us -> 3.84 us
    ppermute x18, waiting for transfers between devices: 65 us -> 71.1 us  [shift_plane(): return lax.ppermute(value, ('etp', 'tp'), pairs)]
    unnamed x30 -> x20, local copies, waits for them, and re-layouts: 6.59 us -> 2.01 us
    pallas_call x3, Pallas kernels: 15.9 us -> 11.5 us  [part(): pl.pallas_call(functools.partial(part_kernel, groups, per), grid_spec=plt...]
    ppermute x8, waiting for transfers between devices: 15.8 us -> 18.4 us  [shift_z(): return lax.ppermute(value, ('expert', 'tp'), pairs)]
    concatenate x3, other arithmetic: 0.03 us -> 2.43 us  [body(): rows = jnp.concatenate([mine[k - 1], other[192 - 64 * k:256 - 64 * k]])]
  transfers between devices with their start and end apart: 32 -> 32, of which waited for: 16 -> 17; matrix products, arithmetic and copies ran while one was open for 0% -> 1% of each run, Pallas kernels for 9% -> 7%
where the time goes in v2:
time: 217 us; the launch traced here: 213 us
  waiting for transfers between devices  90.6 us (42%)
  starting transfers between devices  49.5 us (23%)
  blocking collectives  42.7 us (20%)
  Pallas kernels  23.8 us (11%)
  other arithmetic  3.84 us (2%)
    ppermute x18, waiting for transfers between devices, shift_plane(): return lax.ppermute(value, ('etp', 'tp'), pairs)  71.1 us
    all_to_all x1, blocking collectives, body(): lax.all_to_all(head_partial.reshape(16, 32, 1536), 'etp', 0, 0, tiled=True)  32.4 us
    ppermute x18, starting transfers between devices, shift_plane(): return lax.ppermute(value, ('etp', 'tp'), pairs)  28 us
    ppermute x8, starting transfers between devices, shift_z(): return lax.ppermute(value, ('expert', 'tp'), pairs)  20.4 us
    ppermute x8, waiting for transfers between devices, shift_z(): return lax.ppermute(value, ('expert', 'tp'), pairs)  18.4 us
    pallas_call x3, Pallas kernels, part(): pl.pallas_call(functools.partial(part_kernel, groups, per), grid_spec=plt...  11.5 us
    all_gather x1, blocking collectives, body(): lax.all_gather(d_hidden, 'tp', axis=0, tiled=True)  10.3 us
  transfers between devices with their start and end apart: 32, of which 17 were waited for; matrix products, arithmetic and copies ran while one was open for 1% of the time, Pallas kernels for 7%

profile of v2, /device:TPU:2, one launch (start us, length us, event | category | flops | bytes accessed | tf_op | source)
XLA Modules:
  0.0 213.4 jit_solution(4992530340103065575)
XLA Ops:
  0.7 0.5 compare_select_fusion.10.table
  1.2 1.9 dispatch.1
  3.2 0.5 collective-permute-start.16
  3.7 1.1 collective-permute-done.2
  4.8 0.8 pad_maximum_fusion.1
  5.6 2.0 collective-permute-start.3
  7.6 0.8 pad_maximum_fusion.2
  8.4 3.3 %collective-permute-start.4 = (bf16[128,384]{1,0:T(8,128)(2,1)S(1)}, bf16[128,384]{1,0:T(8,128)(2,1)S(1)}, u32[]{:S(2)}, u32[]{:S(2)}) collective-permute-start(bf16[128,384]{1,0:T(8,128)(2,1)S(1)} %pad_maximum_fusion.2), channel_id=1, source_target_pairs={{0,128},{1,131},{2,130},{3,129},{64,192},{65,195},{66,194},{67,193... | collective-permute-start | bytes 294920 | tf_op jit(solution)/shard_map/ppermute | solution.py:51
  11.7 0.8 pad_maximum_fusion.3
  12.5 4.1 %collective-permute-start.5 = (bf16[128,384]{1,0:T(8,128)(2,1)S(1)}, bf16[128,384]{1,0:T(8,128)(2,1)S(1)}, u32[]{:S(2)}, u32[]{:S(2)}) collective-permute-start(bf16[128,384]{1,0:T(8,128)(2,1)S(1)} %pad_maximum_fusion.3), channel_id=1, source_target_pairs={{0,192},{1,67},{2,194},{3,65},{64,2},{65,131},{66,0},{67,129},{128... | collective-permute-start | bytes 294920 | tf_op jit(solution)/shard_map/ppermute | solution.py:51
  16.7 0.6 collective-permute-start.6
  17.2 7.7 %collective-permute-done.6.refs_4_ = bf16[64,384]{1,0:T(8,128)(2,1)S(1)} collective-permute-done((bf16[64,384]{1,0:T(8,128)(2,1)}, bf16[64,384]{1,0:T(8,128)(2,1)S(1)}, u32[]{:S(2)}, u32[]{:S(2)}) %collective-permute-start.6) | collective-permute-done | bytes 49184 | tf_op jit(solution)/shard_map/ppermute | solution.py:51
  24.9 0.8 copy-done.8
  25.8 0.6 collective-permute-start.7
  26.4 0.5 collective-permute-start
  26.9 6.7 %collective-permute-done.7.refs_1_ = bf16[512,384]{1,0:T(8,128)(2,1)S(1)} collective-permute-done((bf16[512,384]{1,0:T(8,128)(2,1)S(1)}, bf16[512,384]{1,0:T(8,128)(2,1)S(1)}, u32[]{:S(2)}, u32[]{:S(2)}) %collective-permute-start.7) | collective-permute-done | bytes 393248 | tf_op jit(solution)/shard_map/ppermute | solution.py:41
  33.6 0.8 collective-permute-start.10
  34.4 1.2 collective-permute-start.8
  35.6 5.8 %collective-permute-done.10.refs_1_ = bf16[512,384]{1,0:T(8,128)(2,1)S(1)} collective-permute-done((bf16[512,384]{1,0:T(8,128)(2,1)S(1)}, bf16[512,384]{1,0:T(8,128)(2,1)S(1)}, u32[]{:S(2)}, u32[]{:S(2)}) %collective-permute-start.10) | collective-permute-done | bytes 393248 | tf_op jit(solution)/shard_map/ppermute | solution.py:41
  41.4 3.0 %collective-permute-start.11 = (bf16[512,384]{1,0:T(8,128)(2,1)S(1)}, bf16[512,384]{1,0:T(8,128)(2,1)S(1)}, u32[]{:S(2)}, u32[]{:S(2)}) collective-permute-start(bf16[512,384]{1,0:T(8,128)(2,1)S(1)} %collective-permute-done.10.refs_1_), channel_id=1, source_target_pairs={{0,48},{1,13},{2,50},{3,15},{4,52},{5,1},{6,54},{7,3},{8,56},{9,5}... | collective-permute-start | bytes 1179656 | tf_op jit(solution)/shard_map/ppermute | solution.py:41
  44.4 2.0 collective-permute-start.13
  46.4 1.9 factors.1
  48.4 1.3 collective-permute-done.11.far_a.refs_3_
  49.7 1.8 collective-permute-start.12
  51.5 1.9 collective-permute-done.13.far_b.refs_5_
  53.4 1.3 collective-permute-start.9
  54.7 12.9 %collective-permute-done.12.near_b.refs_4_ = bf16[512,1152]{1,0:T(8,128)(2,1)S(1)} collective-permute-done((bf16[512,1152]{1,0:T(8,128)(2,1)S(1)}, bf16[512,1152]{1,0:T(8,128)(2,1)S(1)}, u32[]{:S(2)}, u32[]{:S(2)}) %collective-permute-start.12) | collective-permute-done | bytes 1179680 | tf_op jit(solution)/shard_map/ppermute | solution.py:41
  67.6 2.0 collective-permute-done.9.near_a.refs_2_
  69.7 2.7 %collective-permute-start.14 = (bf16[256,1536]{1,0:T(8,128)(2,1)S(1)}, bf16[256,1536]{1,0:T(8,128)(2,1)S(1)}, u32[]{:S(2)}, u32[]{:S(2)}) collective-permute-start(bf16[256,1536]{1,0:T(8,128)(2,1)S(1)} %get-tuple-element.42), channel_id=1, source_target_pairs={{0,48},{1,13},{2,50},{3,15},{4,52},{5,1},{6,54},{7,3},{8,56},{9,5}... | collective-permute-start | bytes 2359304 | tf_op jit(solution)/shard_map/ppermute | solution.py:41
  72.5 3.2 %act_first.1.refs_10_ = f32[512,512]{1,0:T(8,128)S(1)} custom-call(s32[34]{0:T(128)S(1)} %copy-done.9, bf16[512,1152]{1,0:T(8,128)(2,1)S(1)} %beside.1.refs_0_, bf16[512,384]{1,0:T(8,128)(2,1)S(1)} %collective-permute-done.10.refs_1_, bf16[512,1152]{1,0:T(8,128)(2,1)S(1)} %collective-permute-done.9.near_a.refs_2_, ...), custom_call_target="tpu_custom_call" | custom-call | tf_op jit(solution)/shard_map/act_first/pallas_call | solution.py:194
  75.7 6.3 %collective-permute-done.14.refs_0_ = bf16[256,1536]{1,0:T(8,128)(2,1)S(1)} collective-permute-done((bf16[256,1536]{1,0:T(8,128)(2,1)S(1)}, bf16[256,1536]{1,0:T(8,128)(2,1)S(1)}, u32[]{:S(2)}, u32[]{:S(2)}) %collective-permute-start.14) | collective-permute-done | bytes 786464 | tf_op jit(solution)/shard_map/ppermute | solution.py:41
  82.0 3.7 %collective-permute-done.15.refs_1_ = bf16[256,1536]{1,0:T(8,128)(2,1)S(1)} collective-permute-done((bf16[256,1536]{1,0:T(8,128)(2,1)S(1)}, bf16[256,1536]{1,0:T(8,128)(2,1)S(1)}, u32[]{:S(2)}, u32[]{:S(2)}) %collective-permute-start.15) | collective-permute-done | bytes 786464 | tf_op jit(solution)/shard_map/ppermute | solution.py:41
  85.7 1.6 act_last.1.refs_4_.refs_8_
  87.3 0.2 copy-done.1
  87.5 1.0 copy-done.2
  88.5 3.0 %shard_map.106 = (bf16[1536,256]{1,0:T(8,128)(2,1)S(1)}, bf16[1536,256]{1,0:T(8,128)(2,1)S(1)}) custom-call(s32[34]{0:T(128)S(1)} %copy-done.9, bf16[6144,256]{1,0:T(8,128)(2,1)S(1)} %bitcast.15, bf16[6144,256]{1,0:T(8,128)(2,1)S(1)} %bitcast.16, bf16[6144,256]{1,0:T(8,128)(2,1)S(1)} %collective-permute-done.refs_1_.refs_2_.refs_3_, ...), custom_call_target="tpu_custom_call" | custom-call | tf_op jit(solution)/shard_map/pallas_call | solution.py:275
  91.6 3.2 %collective-permute-start.19 = (bf16[1536,256]{1,0:T(8,128)(2,1)S(1)}, bf16[1536,256]{1,0:T(8,128)(2,1)S(1)}, u32[]{:S(2)}, u32[]{:S(2)}) collective-permute-start(bf16[1536,256]{1,0:T(8,128)(2,1)S(1)} %get-tuple-element.52), channel_id=1, source_target_pairs={{0,48},{1,13},{2,50},{3,15},{4,52},{5,1},{6,54},{7,3},{8,56},{9,5}... | collective-permute-start | bytes 2359304 | tf_op jit(solution)/shard_map/ppermute | solution.py:41
  94.8 5.5 %shard_map.105 = (bf16[1152,512]{1,0:T(8,128)(2,1)S(1)}, bf16[384,512]{1,0:T(8,128)(2,1)S(1)}, bf16[1152,512]{1,0:T(8,128)(2,1)S(1)}, bf16[384,512]{1,0:T(8,128)(2,1)S(1)}) custom-call(s32[34]{0:T(128)S(1)} %copy-done.9, bf16[6144,256]{1,0:T(8,128)(2,1)S(1)} %bitcast.17, bf16[6144,256]{1,0:T(8,128)(2,1)S(1)} %bitcast.18, ...), custom_call_target="tpu_custom_call" | custom-call | tf_op jit(solution)/shard_map/pallas_call | solution.py:275
  100.3 4.5 %collective-permute-done.18.got_a = bf16[1536,256]{1,0:T(8,128)(2,1)S(1)} collective-permute-done((bf16[1536,256]{1,0:T(8,128)(2,1)S(1)}, bf16[1536,256]{1,0:T(8,128)(2,1)S(1)}, u32[]{:S(2)}, u32[]{:S(2)}) %collective-permute-start.18) | collective-permute-done | bytes 786464 | tf_op jit(solution)/shard_map/ppermute | solution.py:41
  104.8 0.4 add_pairs.1
  105.3 3.3 %collective-permute-start.21 = (bf16[1152,512]{1,0:T(8,128)(2,1)S(1)}, bf16[1152,512]{1,0:T(8,128)(2,1)S(1)}, u32[]{:S(2)}, u32[]{:S(2)}) collective-permute-start(bf16[1152,512]{1,0:T(8,128)(2,1)S(1)} %get-tuple-element.54), channel_id=1, source_target_pairs={{0,48},{1,13},{2,50},{3,15},{4,52},{5,1},{6,54},{7,3},{8,56},{9,5}... | collective-permute-start | bytes 3538952 | tf_op jit(solution)/shard_map/ppermute | solution.py:41
  108.6 3.2 %collective-permute-start.23 = (bf16[384,512]{1,0:T(8,128)(2,1)S(1)}, bf16[384,512]{1,0:T(8,128)(2,1)S(1)}, u32[]{:S(2)}, u32[]{:S(2)}) collective-permute-start(bf16[384,512]{1,0:T(8,128)(2,1)S(1)} %get-tuple-element.57), channel_id=1, source_target_pairs={{0,48},{1,13},{2,50},{3,15},{4,52},{5,1},{6,54},{7,3},{8,56},{9,5}... | collective-permute-start | bytes 1179656 | tf_op jit(solution)/shard_map/ppermute | solution.py:41
  111.9 3.0 %shard_map.104 = (bf16[1152,512]{1,0:T(8,128)(2,1)S(1)}, bf16[384,512]{1,0:T(8,128)(2,1)S(1)}) custom-call(s32[34]{0:T(128)S(1)} %copy-done.9, bf16[6144,256]{1,0:T(8,128)(2,1)S(1)} %bitcast.19, bf16[6144,256]{1,0:T(8,128)(2,1)S(1)} %collective-permute-done.refs_1_.refs_2_.refs_3_, bf16[6144,256]{1,0:T(8,128)(2,1)S(1)} %bitcast.25, ...), custom_call_target="tpu_custom_call" | custom-call | tf_op jit(solution)/shard_map/pallas_call | solution.py:275
  114.9 12.0 %collective-permute-done.22.got1 = bf16[384,512]{1,0:T(8,128)(2,1)S(1)} collective-permute-done((bf16[384,512]{1,0:T(8,128)(2,1)S(1)}, bf16[384,512]{1,0:T(8,128)(2,1)S(1)}, u32[]{:S(2)}, u32[]{:S(2)}) %collective-permute-start.22) | collective-permute-done | bytes 393248 | tf_op jit(solution)/shard_map/ppermute | solution.py:41
  126.9 0.1 middle_far.1
  127.1 0.9 collective-permute-start.24
  128.0 8.4 %collective-permute-done.24.far = bf16[384,512]{1,0:T(8,128)(2,1)S(1)} collective-permute-done((bf16[384,512]{1,0:T(8,128)(2,1)S(1)}, bf16[384,512]{1,0:T(8,128)(2,1)S(1)}, u32[]{:S(2)}, u32[]{:S(2)}) %collective-permute-start.24) | collective-permute-done | bytes 393248 | tf_op jit(solution)/shard_map/ppermute | solution.py:41
  136.4 0.5 middle_near.1
  136.9 1.1 collective-permute-start.25
  138.0 2.5 %collective-permute-start.26 = (bf16[384,512]{1,0:T(8,128)(2,1)S(1)}, bf16[384,512]{1,0:T(8,128)(2,1)S(1)}, u32[]{:S(2)}, u32[]{:S(2)}) collective-permute-start(bf16[384,512]{1,0:T(8,128)(2,1)S(1)} %get-tuple-element.60), channel_id=1, source_target_pairs={{0,12},{1,49},{2,14},{3,51},{4,0},{5,53},{6,2},{7,55},{8,4},{9,57}... | collective-permute-start | bytes 1179656 | tf_op jit(solution)/shard_map/ppermute | solution.py:41
  140.6 5.7 %collective-permute-done.25.got1 = bf16[384,512]{1,0:T(8,128)(2,1)S(1)} collective-permute-done((bf16[384,512]{1,0:T(8,128)(2,1)S(1)}, bf16[384,512]{1,0:T(8,128)(2,1)S(1)}, u32[]{:S(2)}, u32[]{:S(2)}) %collective-permute-start.25) | collective-permute-done | bytes 393248 | tf_op jit(solution)/shard_map/ppermute | solution.py:41
  146.3 0.2 last.1
  146.5 4.4 %collective-permute-start.27 = (bf16[128,384]{1,0:T(8,128)(2,1)S(1)}, bf16[128,384]{1,0:T(8,128)(2,1)S(1)}, u32[]{:S(2)}, u32[]{:S(2)}) collective-permute-start(bf16[128,384]{1,0:T(8,128)(2,1)S(1)} %get-tuple-element.61), channel_id=1, source_target_pairs={{0,194},{1,65},{2,192},{3,67},{64,0},{65,129},{66,2},{67,131},{128... | collective-permute-start | bytes 294920 | tf_op jit(solution)/shard_map/ppermute | solution.py:51
  150.9 1.9 collective-permute-start.28
  152.8 0.4 collective-permute-start.29
  153.3 3.2 %collective-permute-done.28.from2 = bf16[128,384]{1,0:T(8,128)(2,1)S(1)} collective-permute-done((bf16[128,384]{1,0:T(8,128)(2,1)S(1)}, bf16[128,384]{1,0:T(8,128)(2,1)S(1)}, u32[]{:S(2)}, u32[]{:S(2)}) %collective-permute-start.28) | collective-permute-done | bytes 98336 | tf_op jit(solution)/shard_map/ppermute | solution.py:51
  156.4 3.0 %collective-permute-done.29.from3 = bf16[128,384]{1,0:T(8,128)(2,1)S(1)} collective-permute-done((bf16[128,384]{1,0:T(8,128)(2,1)S(1)}, bf16[128,384]{1,0:T(8,128)(2,1)S(1)}, u32[]{:S(2)}, u32[]{:S(2)}) %collective-permute-start.29) | collective-permute-done | bytes 98336 | tf_op jit(solution)/shard_map/ppermute | solution.py:51
  159.6 3.6 %collective-permute-start.31 = (bf16[64,384]{1,0:T(8,128)(2,1)S(1)}, bf16[64,384]{1,0:T(8,128)(2,1)S(1)}, u32[]{:S(2)}, u32[]{:S(2)}) collective-permute-start(bf16[64,384]{1,0:T(8,128)(2,1)S(1)} %get-tuple-element.65), channel_id=1, source_target_pairs={{0,2},{1,3},{2,0},{3,1},{64,66},{65,67},{66,64},{67,65},{128,130},... | collective-permute-start | bytes 147464 | tf_op jit(solution)/shard_map/ppermute | solution.py:51
  163.2 4.6 %collective-permute-done.31.across = bf16[64,384]{1,0:T(8,128)(2,1)S(1)} collective-permute-done((bf16[64,384]{1,0:T(8,128)(2,1)S(1)}, bf16[64,384]{1,0:T(8,128)(2,1)S(1)}, u32[]{:S(2)}, u32[]{:S(2)}) %collective-permute-start.31) | collective-permute-done | bytes 49184 | tf_op jit(solution)/shard_map/ppermute | solution.py:51
  167.7 0.9 combine.1
  168.6 10.3 %all_gather.3.tokens = bf16[512,384]{1,0:T(8,128)(2,1)S(1)} all-gather(bf16[128,384]{1,0:T(8,128)(2,1)} %combine.1), channel_id=1, replica_groups=mesh['expert'=4,'etp'=16,'tp'=4] {'tp'}, dimensions={0}, use_global_device_ids=true | all-gather | bytes 491520 | tf_op jit(solution)/shard_map/all_gather | solution.py:474
  179.0 1.2 heads.1
  180.2 32.4 %all_to_all.5 = bf16[16,32,1536]{2,1,0:T(8,128)(2,1)S(1)} all-to-all(bf16[16,32,1536]{2,1,0:T(8,128)(2,1)S(1)} %bitcast.26), channel_id=1, replica_groups=mesh['expert'=4,'etp'=16,'tp'=4] {'etp'}, dimensions={0} | all-to-all | bytes 3145728 | tf_op jit(solution)/shard_map/all_to_all | solution.py:475
  212.6 0.9 reduce_sum.12
  (48 shorter events, 0.7 us)
Async XLA Ops:
  0.6 45.8 %copy-start.4 = (bf16[1,1024,256]{2,1,0:T(8,128)(2,1)S(1)}, bf16[1,1024,256]{2,1,0:T(8,128)(2,1)}, u32[]{:S(2)}) copy-start(bf16[1,1024,256]{2,1,0:T(8,128)(2,1)} %param.12) | copy-start | bytes 1572868
  0.6 45.7 %copy-start.5 = (bf16[1,1024,256]{2,1,0:T(8,128)(2,1)S(1)}, bf16[1,1024,256]{2,1,0:T(8,128)(2,1)}, u32[]{:S(2)}) copy-start(bf16[1,1024,256]{2,1,0:T(8,128)(2,1)} %param.13) | copy-start | bytes 1572868
  1.2 45.2 %copy-start.9 = (s32[34]{0:T(128)S(1)}, s32[34]{0:T(128)}, u32[]{:S(2)}) copy-start(s32[34]{0:T(128)} %compare_select_fusion.10.table) | copy-start | bytes 412
  3.2 1.6 collective-permute-start.2
  3.2 69.3 %collective-permute-start.16 = (bf16[256,6144]{1,0:T(8,128)(2,1)}, bf16[256,6144]{1,0:T(8,128)(2,1)S(1)}, u32[]{:S(2)}, u32[]{:S(2)}) collective-permute-start(bf16[256,6144]{1,0:T(8,128)(2,1)} %bitcast.8), channel_id=1, source_target_pairs={{0,1},{1,0},{2,3},{3,2},{4,5},{5,4},{6,7},{7,6},{8,9},{9,8},{10,11... | collective-permute-start | bytes 9437192 | tf_op jit(solution)/shard_map/ppermute | solution.py:55
  5.6 19.3 %collective-permute-start.3 = (bf16[128,384]{1,0:T(8,128)(2,1)S(1)}, bf16[128,384]{1,0:T(8,128)(2,1)S(1)}, u32[]{:S(2)}, u32[]{:S(2)}) collective-permute-start(bf16[128,384]{1,0:T(8,128)(2,1)S(1)} %pad_maximum_fusion.1), channel_id=1, source_target_pairs={{0,64},{1,195},{2,66},{3,193},{64,128},{65,1},{66,130},{67,3},{128... | collective-permute-start | bytes 294920 | tf_op jit(solution)/shard_map/ppermute | solution.py:51
  8.4 16.5 %collective-permute-start.4 = (bf16[128,384]{1,0:T(8,128)(2,1)S(1)}, bf16[128,384]{1,0:T(8,128)(2,1)S(1)}, u32[]{:S(2)}, u32[]{:S(2)}) collective-permute-start(bf16[128,384]{1,0:T(8,128)(2,1)S(1)} %pad_maximum_fusion.2), channel_id=1, source_target_pairs={{0,128},{1,131},{2,130},{3,129},{64,192},{65,195},{66,194},{67,193... | collective-permute-start | bytes 294920 | tf_op jit(solution)/shard_map/ppermute | solution.py:51
  12.5 12.4 %collective-permute-start.5 = (bf16[128,384]{1,0:T(8,128)(2,1)S(1)}, bf16[128,384]{1,0:T(8,128)(2,1)S(1)}, u32[]{:S(2)}, u32[]{:S(2)}) collective-permute-start(bf16[128,384]{1,0:T(8,128)(2,1)S(1)} %pad_maximum_fusion.3), channel_id=1, source_target_pairs={{0,192},{1,67},{2,194},{3,65},{64,2},{65,131},{66,0},{67,129},{128... | collective-permute-start | bytes 294920 | tf_op jit(solution)/shard_map/ppermute | solution.py:51
  16.7 8.2 %collective-permute-start.6 = (bf16[64,384]{1,0:T(8,128)(2,1)}, bf16[64,384]{1,0:T(8,128)(2,1)S(1)}, u32[]{:S(2)}, u32[]{:S(2)}) collective-permute-start(bf16[64,384]{1,0:T(8,128)(2,1)} %get-tuple-element.39.refs_3_), channel_id=1, source_target_pairs={{0,2},{1,3},{2,0},{3,1},{64,66},{65,67},{66,64},{67,65},{128,130},... | collective-permute-start | bytes 147464 | tf_op jit(solution)/shard_map/ppermute | solution.py:51
  24.9 0.8 copy-start.8
  25.8 7.9 %collective-permute-start.7 = (bf16[512,384]{1,0:T(8,128)(2,1)S(1)}, bf16[512,384]{1,0:T(8,128)(2,1)S(1)}, u32[]{:S(2)}, u32[]{:S(2)}) collective-permute-start(bf16[512,384]{1,0:T(8,128)(2,1)S(1)} %pack.1.refs_0_), channel_id=1, source_target_pairs={{0,12},{1,49},{2,14},{3,51},{4,0},{5,53},{6,2},{7,55},{8,4},{9,57}... | collective-permute-start | bytes 1179656 | tf_op jit(solution)/shard_map/ppermute | solution.py:41
  26.4 60.9 %collective-permute-start = (bf16[6144,256]{1,0:T(8,128)(2,1)}, bf16[6144,256]{1,0:T(8,128)(2,1)S(1)}, u32[]{:S(2)}, u32[]{:S(2)}) collective-permute-start(bf16[6144,256]{1,0:T(8,128)(2,1)} %bitcast.14), channel_id=1, source_target_pairs={{0,1},{1,0},{2,3},{3,2},{4,5},{5,4},{6,7},{7,6},{8,9},{9,8},{10,11... | collective-permute-start | bytes 9437192 | tf_op jit(solution)/shard_map/ppermute | solution.py:55
  26.9 60.4 %collective-permute-start.1 = (bf16[6144,256]{1,0:T(8,128)(2,1)}, bf16[6144,256]{1,0:T(8,128)(2,1)S(1)}, u32[]{:S(2)}, u32[]{:S(2)}) collective-permute-start(bf16[6144,256]{1,0:T(8,128)(2,1)} %bitcast.20), channel_id=1, source_target_pairs={{0,1},{1,0},{2,3},{3,2},{4,5},{5,4},{6,7},{7,6},{8,9},{9,8},{10,11... | collective-permute-start | bytes 9437192 | tf_op jit(solution)/shard_map/ppermute | solution.py:55
  33.6 7.8 %collective-permute-start.10 = (bf16[512,384]{1,0:T(8,128)(2,1)S(1)}, bf16[512,384]{1,0:T(8,128)(2,1)S(1)}, u32[]{:S(2)}, u32[]{:S(2)}) collective-permute-start(bf16[512,384]{1,0:T(8,128)(2,1)S(1)} %collective-permute-done.7.refs_1_), channel_id=1, source_target_pairs={{0,12},{1,49},{2,14},{3,51},{4,0},{5,53},{6,2},{7,55},{8,4},{9,57}... | collective-permute-start | bytes 1179656 | tf_op jit(solution)/shard_map/ppermute | solution.py:41
  34.4 10.0 %collective-permute-start.8 = (bf16[512,384]{1,0:T(8,128)(2,1)S(1)}, bf16[512,384]{1,0:T(8,128)(2,1)S(1)}, u32[]{:S(2)}, u32[]{:S(2)}) collective-permute-start(bf16[512,384]{1,0:T(8,128)(2,1)S(1)} %pack.1.refs_0_), channel_id=1, source_target_pairs={{0,4},{1,17},{2,6},{3,19},{4,8},{5,21},{6,10},{7,23},{8,12},{9,25}... | collective-permute-start | bytes 1179656 | tf_op jit(solution)/shard_map/ppermute | solution.py:41
  41.4 8.3 %collective-permute-start.11 = (bf16[512,384]{1,0:T(8,128)(2,1)S(1)}, bf16[512,384]{1,0:T(8,128)(2,1)S(1)}, u32[]{:S(2)}, u32[]{:S(2)}) collective-permute-start(bf16[512,384]{1,0:T(8,128)(2,1)S(1)} %collective-permute-done.10.refs_1_), channel_id=1, source_target_pairs={{0,48},{1,13},{2,50},{3,15},{4,52},{5,1},{6,54},{7,3},{8,56},{9,5}... | collective-permute-start | bytes 1179656 | tf_op jit(solution)/shard_map/ppermute | solution.py:41
  44.4 9.0 %collective-permute-start.13 = (bf16[512,384]{1,0:T(8,128)(2,1)S(1)}, bf16[512,384]{1,0:T(8,128)(2,1)S(1)}, u32[]{:S(2)}, u32[]{:S(2)}) collective-permute-start(bf16[512,384]{1,0:T(8,128)(2,1)S(1)} %collective-permute-done.10.refs_1_), channel_id=1, source_target_pairs={{0,16},{1,5},{2,18},{3,7},{4,20},{5,9},{6,22},{7,11},{8,24},{9,13}... | collective-permute-start | bytes 1179656 | tf_op jit(solution)/shard_map/ppermute | solution.py:41
  48.4 24.0 %copy-start = (bf16[1,256,6144]{2,1,0:T(8,128)(2,1)S(1)}, bf16[1,256,6144]{2,1,0:T(8,128)(2,1)}, u32[]{:S(2)}) copy-start(bf16[1,256,6144]{2,1,0:T(8,128)(2,1)} %param.16) | copy-start | bytes 9437188
  49.7 17.9 %collective-permute-start.12 = (bf16[512,1152]{1,0:T(8,128)(2,1)S(1)}, bf16[512,1152]{1,0:T(8,128)(2,1)S(1)}, u32[]{:S(2)}, u32[]{:S(2)}) collective-permute-start(bf16[512,1152]{1,0:T(8,128)(2,1)S(1)} %beside.1.refs_0_), channel_id=1, source_target_pairs={{0,16},{1,5},{2,18},{3,7},{4,20},{5,9},{6,22},{7,11},{8,24},{9,13}... | collective-permute-start | bytes 3538952 | tf_op jit(solution)/shard_map/ppermute | solution.py:41
  53.4 16.2 %collective-permute-start.9 = (bf16[512,1152]{1,0:T(8,128)(2,1)S(1)}, bf16[512,1152]{1,0:T(8,128)(2,1)S(1)}, u32[]{:S(2)}, u32[]{:S(2)}) collective-permute-start(bf16[512,1152]{1,0:T(8,128)(2,1)S(1)} %beside.1.refs_0_), channel_id=1, source_target_pairs={{0,48},{1,13},{2,50},{3,15},{4,52},{5,1},{6,54},{7,3},{8,56},{9,5}... | collective-permute-start | bytes 3538952 | tf_op jit(solution)/shard_map/ppermute | solution.py:41
  67.6 8.1 %collective-permute-start.17 = (f32[512,512]{1,0:T(8,128)S(1)}, f32[512,512]{1,0:T(8,128)S(1)}, u32[]{:S(2)}, u32[]{:S(2)}) collective-permute-start(f32[512,512]{1,0:T(8,128)S(1)} %get-tuple-element.45), channel_id=1, source_target_pairs={{0,1},{1,0},{2,3},{3,2},{4,5},{5,4},{6,7},{7,6},{8,9},{9,8},{10,11... | collective-permute-start | bytes 3145736 | tf_op jit(solution)/shard_map/ppermute | solution.py:55
  69.7 12.2 %collective-permute-start.14 = (bf16[256,1536]{1,0:T(8,128)(2,1)S(1)}, bf16[256,1536]{1,0:T(8,128)(2,1)S(1)}, u32[]{:S(2)}, u32[]{:S(2)}) collective-permute-start(bf16[256,1536]{1,0:T(8,128)(2,1)S(1)} %get-tuple-element.42), channel_id=1, source_target_pairs={{0,48},{1,13},{2,50},{3,15},{4,52},{5,1},{6,54},{7,3},{8,56},{9,5}... | collective-permute-start | bytes 2359304 | tf_op jit(solution)/shard_map/ppermute | solution.py:41
  72.5 13.2 %collective-permute-start.15 = (bf16[256,1536]{1,0:T(8,128)(2,1)S(1)}, bf16[256,1536]{1,0:T(8,128)(2,1)S(1)}, u32[]{:S(2)}, u32[]{:S(2)}) collective-permute-start(bf16[256,1536]{1,0:T(8,128)(2,1)S(1)} %get-tuple-element.43), channel_id=1, source_target_pairs={{0,16},{1,5},{2,18},{3,7},{4,20},{5,9},{6,22},{7,11},{8,24},{9,13}... | collective-permute-start | bytes 2359304 | tf_op jit(solution)/shard_map/ppermute | solution.py:41
  85.7 1.9 copy-start.1
  85.7 2.8 %copy-start.2 = (bf16[1,6144,256]{2,1,0:T(8,128)(2,1)S(1)}, bf16[1,6144,256]{2,1,0:T(8,128)(2,1)}, u32[]{:S(2)}) copy-start(bf16[1,6144,256]{2,1,0:T(8,128)(2,1)} %param.15) | copy-start | bytes 9437188
  91.5 13.3 %collective-permute-start.18 = (bf16[1536,256]{1,0:T(8,128)(2,1)S(1)}, bf16[1536,256]{1,0:T(8,128)(2,1)S(1)}, u32[]{:S(2)}, u32[]{:S(2)}) collective-permute-start(bf16[1536,256]{1,0:T(8,128)(2,1)S(1)} %get-tuple-element.49), channel_id=1, source_target_pairs={{0,16},{1,5},{2,18},{3,7},{4,20},{5,9},{6,22},{7,11},{8,24},{9,13}... | collective-permute-start | bytes 2359304 | tf_op jit(solution)/shard_map/ppermute | solution.py:41
  91.6 13.2 %collective-permute-start.19 = (bf16[1536,256]{1,0:T(8,128)(2,1)S(1)}, bf16[1536,256]{1,0:T(8,128)(2,1)S(1)}, u32[]{:S(2)}, u32[]{:S(2)}) collective-permute-start(bf16[1536,256]{1,0:T(8,128)(2,1)S(1)} %get-tuple-element.52), channel_id=1, source_target_pairs={{0,48},{1,13},{2,50},{3,15},{4,52},{5,1},{6,54},{7,3},{8,56},{9,5}... | collective-permute-start | bytes 2359304 | tf_op jit(solution)/shard_map/ppermute | solution.py:41
  105.2 31.2 %collective-permute-start.20 = (bf16[1152,512]{1,0:T(8,128)(2,1)S(1)}, bf16[1152,512]{1,0:T(8,128)(2,1)S(1)}, u32[]{:S(2)}, u32[]{:S(2)}) collective-permute-start(bf16[1152,512]{1,0:T(8,128)(2,1)S(1)} %get-tuple-element.53), channel_id=1, source_target_pairs={{0,16},{1,5},{2,18},{3,7},{4,20},{5,9},{6,22},{7,11},{8,24},{9,13}... | collective-permute-start | bytes 3538952 | tf_op jit(solution)/shard_map/ppermute | solution.py:41
  105.3 31.1 %collective-permute-start.21 = (bf16[1152,512]{1,0:T(8,128)(2,1)S(1)}, bf16[1152,512]{1,0:T(8,128)(2,1)S(1)}, u32[]{:S(2)}, u32[]{:S(2)}) collective-permute-start(bf16[1152,512]{1,0:T(8,128)(2,1)S(1)} %get-tuple-element.54), channel_id=1, source_target_pairs={{0,48},{1,13},{2,50},{3,15},{4,52},{5,1},{6,54},{7,3},{8,56},{9,5}... | collective-permute-start | bytes 3538952 | tf_op jit(solution)/shard_map/ppermute | solution.py:41
  108.6 18.3 %collective-permute-start.22 = (bf16[384,512]{1,0:T(8,128)(2,1)S(1)}, bf16[384,512]{1,0:T(8,128)(2,1)S(1)}, u32[]{:S(2)}, u32[]{:S(2)}) collective-permute-start(bf16[384,512]{1,0:T(8,128)(2,1)S(1)} %get-tuple-element.56), channel_id=1, source_target_pairs={{0,16},{1,5},{2,18},{3,7},{4,20},{5,9},{6,22},{7,11},{8,24},{9,13}... | collective-permute-start | bytes 1179656 | tf_op jit(solution)/shard_map/ppermute | solution.py:41
  108.6 18.3 %collective-permute-start.23 = (bf16[384,512]{1,0:T(8,128)(2,1)S(1)}, bf16[384,512]{1,0:T(8,128)(2,1)S(1)}, u32[]{:S(2)}, u32[]{:S(2)}) collective-permute-start(bf16[384,512]{1,0:T(8,128)(2,1)S(1)} %get-tuple-element.57), channel_id=1, source_target_pairs={{0,48},{1,13},{2,50},{3,15},{4,52},{5,1},{6,54},{7,3},{8,56},{9,5}... | collective-permute-start | bytes 1179656 | tf_op jit(solution)/shard_map/ppermute | solution.py:41
  127.1 9.3 %collective-permute-start.24 = (bf16[384,512]{1,0:T(8,128)(2,1)S(1)}, bf16[384,512]{1,0:T(8,128)(2,1)S(1)}, u32[]{:S(2)}, u32[]{:S(2)}) collective-permute-start(bf16[384,512]{1,0:T(8,128)(2,1)S(1)} %middle_far.1), channel_id=1, source_target_pairs={{0,4},{1,17},{2,6},{3,19},{4,8},{5,21},{6,10},{7,23},{8,12},{9,25}... | collective-permute-start | bytes 1179656 | tf_op jit(solution)/shard_map/ppermute | solution.py:41
  136.9 30.8 %copy-start.6 = (bf16[128,384]{1,0:T(8,128)(2,1)S(1)}, bf16[128,384]{1,0:T(8,128)(2,1)}, u32[]{:S(2)}) copy-start(bf16[128,384]{1,0:T(8,128)(2,1)} %grads.3) | copy-start | bytes 294916
  136.9 30.8 %copy-start.7 = (bf16[256,128]{1,0:T(8,128)(2,1)S(1)}, bf16[256,128]{1,0:T(8,128)(2,1)}, u32[]{:S(2)}) copy-start(bf16[256,128]{1,0:T(8,128)(2,1)} %get-tuple-element.34.sel) | copy-start | bytes 196612
  136.9 9.3 %collective-permute-start.25 = (bf16[384,512]{1,0:T(8,128)(2,1)S(1)}, bf16[384,512]{1,0:T(8,128)(2,1)S(1)}, u32[]{:S(2)}, u32[]{:S(2)}) collective-permute-start(bf16[384,512]{1,0:T(8,128)(2,1)S(1)} %get-tuple-element.59), channel_id=1, source_target_pairs={{0,4},{1,17},{2,6},{3,19},{4,8},{5,21},{6,10},{7,23},{8,12},{9,25}... | collective-permute-start | bytes 1179656 | tf_op jit(solution)/shard_map/ppermute | solution.py:41
  138.0 8.2 %collective-permute-start.26 = (bf16[384,512]{1,0:T(8,128)(2,1)S(1)}, bf16[384,512]{1,0:T(8,128)(2,1)S(1)}, u32[]{:S(2)}, u32[]{:S(2)}) collective-permute-start(bf16[384,512]{1,0:T(8,128)(2,1)S(1)} %get-tuple-element.60), channel_id=1, source_target_pairs={{0,12},{1,49},{2,14},{3,51},{4,0},{5,53},{6,2},{7,55},{8,4},{9,57}... | collective-permute-start | bytes 1179656 | tf_op jit(solution)/shard_map/ppermute | solution.py:41
  146.4 32.5 %copy-start.3 = (bf16[1536,384]{1,0:T(8,128)(2,1)S(1)}, bf16[1536,384]{1,0:T(8,128)(2,1)}, u32[]{:S(2)}) copy-start(bf16[1536,384]{1,0:T(8,128)(2,1)} %weights.1) | copy-start | bytes 3538948
  146.5 6.8 %collective-permute-start.27 = (bf16[128,384]{1,0:T(8,128)(2,1)S(1)}, bf16[128,384]{1,0:T(8,128)(2,1)S(1)}, u32[]{:S(2)}, u32[]{:S(2)}) collective-permute-start(bf16[128,384]{1,0:T(8,128)(2,1)S(1)} %get-tuple-element.61), channel_id=1, source_target_pairs={{0,194},{1,65},{2,192},{3,67},{64,0},{65,129},{66,2},{67,131},{128... | collective-permute-start | bytes 294920 | tf_op jit(solution)/shard_map/ppermute | solution.py:51
  150.9 5.5 %collective-permute-start.28 = (bf16[128,384]{1,0:T(8,128)(2,1)S(1)}, bf16[128,384]{1,0:T(8,128)(2,1)S(1)}, u32[]{:S(2)}, u32[]{:S(2)}) collective-permute-start(bf16[128,384]{1,0:T(8,128)(2,1)S(1)} %get-tuple-element.62), channel_id=1, source_target_pairs={{0,130},{1,129},{2,128},{3,131},{64,194},{65,193},{66,192},{67,195... | collective-permute-start | bytes 294920 | tf_op jit(solution)/shard_map/ppermute | solution.py:51
  152.8 6.6 %collective-permute-start.29 = (bf16[128,384]{1,0:T(8,128)(2,1)S(1)}, bf16[128,384]{1,0:T(8,128)(2,1)S(1)}, u32[]{:S(2)}, u32[]{:S(2)}) collective-permute-start(bf16[128,384]{1,0:T(8,128)(2,1)S(1)} %get-tuple-element.63), channel_id=1, source_target_pairs={{0,66},{1,193},{2,64},{3,195},{64,130},{65,3},{66,128},{67,1},{128... | collective-permute-start | bytes 294920 | tf_op jit(solution)/shard_map/ppermute | solution.py:51
  159.5 8.2 %collective-permute-start.30 = (bf16[192,384]{1,0:T(8,128)(2,1)S(1)}, bf16[192,384]{1,0:T(8,128)(2,1)S(1)}, u32[]{:S(2)}, u32[]{:S(2)}) collective-permute-start(bf16[192,384]{1,0:T(8,128)(2,1)S(1)} %pad_maximum_fusion), channel_id=1, source_target_pairs={{0,1},{1,0},{2,3},{3,2},{4,5},{5,4},{6,7},{7,6},{8,9},{9,8},{10,11... | collective-permute-start | bytes 442376 | tf_op jit(solution)/shard_map/ppermute | solution.py:55
  159.6 8.1 %collective-permute-start.31 = (bf16[64,384]{1,0:T(8,128)(2,1)S(1)}, bf16[64,384]{1,0:T(8,128)(2,1)S(1)}, u32[]{:S(2)}, u32[]{:S(2)}) collective-permute-start(bf16[64,384]{1,0:T(8,128)(2,1)S(1)} %get-tuple-element.65), channel_id=1, source_target_pairs={{0,2},{1,3},{2,0},{3,1},{64,66},{65,67},{66,64},{67,65},{128,130},... | collective-permute-start | bytes 147464 | tf_op jit(solution)/shard_map/ppermute | solution.py:51

commit v3 on v2

--- a/solution.py
+++ b/solution.py
@@ -55,7 +55,7 @@
     return lax.ppermute(value, "tp", [(t, t ^ 1) for t in range(4)])
 
 
-def dispatch_kernel(table, ids, gates, grads, near, far1, far2, far3, far, sel_out):
+def dispatch_kernel(table, ids, gates, grads, near, far, sel_out):
     expert = (table[32] + table[33] * lax.broadcasted_iota(I32, (8, 128), 0)) & 3
     hit0 = ids[0:1, :] == expert
     hit1 = ids[1:2, :] == expert
@@ -76,7 +76,6 @@
             near[...] = rows
         else:
             far[64 * (s - 1) : 64 * s, :] = rows
-            (far1, far2, far3)[s - 1][...] = rows
         sel_out[64 * s : 64 * (s + 1), :] = sel_bf
 
 
@@ -84,10 +83,26 @@
     return pl.pallas_call(
         dispatch_kernel,
         in_specs=[SM, VM, VM, VM],
-        out_specs=[VM] * 6,
-        out_shape=[shape((64, 384))] * 4 + [shape((192, 384)), shape((256, 128))],
+        out_specs=[VM] * 3,
+        out_shape=[shape((64, 384)), shape((192, 384)), shape((256, 128))],
         name="dispatch",
     )(table, ids, gates, grads)
+
+
+def messages_kernel(far, other, own, out1, out2, out3, near):
+    for k, out in enumerate((out1, out2, out3)):
+        out[0:64, :] = far[64 * k : 64 * (k + 1), :]
+        out[64:128, :] = other[64 * (2 - k) : 64 * (3 - k), :]
+    near[...] = own[...]
+
+
+def messages(*args):
+    return pl.pallas_call(
+        messages_kernel,
+        out_shape=[shape((128, 384))] * 3 + [shape((64, 384))],
+        name="messages",
+        compiler_params=room(4),
+    )(*args)
 
 
 def combine_kernel(sel, grads, from1, from2, from3, other, own, across, out):
@@ -318,26 +333,32 @@
     )(*args)
 
 
-def far_kernel(own, got1, got2, out):
-    out[...] = add(own[...], got1[...], got2[...]).astype(BF)
+def far_kernel(own, got1, got2, top, bottom):
+    total = add(own[...], got1[...], got2[...]).astype(BF)
+    top[...] = total[:, 0:256]
+    bottom[...] = total[:, 256:512]
 
 
 def middle_far(*args):
     return pl.pallas_call(
-        far_kernel, out_shape=shape((384, 512)), name="middle_far", compiler_params=room(6)
-    )(*args)
-
-
-def near_kernel(mine, got1, got2, far, own, ahead, behind):
+        far_kernel, out_shape=[shape((384, 256))] * 2, name="middle_far", compiler_params=room(6)
+    )(*args)
+
+
+def near_kernel(mine, got1, got2, far_top, far_bottom, own, ahead, behind):
     for k, out in enumerate((own, ahead, behind)):
 
         def some_rows(r, carry, k=k, out=out):
             to = pl.ds(pl.multiple_of(r * 128, 128), 128)
             here = pl.ds(pl.multiple_of(384 * k + r * 128, 128), 128)
             total = add(mine[here, :], got1[here, :], got2[here, :])
+            top, bottom = total[:, 0:256], total[:, 256:512]
             if k == 1:
-                total = total + far[to, :].astype(F32)
-            out[to, :] = total.astype(out.dtype)
+                top = top + far_top[to, :].astype(F32)
+            if k == 2:
+                bottom = bottom + far_bottom[to, :].astype(F32)
+            out[to, 0:256] = top.astype(out.dtype)
+            out[to, 256:512] = bottom.astype(out.dtype)
             return carry
 
         lax.fori_loop(0, 3, some_rows, 0)
@@ -406,12 +427,12 @@
     table = jnp.where(i < 16, feature, 4 * (place % 4) + 2 * (place // 4) + source_core)
     table = jnp.where(i == 32, expert, jnp.where(i == 33, direction, table))
 
-    near, *mine, far, sel = dispatch(table, expert_ids.T, gate_weights.T, d_out)
+    near, far, sel = dispatch(table, expert_ids.T, gate_weights.T, d_out)
     other = swap_core(far)
     across = shift_z(near, 4)
+    *sent, near = messages(far, other, near)
     received = []
-    for k in (1, 2, 3):
-        rows = jnp.concatenate([mine[k - 1], other[192 - 64 * k : 256 - 64 * k]])
+    for k, rows in zip((1, 2, 3), sent):
         received.append(shift_z(rows, k))
 
     down_own, gate_own, up_own = w_down[0], w_gate[0], w_up[0]
@@ -425,7 +446,9 @@
     behind = shift_plane(rows, 1, True)
     near, sent_factor = lax.optimization_barrier((beside(rows, ahead, behind), sent_factor))
     factor_other = swap_core(sent_factor)
-    far = shift_plane(ahead, -1, True)
+    far_top = shift_plane(ahead[:256], -1, True)
+    far_bottom = shift_plane(behind[256:], 1, True)
+    far = jnp.concatenate([far_top, far_bottom], axis=0)
 
     behind_near = shift_plane(near, 1, False)
     ahead_near = shift_plane(near, -1, False)
@@ -457,8 +480,12 @@
     from_behind_near = shift_plane(up_near, 1, False)
     from_ahead_near = shift_plane(down_near, -1, False)
 
-    got_far = shift_plane(middle_far(own_far, from_behind_far, from_ahead_far), 1, True)
-    own, to_ahead, to_behind = middle_near(own_near, from_behind_near, from_ahead_near, got_far)
+    far_top, far_bottom = middle_far(own_far, from_behind_far, from_ahead_far)
+    got_top = shift_plane(far_top, 1, True)
+    got_bottom = shift_plane(far_bottom, -1, True)
+    own, to_ahead, to_behind = middle_near(
+        own_near, from_behind_near, from_ahead_near, got_top, got_bottom
+    )
     from_behind = shift_plane(to_ahead, 1, True)
     from_ahead = shift_plane(to_behind, -1, True)
     *back, near, across = last(own, from_behind, from_ahead)

time: 217 us -> 216 us (level)
  starting transfers between devices: 49.5 us -> 53.5 us
  other arithmetic: 3.84 us -> 1.52 us
    ppermute x18 -> x20, starting transfers between devices: 28 us -> 32.4 us  [shift_plane(): return lax.ppermute(value, ('etp', 'tp'), pairs)]
    concatenate x3 -> x0, other arithmetic: 2.43 us -> none  [body(): rows = jnp.concatenate([mine[k - 1], other[192 - 64 * k:256 - 64 * k]])]
    ppermute x8, waiting for transfers between devices: 18.4 us -> 16.1 us  [shift_z(): return lax.ppermute(value, ('expert', 'tp'), pairs)]
    ppermute x18 -> x20, waiting for transfers between devices: 71.1 us -> 69.7 us  [shift_plane(): return lax.ppermute(value, ('etp', 'tp'), pairs)]
  transfers between devices with their start and end apart: 32 -> 34, of which waited for: 17 -> 19; matrix products, arithmetic and copies ran while one was open for 1% -> 0% of each run, Pallas kernels for 7% -> 8%
where the time goes in v3:
time: 216 us; the launch traced here: 212 us
  waiting for transfers between devices  88.8 us (41%)
  starting transfers between devices  53.5 us (25%)
  blocking collectives  40.6 us (19%)
  Pallas kernels  23.9 us (11%)
  local copies, waits for them, and re-layouts  3.01 us (1%)
    ppermute x20, waiting for transfers between devices, shift_plane(): return lax.ppermute(value, ('etp', 'tp'), pairs)  69.7 us
    ppermute x20, starting transfers between devices, shift_plane(): return lax.ppermute(value, ('etp', 'tp'), pairs)  32.4 us
    all_to_all x1, blocking collectives, body(): lax.all_to_all(head_partial.reshape(16, 32, 1536), 'etp', 0, 0, tiled=True)  30.3 us
    ppermute x8, starting transfers between devices, shift_z(): return lax.ppermute(value, ('expert', 'tp'), pairs)  20 us
    ppermute x8, waiting for transfers between devices, shift_z(): return lax.ppermute(value, ('expert', 'tp'), pairs)  16.1 us
    pallas_call x3, Pallas kernels, part(): pl.pallas_call(functools.partial(part_kernel, groups, per), grid_spec=plt...  11.5 us
    all_gather x1, blocking collectives, body(): lax.all_gather(d_hidden, 'tp', axis=0, tiled=True)  10.3 us
  transfers between devices with their start and end apart: 34, of which 19 were waited for; matrix products, arithmetic and copies ran while one was open for 0% of the time, Pallas kernels for 8%

profile of v3, /device:TPU:2, one launch (start us, length us, event | category | flops | bytes accessed | tf_op | source)
XLA Modules:
  0.0 212.4 jit_solution(7881717208057819274)
XLA Ops:
  0.8 0.6 compare_select_fusion.10.table
  1.4 2.0 dispatch.1
  3.4 0.5 collective-permute-start.2
  3.8 3.0 %collective-permute-done.2.other = bf16[192,384]{1,0:T(8,128)(2,1)S(1)} collective-permute-done((bf16[192,384]{1,0:T(8,128)(2,1)}, bf16[192,384]{1,0:T(8,128)(2,1)S(1)}, u32[]{:S(2)}, u32[]{:S(2)}) %collective-permute-start.2) | collective-permute-done | bytes 147488 | tf_op jit(solution)/shard_map/ppermute | solution.py:55
  6.8 0.9 copy-done.7
  7.7 0.8 copy-done.9
  8.5 2.0 collective-permute-start.3
  10.5 3.3 %collective-permute-start.4 = (bf16[128,384]{1,0:T(8,128)(2,1)S(1)}, bf16[128,384]{1,0:T(8,128)(2,1)S(1)}, u32[]{:S(2)}, u32[]{:S(2)}) collective-permute-start(bf16[128,384]{1,0:T(8,128)(2,1)S(1)} %get-tuple-element.41), channel_id=1, source_target_pairs={{0,128},{1,131},{2,130},{3,129},{64,192},{65,195},{66,194},{67,193... | collective-permute-start | bytes 294920 | tf_op jit(solution)/shard_map/ppermute | solution.py:51
  13.8 4.0 %collective-permute-start.5 = (bf16[128,384]{1,0:T(8,128)(2,1)S(1)}, bf16[128,384]{1,0:T(8,128)(2,1)S(1)}, u32[]{:S(2)}, u32[]{:S(2)}) collective-permute-start(bf16[128,384]{1,0:T(8,128)(2,1)S(1)} %get-tuple-element.42), channel_id=1, source_target_pairs={{0,192},{1,67},{2,194},{3,65},{64,2},{65,131},{66,0},{67,129},{128... | collective-permute-start | bytes 294920 | tf_op jit(solution)/shard_map/ppermute | solution.py:51
  17.8 0.5 collective-permute-start.6
  18.4 7.8 %collective-permute-done.6.refs_4_ = bf16[64,384]{1,0:T(8,128)(2,1)S(1)} collective-permute-done((bf16[64,384]{1,0:T(8,128)(2,1)S(1)}, bf16[64,384]{1,0:T(8,128)(2,1)S(1)}, u32[]{:S(2)}, u32[]{:S(2)}) %collective-permute-start.6) | collective-permute-done | bytes 49184 | tf_op jit(solution)/shard_map/ppermute | solution.py:51
  26.3 0.6 collective-permute-start.7
  26.9 1.5 collective-permute-start.8
  28.4 0.5 collective-permute-start.1
  28.9 5.2 %collective-permute-done.7.refs_1_ = bf16[512,384]{1,0:T(8,128)(2,1)S(1)} collective-permute-done((bf16[512,384]{1,0:T(8,128)(2,1)S(1)}, bf16[512,384]{1,0:T(8,128)(2,1)S(1)}, u32[]{:S(2)}, u32[]{:S(2)}) %collective-permute-start.7) | collective-permute-done | bytes 393248 | tf_op jit(solution)/shard_map/ppermute | solution.py:41
  34.2 0.9 collective-permute-start.10
  35.1 0.4 collective-permute-done.8.refs_2_
  35.4 0.9 collective-permute-start.11
  36.4 3.5 %collective-permute-done.10 = bf16[256,384]{1,0:T(8,128)(2,1)S(1)} collective-permute-done((bf16[256,384]{1,0:T(8,128)(2,1)S(1)}, bf16[256,384]{1,0:T(8,128)(2,1)S(1)}, u32[]{:S(2)}, u32[]{:S(2)}) %collective-permute-start.10) | collective-permute-done | bytes 196640 | tf_op jit(solution)/shard_map/ppermute | solution.py:41
  39.9 2.6 %collective-permute-done.11 = bf16[256,384]{1,0:T(8,128)(2,1)S(1)} collective-permute-done((bf16[256,384]{1,0:T(8,128)(2,1)S(1)}, bf16[256,384]{1,0:T(8,128)(2,1)S(1)}, u32[]{:S(2)}, u32[]{:S(2)}) %collective-permute-start.11) | collective-permute-done | bytes 196640 | tf_op jit(solution)/shard_map/ppermute | solution.py:41
  42.5 3.2 %collective-permute-start.12 = (bf16[512,384]{1,0:T(8,128)(2,1)S(1)}, bf16[512,384]{1,0:T(8,128)(2,1)S(1)}, u32[]{:S(2)}, u32[]{:S(2)}) collective-permute-start(bf16[512,384]{1,0:T(8,128)(2,1)S(1)} %constant_dynamic-update-slice_fusion.refs_1_), channel_id=1, source_target_pairs={{0,48},{1,13},{2,50},{3,15},{4,52},{5,1},{6,54},{7,3},{8,56},{9,5}... | collective-permute-start | bytes 1179656 | tf_op jit(solution)/shard_map/ppermute | solution.py:41
  45.7 1.9 factors.1
  47.8 3.2 %collective-permute-done.12.far_a.refs_3_ = bf16[512,384]{1,0:T(8,128)(2,1)S(1)} collective-permute-done((bf16[512,384]{1,0:T(8,128)(2,1)S(1)}, bf16[512,384]{1,0:T(8,128)(2,1)S(1)}, u32[]{:S(2)}, u32[]{:S(2)}) %collective-permute-start.12) | collective-permute-done | bytes 393248 | tf_op jit(solution)/shard_map/ppermute | solution.py:41
  51.0 2.3 %collective-permute-start.13 = (bf16[512,1152]{1,0:T(8,128)(2,1)S(1)}, bf16[512,1152]{1,0:T(8,128)(2,1)S(1)}, u32[]{:S(2)}, u32[]{:S(2)}) collective-permute-start(bf16[512,1152]{1,0:T(8,128)(2,1)S(1)} %beside.1.refs_0_), channel_id=1, source_target_pairs={{0,16},{1,5},{2,18},{3,7},{4,20},{5,9},{6,22},{7,11},{8,24},{9,13}... | collective-permute-start | bytes 3538952 | tf_op jit(solution)/shard_map/ppermute | solution.py:41
  53.3 1.4 collective-permute-done.14.far_b.refs_5_
  54.7 1.2 collective-permute-start.9
  55.9 13.0 %collective-permute-done.13.near_b.refs_4_ = bf16[512,1152]{1,0:T(8,128)(2,1)S(1)} collective-permute-done((bf16[512,1152]{1,0:T(8,128)(2,1)S(1)}, bf16[512,1152]{1,0:T(8,128)(2,1)S(1)}, u32[]{:S(2)}, u32[]{:S(2)}) %collective-permute-start.13) | collective-permute-done | bytes 1179680 | tf_op jit(solution)/shard_map/ppermute | solution.py:41
  68.9 2.0 collective-permute-done.9.near_a.refs_2_
  71.0 2.5 %collective-permute-start.15 = (bf16[256,1536]{1,0:T(8,128)(2,1)S(1)}, bf16[256,1536]{1,0:T(8,128)(2,1)S(1)}, u32[]{:S(2)}, u32[]{:S(2)}) collective-permute-start(bf16[256,1536]{1,0:T(8,128)(2,1)S(1)} %get-tuple-element.46), channel_id=1, source_target_pairs={{0,48},{1,13},{2,50},{3,15},{4,52},{5,1},{6,54},{7,3},{8,56},{9,5}... | collective-permute-start | bytes 2359304 | tf_op jit(solution)/shard_map/ppermute | solution.py:41
  73.5 3.2 %act_first.1.refs_10_ = f32[512,512]{1,0:T(8,128)S(1)} custom-call(s32[34]{0:T(128)S(1)} %copy-done.10, bf16[512,1152]{1,0:T(8,128)(2,1)S(1)} %beside.1.refs_0_, bf16[512,384]{1,0:T(8,128)(2,1)S(1)} %constant_dynamic-update-slice_fusion.refs_1_, bf16[512,1152]{1,0:T(8,128)(2,1)S(1)} %collective-permute-done.9.near_a.refs_2_, ...), custom_call_target="tpu_custom_call" | custom-call | tf_op jit(solution)/shard_map/act_first/pallas_call | solution.py:209
  76.7 6.4 %collective-permute-done.15.refs_0_ = bf16[256,1536]{1,0:T(8,128)(2,1)S(1)} collective-permute-done((bf16[256,1536]{1,0:T(8,128)(2,1)S(1)}, bf16[256,1536]{1,0:T(8,128)(2,1)S(1)}, u32[]{:S(2)}, u32[]{:S(2)}) %collective-permute-start.15) | collective-permute-done | bytes 786464 | tf_op jit(solution)/shard_map/ppermute | solution.py:41
  83.1 3.6 %collective-permute-done.16.refs_1_ = bf16[256,1536]{1,0:T(8,128)(2,1)S(1)} collective-permute-done((bf16[256,1536]{1,0:T(8,128)(2,1)S(1)}, bf16[256,1536]{1,0:T(8,128)(2,1)S(1)}, u32[]{:S(2)}, u32[]{:S(2)}) %collective-permute-start.16) | collective-permute-done | bytes 786464 | tf_op jit(solution)/shard_map/ppermute | solution.py:41
  86.7 1.7 act_last.1.refs_4_.refs_8_
  88.4 0.2 copy-done.1
  88.6 1.0 copy-done.2
  89.5 3.0 %shard_map.106 = (bf16[1536,256]{1,0:T(8,128)(2,1)S(1)}, bf16[1536,256]{1,0:T(8,128)(2,1)S(1)}) custom-call(s32[34]{0:T(128)S(1)} %copy-done.10, bf16[6144,256]{1,0:T(8,128)(2,1)S(1)} %bitcast.15, bf16[6144,256]{1,0:T(8,128)(2,1)S(1)} %bitcast.16, bf16[6144,256]{1,0:T(8,128)(2,1)S(1)} %collective-permute-done.refs_1_.refs_2_.refs_3_, ...), custom_call_target="tpu_custom_call" | custom-call | tf_op jit(solution)/shard_map/pallas_call | solution.py:290
  92.7 3.2 %collective-permute-start.20 = (bf16[1536,256]{1,0:T(8,128)(2,1)S(1)}, bf16[1536,256]{1,0:T(8,128)(2,1)S(1)}, u32[]{:S(2)}, u32[]{:S(2)}) collective-permute-start(bf16[1536,256]{1,0:T(8,128)(2,1)S(1)} %get-tuple-element.56), channel_id=1, source_target_pairs={{0,48},{1,13},{2,50},{3,15},{4,52},{5,1},{6,54},{7,3},{8,56},{9,5}... | collective-permute-start | bytes 2359304 | tf_op jit(solution)/shard_map/ppermute | solution.py:41
  95.9 5.5 %shard_map.105 = (bf16[1152,512]{1,0:T(8,128)(2,1)S(1)}, bf16[384,512]{1,0:T(8,128)(2,1)S(1)}, bf16[1152,512]{1,0:T(8,128)(2,1)S(1)}, bf16[384,512]{1,0:T(8,128)(2,1)S(1)}) custom-call(s32[34]{0:T(128)S(1)} %copy-done.10, bf16[6144,256]{1,0:T(8,128)(2,1)S(1)} %bitcast.17, bf16[6144,256]{1,0:T(8,128)(2,1)S(1)} %bitcast.18, ...), custom_call_target="tpu_custom_call" | custom-call | tf_op jit(solution)/shard_map/pallas_call | solution.py:290
  101.4 4.5 %collective-permute-done.19.got_a = bf16[1536,256]{1,0:T(8,128)(2,1)S(1)} collective-permute-done((bf16[1536,256]{1,0:T(8,128)(2,1)S(1)}, bf16[1536,256]{1,0:T(8,128)(2,1)S(1)}, u32[]{:S(2)}, u32[]{:S(2)}) %collective-permute-start.19) | collective-permute-done | bytes 786464 | tf_op jit(solution)/shard_map/ppermute | solution.py:41
  105.8 0.4 add_pairs.1
  106.4 3.3 %collective-permute-start.22 = (bf16[1152,512]{1,0:T(8,128)(2,1)S(1)}, bf16[1152,512]{1,0:T(8,128)(2,1)S(1)}, u32[]{:S(2)}, u32[]{:S(2)}) collective-permute-start(bf16[1152,512]{1,0:T(8,128)(2,1)S(1)} %get-tuple-element.58), channel_id=1, source_target_pairs={{0,48},{1,13},{2,50},{3,15},{4,52},{5,1},{6,54},{7,3},{8,56},{9,5}... | collective-permute-start | bytes 3538952 | tf_op jit(solution)/shard_map/ppermute | solution.py:41
  109.7 3.2 %collective-permute-start.24 = (bf16[384,512]{1,0:T(8,128)(2,1)S(1)}, bf16[384,512]{1,0:T(8,128)(2,1)S(1)}, u32[]{:S(2)}, u32[]{:S(2)}) collective-permute-start(bf16[384,512]{1,0:T(8,128)(2,1)S(1)} %get-tuple-element.61), channel_id=1, source_target_pairs={{0,48},{1,13},{2,50},{3,15},{4,52},{5,1},{6,54},{7,3},{8,56},{9,5}... | collective-permute-start | bytes 1179656 | tf_op jit(solution)/shard_map/ppermute | solution.py:41
  112.9 3.0 %shard_map.104 = (bf16[1152,512]{1,0:T(8,128)(2,1)S(1)}, bf16[384,512]{1,0:T(8,128)(2,1)S(1)}) custom-call(s32[34]{0:T(128)S(1)} %copy-done.10, bf16[6144,256]{1,0:T(8,128)(2,1)S(1)} %bitcast.19, bf16[6144,256]{1,0:T(8,128)(2,1)S(1)} %collective-permute-done.refs_1_.refs_2_.refs_3_, bf16[6144,256]{1,0:T(8,128)(2,1)S(1)} %bitcast.25, ...), custom_call_target="tpu_custom_call" | custom-call | tf_op jit(solution)/shard_map/pallas_call | solution.py:290
  115.9 12.0 %collective-permute-done.23.got1 = bf16[384,512]{1,0:T(8,128)(2,1)S(1)} collective-permute-done((bf16[384,512]{1,0:T(8,128)(2,1)S(1)}, bf16[384,512]{1,0:T(8,128)(2,1)S(1)}, u32[]{:S(2)}, u32[]{:S(2)}) %collective-permute-start.23) | collective-permute-done | bytes 393248 | tf_op jit(solution)/shard_map/ppermute | solution.py:41
  128.1 0.3 collective-permute-start.25
  128.4 5.7 %collective-permute-start.26 = (bf16[384,256]{1,0:T(8,128)(2,1)S(1)}, bf16[384,256]{1,0:T(8,128)(2,1)S(1)}, u32[]{:S(2)}, u32[]{:S(2)}) collective-permute-start(bf16[384,256]{1,0:T(8,128)(2,1)S(1)} %get-tuple-element.63), channel_id=1, source_target_pairs={{0,12},{1,49},{2,14},{3,51},{4,0},{5,53},{6,2},{7,55},{8,4},{9,57}... | collective-permute-start | bytes 589832 | tf_op jit(solution)/shard_map/ppermute | solution.py:41
  134.1 3.6 %collective-permute-done.25.far_top = bf16[384,256]{1,0:T(8,128)(2,1)S(1)} collective-permute-done((bf16[384,256]{1,0:T(8,128)(2,1)S(1)}, bf16[384,256]{1,0:T(8,128)(2,1)S(1)}, u32[]{:S(2)}, u32[]{:S(2)}) %collective-permute-start.25) | collective-permute-done | bytes 196640 | tf_op jit(solution)/shard_map/ppermute | solution.py:41
  137.7 0.5 middle_near.1
  138.2 2.7 %collective-permute-start.27 = (bf16[384,512]{1,0:T(8,128)(2,1)S(1)}, bf16[384,512]{1,0:T(8,128)(2,1)S(1)}, u32[]{:S(2)}, u32[]{:S(2)}) collective-permute-start(bf16[384,512]{1,0:T(8,128)(2,1)S(1)} %get-tuple-element.65), channel_id=1, source_target_pairs={{0,4},{1,17},{2,6},{3,19},{4,8},{5,21},{6,10},{7,23},{8,12},{9,25}... | collective-permute-start | bytes 1179656 | tf_op jit(solution)/shard_map/ppermute | solution.py:41
  140.9 0.7 collective-permute-start.28
  141.6 5.7 %collective-permute-done.27.got1 = bf16[384,512]{1,0:T(8,128)(2,1)S(1)} collective-permute-done((bf16[384,512]{1,0:T(8,128)(2,1)S(1)}, bf16[384,512]{1,0:T(8,128)(2,1)S(1)}, u32[]{:S(2)}, u32[]{:S(2)}) %collective-permute-start.27) | collective-permute-done | bytes 393248 | tf_op jit(solution)/shard_map/ppermute | solution.py:41
  147.3 2.6 %collective-permute-done.28.got2 = bf16[384,512]{1,0:T(8,128)(2,1)S(1)} collective-permute-done((bf16[384,512]{1,0:T(8,128)(2,1)S(1)}, bf16[384,512]{1,0:T(8,128)(2,1)S(1)}, u32[]{:S(2)}, u32[]{:S(2)}) %collective-permute-start.28) | collective-permute-done | bytes 393248 | tf_op jit(solution)/shard_map/ppermute | solution.py:41
  149.9 0.2 last.1
  150.1 1.6 collective-permute-start.29
  151.8 1.5 collective-permute-start.30
  153.3 4.0 %collective-permute-start.31 = (bf16[128,384]{1,0:T(8,128)(2,1)S(1)}, bf16[128,384]{1,0:T(8,128)(2,1)S(1)}, u32[]{:S(2)}, u32[]{:S(2)}) collective-permute-start(bf16[128,384]{1,0:T(8,128)(2,1)S(1)} %get-tuple-element.69), channel_id=1, source_target_pairs={{0,66},{1,193},{2,64},{3,195},{64,130},{65,3},{66,128},{67,1},{128... | collective-permute-start | bytes 294920 | tf_op jit(solution)/shard_map/ppermute | solution.py:51
  157.3 3.2 %collective-permute-done.31.from3 = bf16[128,384]{1,0:T(8,128)(2,1)S(1)} collective-permute-done((bf16[128,384]{1,0:T(8,128)(2,1)S(1)}, bf16[128,384]{1,0:T(8,128)(2,1)S(1)}, u32[]{:S(2)}, u32[]{:S(2)}) %collective-permute-start.31) | collective-permute-done | bytes 98336 | tf_op jit(solution)/shard_map/ppermute | solution.py:51
  160.6 3.0 %collective-permute-start.33 = (bf16[64,384]{1,0:T(8,128)(2,1)S(1)}, bf16[64,384]{1,0:T(8,128)(2,1)S(1)}, u32[]{:S(2)}, u32[]{:S(2)}) collective-permute-start(bf16[64,384]{1,0:T(8,128)(2,1)S(1)} %get-tuple-element.71), channel_id=1, source_target_pairs={{0,2},{1,3},{2,0},{3,1},{64,66},{65,67},{66,64},{67,65},{128,130},... | collective-permute-start | bytes 147464 | tf_op jit(solution)/shard_map/ppermute | solution.py:51
  163.6 5.1 %collective-permute-done.33.across = bf16[64,384]{1,0:T(8,128)(2,1)S(1)} collective-permute-done((bf16[64,384]{1,0:T(8,128)(2,1)S(1)}, bf16[64,384]{1,0:T(8,128)(2,1)S(1)}, u32[]{:S(2)}, u32[]{:S(2)}) %collective-permute-start.33) | collective-permute-done | bytes 49184 | tf_op jit(solution)/shard_map/ppermute | solution.py:51
  168.7 0.9 combine.1
  169.6 10.3 %all_gather.3.tokens = bf16[512,384]{1,0:T(8,128)(2,1)S(1)} all-gather(bf16[128,384]{1,0:T(8,128)(2,1)} %combine.1), channel_id=1, replica_groups=mesh['expert'=4,'etp'=16,'tp'=4] {'tp'}, dimensions={0}, use_global_device_ids=true | all-gather | bytes 491520 | tf_op jit(solution)/shard_map/all_gather | solution.py:501
  180.0 1.2 heads.1
  181.2 30.3 %all_to_all.5 = bf16[16,32,1536]{2,1,0:T(8,128)(2,1)S(1)} all-to-all(bf16[16,32,1536]{2,1,0:T(8,128)(2,1)S(1)} %bitcast.26), channel_id=1, replica_groups=mesh['expert'=4,'etp'=16,'tp'=4] {'etp'}, dimensions={0} | all-to-all | bytes 3145728 | tf_op jit(solution)/shard_map/all_to_all | solution.py:502
  211.5 0.9 reduce_sum.12
  (55 shorter events, 1.0 us)
Async XLA Ops:
  0.6 72.9 %collective-permute-start.17 = (bf16[256,6144]{1,0:T(8,128)(2,1)}, bf16[256,6144]{1,0:T(8,128)(2,1)S(1)}, u32[]{:S(2)}, u32[]{:S(2)}) collective-permute-start(bf16[256,6144]{1,0:T(8,128)(2,1)} %bitcast.8), channel_id=1, source_target_pairs={{0,1},{1,0},{2,3},{3,2},{4,5},{5,4},{6,7},{7,6},{8,9},{9,8},{10,11... | collective-permute-start | bytes 9437192 | tf_op jit(solution)/shard_map/ppermute | solution.py:55
  3.4 3.4 %collective-permute-start.2 = (bf16[192,384]{1,0:T(8,128)(2,1)}, bf16[192,384]{1,0:T(8,128)(2,1)S(1)}, u32[]{:S(2)}, u32[]{:S(2)}) collective-permute-start(bf16[192,384]{1,0:T(8,128)(2,1)} %get-tuple-element.38.far), channel_id=1, source_target_pairs={{0,1},{1,0},{2,3},{3,2},{4,5},{5,4},{6,7},{7,6},{8,9},{9,8},{10,11... | collective-permute-start | bytes 442376 | tf_op jit(solution)/shard_map/ppermute | solution.py:55
  6.8 0.9 copy-start.7
  7.7 0.8 copy-start.9
  8.5 17.7 %collective-permute-start.3 = (bf16[128,384]{1,0:T(8,128)(2,1)S(1)}, bf16[128,384]{1,0:T(8,128)(2,1)S(1)}, u32[]{:S(2)}, u32[]{:S(2)}) collective-permute-start(bf16[128,384]{1,0:T(8,128)(2,1)S(1)} %get-tuple-element.40), channel_id=1, source_target_pairs={{0,64},{1,195},{2,66},{3,193},{64,128},{65,1},{66,130},{67,3},{128... | collective-permute-start | bytes 294920 | tf_op jit(solution)/shard_map/ppermute | solution.py:51
  10.5 15.7 %collective-permute-start.4 = (bf16[128,384]{1,0:T(8,128)(2,1)S(1)}, bf16[128,384]{1,0:T(8,128)(2,1)S(1)}, u32[]{:S(2)}, u32[]{:S(2)}) collective-permute-start(bf16[128,384]{1,0:T(8,128)(2,1)S(1)} %get-tuple-element.41), channel_id=1, source_target_pairs={{0,128},{1,131},{2,130},{3,129},{64,192},{65,195},{66,194},{67,193... | collective-permute-start | bytes 294920 | tf_op jit(solution)/shard_map/ppermute | solution.py:51
  13.8 12.4 %collective-permute-start.5 = (bf16[128,384]{1,0:T(8,128)(2,1)S(1)}, bf16[128,384]{1,0:T(8,128)(2,1)S(1)}, u32[]{:S(2)}, u32[]{:S(2)}) collective-permute-start(bf16[128,384]{1,0:T(8,128)(2,1)S(1)} %get-tuple-element.42), channel_id=1, source_target_pairs={{0,192},{1,67},{2,194},{3,65},{64,2},{65,131},{66,0},{67,129},{128... | collective-permute-start | bytes 294920 | tf_op jit(solution)/shard_map/ppermute | solution.py:51
  17.8 8.4 %collective-permute-start.6 = (bf16[64,384]{1,0:T(8,128)(2,1)S(1)}, bf16[64,384]{1,0:T(8,128)(2,1)S(1)}, u32[]{:S(2)}, u32[]{:S(2)}) collective-permute-start(bf16[64,384]{1,0:T(8,128)(2,1)S(1)} %copy-done.9), channel_id=1, source_target_pairs={{0,2},{1,3},{2,0},{3,1},{64,66},{65,67},{66,64},{67,65},{128,130},... | collective-permute-start | bytes 147464 | tf_op jit(solution)/shard_map/ppermute | solution.py:51
  26.2 19.5 %copy-start.4 = (bf16[1,1024,256]{2,1,0:T(8,128)(2,1)S(1)}, bf16[1,1024,256]{2,1,0:T(8,128)(2,1)}, u32[]{:S(2)}) copy-start(bf16[1,1024,256]{2,1,0:T(8,128)(2,1)} %param.12) | copy-start | bytes 1572868
  26.2 19.5 %copy-start.5 = (bf16[1,1024,256]{2,1,0:T(8,128)(2,1)S(1)}, bf16[1,1024,256]{2,1,0:T(8,128)(2,1)}, u32[]{:S(2)}) copy-start(bf16[1,1024,256]{2,1,0:T(8,128)(2,1)} %param.13) | copy-start | bytes 1572868
  26.2 19.5 %copy-start.10 = (s32[34]{0:T(128)S(1)}, s32[34]{0:T(128)}, u32[]{:S(2)}) copy-start(s32[34]{0:T(128)} %compare_select_fusion.10.table) | copy-start | bytes 412
  26.3 7.9 %collective-permute-start.7 = (bf16[512,384]{1,0:T(8,128)(2,1)S(1)}, bf16[512,384]{1,0:T(8,128)(2,1)S(1)}, u32[]{:S(2)}, u32[]{:S(2)}) collective-permute-start(bf16[512,384]{1,0:T(8,128)(2,1)S(1)} %pack.1.refs_0_), channel_id=1, source_target_pairs={{0,12},{1,49},{2,14},{3,51},{4,0},{5,53},{6,2},{7,55},{8,4},{9,57}... | collective-permute-start | bytes 1179656 | tf_op jit(solution)/shard_map/ppermute | solution.py:41
  26.9 8.5 %collective-permute-start.8 = (bf16[512,384]{1,0:T(8,128)(2,1)S(1)}, bf16[512,384]{1,0:T(8,128)(2,1)S(1)}, u32[]{:S(2)}, u32[]{:S(2)}) collective-permute-start(bf16[512,384]{1,0:T(8,128)(2,1)S(1)} %pack.1.refs_0_), channel_id=1, source_target_pairs={{0,4},{1,17},{2,6},{3,19},{4,8},{5,21},{6,10},{7,23},{8,12},{9,25}... | collective-permute-start | bytes 1179656 | tf_op jit(solution)/shard_map/ppermute | solution.py:41
  28.4 60.0 %collective-permute-start = (bf16[6144,256]{1,0:T(8,128)(2,1)}, bf16[6144,256]{1,0:T(8,128)(2,1)S(1)}, u32[]{:S(2)}, u32[]{:S(2)}) collective-permute-start(bf16[6144,256]{1,0:T(8,128)(2,1)} %bitcast.14), channel_id=1, source_target_pairs={{0,1},{1,0},{2,3},{3,2},{4,5},{5,4},{6,7},{7,6},{8,9},{9,8},{10,11... | collective-permute-start | bytes 9437192 | tf_op jit(solution)/shard_map/ppermute | solution.py:55
  28.4 60.0 %collective-permute-start.1 = (bf16[6144,256]{1,0:T(8,128)(2,1)}, bf16[6144,256]{1,0:T(8,128)(2,1)S(1)}, u32[]{:S(2)}, u32[]{:S(2)}) collective-permute-start(bf16[6144,256]{1,0:T(8,128)(2,1)} %bitcast.20), channel_id=1, source_target_pairs={{0,1},{1,0},{2,3},{3,2},{4,5},{5,4},{6,7},{7,6},{8,9},{9,8},{10,11... | collective-permute-start | bytes 9437192 | tf_op jit(solution)/shard_map/ppermute | solution.py:55
  34.2 5.7 %collective-permute-start.10 = (bf16[256,384]{1,0:T(8,128)(2,1)S(1)}, bf16[256,384]{1,0:T(8,128)(2,1)S(1)}, u32[]{:S(2)}, u32[]{:S(2)}) collective-permute-start(bf16[256,384]{1,0:T(8,128)(2,1)S(1)} %slice.20), channel_id=1, source_target_pairs={{0,12},{1,49},{2,14},{3,51},{4,0},{5,53},{6,2},{7,55},{8,4},{9,57}... | collective-permute-start | bytes 589832 | tf_op jit(solution)/shard_map/ppermute | solution.py:41
  35.4 7.1 %collective-permute-start.11 = (bf16[256,384]{1,0:T(8,128)(2,1)S(1)}, bf16[256,384]{1,0:T(8,128)(2,1)S(1)}, u32[]{:S(2)}, u32[]{:S(2)}) collective-permute-start(bf16[256,384]{1,0:T(8,128)(2,1)S(1)} %slice.21), channel_id=1, source_target_pairs={{0,4},{1,17},{2,6},{3,19},{4,8},{5,21},{6,10},{7,23},{8,12},{9,25}... | collective-permute-start | bytes 589832 | tf_op jit(solution)/shard_map/ppermute | solution.py:41
  42.5 8.4 %collective-permute-start.12 = (bf16[512,384]{1,0:T(8,128)(2,1)S(1)}, bf16[512,384]{1,0:T(8,128)(2,1)S(1)}, u32[]{:S(2)}, u32[]{:S(2)}) collective-permute-start(bf16[512,384]{1,0:T(8,128)(2,1)S(1)} %constant_dynamic-update-slice_fusion.refs_1_), channel_id=1, source_target_pairs={{0,48},{1,13},{2,50},{3,15},{4,52},{5,1},{6,54},{7,3},{8,56},{9,5}... | collective-permute-start | bytes 1179656 | tf_op jit(solution)/shard_map/ppermute | solution.py:41
  45.7 9.0 %collective-permute-start.14 = (bf16[512,384]{1,0:T(8,128)(2,1)S(1)}, bf16[512,384]{1,0:T(8,128)(2,1)S(1)}, u32[]{:S(2)}, u32[]{:S(2)}) collective-permute-start(bf16[512,384]{1,0:T(8,128)(2,1)S(1)} %constant_dynamic-update-slice_fusion.refs_1_), channel_id=1, source_target_pairs={{0,16},{1,5},{2,18},{3,7},{4,20},{5,9},{6,22},{7,11},{8,24},{9,13}... | collective-permute-start | bytes 1179656 | tf_op jit(solution)/shard_map/ppermute | solution.py:41
  47.8 25.7 %copy-start = (bf16[1,256,6144]{2,1,0:T(8,128)(2,1)S(1)}, bf16[1,256,6144]{2,1,0:T(8,128)(2,1)}, u32[]{:S(2)}) copy-start(bf16[1,256,6144]{2,1,0:T(8,128)(2,1)} %param.16) | copy-start | bytes 9437188
  51.0 17.9 %collective-permute-start.13 = (bf16[512,1152]{1,0:T(8,128)(2,1)S(1)}, bf16[512,1152]{1,0:T(8,128)(2,1)S(1)}, u32[]{:S(2)}, u32[]{:S(2)}) collective-permute-start(bf16[512,1152]{1,0:T(8,128)(2,1)S(1)} %beside.1.refs_0_), channel_id=1, source_target_pairs={{0,16},{1,5},{2,18},{3,7},{4,20},{5,9},{6,22},{7,11},{8,24},{9,13}... | collective-permute-start | bytes 3538952 | tf_op jit(solution)/shard_map/ppermute | solution.py:41
  54.7 16.2 %collective-permute-start.9 = (bf16[512,1152]{1,0:T(8,128)(2,1)S(1)}, bf16[512,1152]{1,0:T(8,128)(2,1)S(1)}, u32[]{:S(2)}, u32[]{:S(2)}) collective-permute-start(bf16[512,1152]{1,0:T(8,128)(2,1)S(1)} %beside.1.refs_0_), channel_id=1, source_target_pairs={{0,48},{1,13},{2,50},{3,15},{4,52},{5,1},{6,54},{7,3},{8,56},{9,5}... | collective-permute-start | bytes 3538952 | tf_op jit(solution)/shard_map/ppermute | solution.py:41
  68.9 7.8 %collective-permute-start.18 = (f32[512,512]{1,0:T(8,128)S(1)}, f32[512,512]{1,0:T(8,128)S(1)}, u32[]{:S(2)}, u32[]{:S(2)}) collective-permute-start(f32[512,512]{1,0:T(8,128)S(1)} %get-tuple-element.49), channel_id=1, source_target_pairs={{0,1},{1,0},{2,3},{3,2},{4,5},{5,4},{6,7},{7,6},{8,9},{9,8},{10,11... | collective-permute-start | bytes 3145736 | tf_op jit(solution)/shard_map/ppermute | solution.py:55
  71.0 12.1 %collective-permute-start.15 = (bf16[256,1536]{1,0:T(8,128)(2,1)S(1)}, bf16[256,1536]{1,0:T(8,128)(2,1)S(1)}, u32[]{:S(2)}, u32[]{:S(2)}) collective-permute-start(bf16[256,1536]{1,0:T(8,128)(2,1)S(1)} %get-tuple-element.46), channel_id=1, source_target_pairs={{0,48},{1,13},{2,50},{3,15},{4,52},{5,1},{6,54},{7,3},{8,56},{9,5}... | collective-permute-start | bytes 2359304 | tf_op jit(solution)/shard_map/ppermute | solution.py:41
  73.5 13.2 %collective-permute-start.16 = (bf16[256,1536]{1,0:T(8,128)(2,1)S(1)}, bf16[256,1536]{1,0:T(8,128)(2,1)S(1)}, u32[]{:S(2)}, u32[]{:S(2)}) collective-permute-start(bf16[256,1536]{1,0:T(8,128)(2,1)S(1)} %get-tuple-element.47), channel_id=1, source_target_pairs={{0,16},{1,5},{2,18},{3,7},{4,20},{5,9},{6,22},{7,11},{8,24},{9,13}... | collective-permute-start | bytes 2359304 | tf_op jit(solution)/shard_map/ppermute | solution.py:41
  86.7 1.9 copy-start.1
  86.7 2.8 %copy-start.2 = (bf16[1,6144,256]{2,1,0:T(8,128)(2,1)S(1)}, bf16[1,6144,256]{2,1,0:T(8,128)(2,1)}, u32[]{:S(2)}) copy-start(bf16[1,6144,256]{2,1,0:T(8,128)(2,1)} %param.15) | copy-start | bytes 9437188
  92.6 13.3 %collective-permute-start.19 = (bf16[1536,256]{1,0:T(8,128)(2,1)S(1)}, bf16[1536,256]{1,0:T(8,128)(2,1)S(1)}, u32[]{:S(2)}, u32[]{:S(2)}) collective-permute-start(bf16[1536,256]{1,0:T(8,128)(2,1)S(1)} %get-tuple-element.53), channel_id=1, source_target_pairs={{0,16},{1,5},{2,18},{3,7},{4,20},{5,9},{6,22},{7,11},{8,24},{9,13}... | collective-permute-start | bytes 2359304 | tf_op jit(solution)/shard_map/ppermute | solution.py:41
  92.7 13.2 %collective-permute-start.20 = (bf16[1536,256]{1,0:T(8,128)(2,1)S(1)}, bf16[1536,256]{1,0:T(8,128)(2,1)S(1)}, u32[]{:S(2)}, u32[]{:S(2)}) collective-permute-start(bf16[1536,256]{1,0:T(8,128)(2,1)S(1)} %get-tuple-element.56), channel_id=1, source_target_pairs={{0,48},{1,13},{2,50},{3,15},{4,52},{5,1},{6,54},{7,3},{8,56},{9,5}... | collective-permute-start | bytes 2359304 | tf_op jit(solution)/shard_map/ppermute | solution.py:41
  106.3 31.4 %collective-permute-start.21 = (bf16[1152,512]{1,0:T(8,128)(2,1)S(1)}, bf16[1152,512]{1,0:T(8,128)(2,1)S(1)}, u32[]{:S(2)}, u32[]{:S(2)}) collective-permute-start(bf16[1152,512]{1,0:T(8,128)(2,1)S(1)} %get-tuple-element.57), channel_id=1, source_target_pairs={{0,16},{1,5},{2,18},{3,7},{4,20},{5,9},{6,22},{7,11},{8,24},{9,13}... | collective-permute-start | bytes 3538952 | tf_op jit(solution)/shard_map/ppermute | solution.py:41
  106.4 31.3 %collective-permute-start.22 = (bf16[1152,512]{1,0:T(8,128)(2,1)S(1)}, bf16[1152,512]{1,0:T(8,128)(2,1)S(1)}, u32[]{:S(2)}, u32[]{:S(2)}) collective-permute-start(bf16[1152,512]{1,0:T(8,128)(2,1)S(1)} %get-tuple-element.58), channel_id=1, source_target_pairs={{0,48},{1,13},{2,50},{3,15},{4,52},{5,1},{6,54},{7,3},{8,56},{9,5}... | collective-permute-start | bytes 3538952 | tf_op jit(solution)/shard_map/ppermute | solution.py:41
  109.7 18.3 %collective-permute-start.23 = (bf16[384,512]{1,0:T(8,128)(2,1)S(1)}, bf16[384,512]{1,0:T(8,128)(2,1)S(1)}, u32[]{:S(2)}, u32[]{:S(2)}) collective-permute-start(bf16[384,512]{1,0:T(8,128)(2,1)S(1)} %get-tuple-element.60), channel_id=1, source_target_pairs={{0,16},{1,5},{2,18},{3,7},{4,20},{5,9},{6,22},{7,11},{8,24},{9,13}... | collective-permute-start | bytes 1179656 | tf_op jit(solution)/shard_map/ppermute | solution.py:41
  109.7 18.3 %collective-permute-start.24 = (bf16[384,512]{1,0:T(8,128)(2,1)S(1)}, bf16[384,512]{1,0:T(8,128)(2,1)S(1)}, u32[]{:S(2)}, u32[]{:S(2)}) collective-permute-start(bf16[384,512]{1,0:T(8,128)(2,1)S(1)} %get-tuple-element.61), channel_id=1, source_target_pairs={{0,48},{1,13},{2,50},{3,15},{4,52},{5,1},{6,54},{7,3},{8,56},{9,5}... | collective-permute-start | bytes 1179656 | tf_op jit(solution)/shard_map/ppermute | solution.py:41
  128.1 9.6 %collective-permute-start.25 = (bf16[384,256]{1,0:T(8,128)(2,1)S(1)}, bf16[384,256]{1,0:T(8,128)(2,1)S(1)}, u32[]{:S(2)}, u32[]{:S(2)}) collective-permute-start(bf16[384,256]{1,0:T(8,128)(2,1)S(1)} %get-tuple-element.62), channel_id=1, source_target_pairs={{0,4},{1,17},{2,6},{3,19},{4,8},{5,21},{6,10},{7,23},{8,12},{9,25}... | collective-permute-start | bytes 589832 | tf_op jit(solution)/shard_map/ppermute | solution.py:41
  128.4 9.2 %collective-permute-start.26 = (bf16[384,256]{1,0:T(8,128)(2,1)S(1)}, bf16[384,256]{1,0:T(8,128)(2,1)S(1)}, u32[]{:S(2)}, u32[]{:S(2)}) collective-permute-start(bf16[384,256]{1,0:T(8,128)(2,1)S(1)} %get-tuple-element.63), channel_id=1, source_target_pairs={{0,12},{1,49},{2,14},{3,51},{4,0},{5,53},{6,2},{7,55},{8,4},{9,57}... | collective-permute-start | bytes 589832 | tf_op jit(solution)/shard_map/ppermute | solution.py:41
  138.2 30.5 %copy-start.6 = (bf16[128,384]{1,0:T(8,128)(2,1)S(1)}, bf16[128,384]{1,0:T(8,128)(2,1)}, u32[]{:S(2)}) copy-start(bf16[128,384]{1,0:T(8,128)(2,1)} %grads.3) | copy-start | bytes 294916
  138.2 30.5 %copy-start.8 = (bf16[256,128]{1,0:T(8,128)(2,1)S(1)}, bf16[256,128]{1,0:T(8,128)(2,1)}, u32[]{:S(2)}) copy-start(bf16[256,128]{1,0:T(8,128)(2,1)} %get-tuple-element.37.sel) | copy-start | bytes 196612
  138.2 9.1 %collective-permute-start.27 = (bf16[384,512]{1,0:T(8,128)(2,1)S(1)}, bf16[384,512]{1,0:T(8,128)(2,1)S(1)}, u32[]{:S(2)}, u32[]{:S(2)}) collective-permute-start(bf16[384,512]{1,0:T(8,128)(2,1)S(1)} %get-tuple-element.65), channel_id=1, source_target_pairs={{0,4},{1,17},{2,6},{3,19},{4,8},{5,21},{6,10},{7,23},{8,12},{9,25}... | collective-permute-start | bytes 1179656 | tf_op jit(solution)/shard_map/ppermute | solution.py:41
  140.9 9.0 %collective-permute-start.28 = (bf16[384,512]{1,0:T(8,128)(2,1)S(1)}, bf16[384,512]{1,0:T(8,128)(2,1)S(1)}, u32[]{:S(2)}, u32[]{:S(2)}) collective-permute-start(bf16[384,512]{1,0:T(8,128)(2,1)S(1)} %get-tuple-element.66), channel_id=1, source_target_pairs={{0,12},{1,49},{2,14},{3,51},{4,0},{5,53},{6,2},{7,55},{8,4},{9,57}... | collective-permute-start | bytes 1179656 | tf_op jit(solution)/shard_map/ppermute | solution.py:41
  150.1 29.9 %copy-start.3 = (bf16[1536,384]{1,0:T(8,128)(2,1)S(1)}, bf16[1536,384]{1,0:T(8,128)(2,1)}, u32[]{:S(2)}) copy-start(bf16[1536,384]{1,0:T(8,128)(2,1)} %weights.1) | copy-start | bytes 3538948
  150.1 7.2 %collective-permute-start.29 = (bf16[128,384]{1,0:T(8,128)(2,1)S(1)}, bf16[128,384]{1,0:T(8,128)(2,1)S(1)}, u32[]{:S(2)}, u32[]{:S(2)}) collective-permute-start(bf16[128,384]{1,0:T(8,128)(2,1)S(1)} %get-tuple-element.67), channel_id=1, source_target_pairs={{0,194},{1,65},{2,192},{3,67},{64,0},{65,129},{66,2},{67,131},{128... | collective-permute-start | bytes 294920 | tf_op jit(solution)/shard_map/ppermute | solution.py:51
  151.8 5.6 %collective-permute-start.30 = (bf16[128,384]{1,0:T(8,128)(2,1)S(1)}, bf16[128,384]{1,0:T(8,128)(2,1)S(1)}, u32[]{:S(2)}, u32[]{:S(2)}) collective-permute-start(bf16[128,384]{1,0:T(8,128)(2,1)S(1)} %get-tuple-element.68), channel_id=1, source_target_pairs={{0,130},{1,129},{2,128},{3,131},{64,194},{65,193},{66,192},{67,195... | collective-permute-start | bytes 294920 | tf_op jit(solution)/shard_map/ppermute | solution.py:51
  153.3 7.2 %collective-permute-start.31 = (bf16[128,384]{1,0:T(8,128)(2,1)S(1)}, bf16[128,384]{1,0:T(8,128)(2,1)S(1)}, u32[]{:S(2)}, u32[]{:S(2)}) collective-permute-start(bf16[128,384]{1,0:T(8,128)(2,1)S(1)} %get-tuple-element.69), channel_id=1, source_target_pairs={{0,66},{1,193},{2,64},{3,195},{64,130},{65,3},{66,128},{67,1},{128... | collective-permute-start | bytes 294920 | tf_op jit(solution)/shard_map/ppermute | solution.py:51
  160.5 8.2 %collective-permute-start.32 = (bf16[192,384]{1,0:T(8,128)(2,1)S(1)}, bf16[192,384]{1,0:T(8,128)(2,1)S(1)}, u32[]{:S(2)}, u32[]{:S(2)}) collective-permute-start(bf16[192,384]{1,0:T(8,128)(2,1)S(1)} %pad_maximum_fusion), channel_id=1, source_target_pairs={{0,1},{1,0},{2,3},{3,2},{4,5},{5,4},{6,7},{7,6},{8,9},{9,8},{10,11... | collective-permute-start | bytes 442376 | tf_op jit(solution)/shard_map/ppermute | solution.py:55
  160.6 8.1 %collective-permute-start.33 = (bf16[64,384]{1,0:T(8,128)(2,1)S(1)}, bf16[64,384]{1,0:T(8,128)(2,1)S(1)}, u32[]{:S(2)}, u32[]{:S(2)}) collective-permute-start(bf16[64,384]{1,0:T(8,128)(2,1)S(1)} %get-tuple-element.71), channel_id=1, source_target_pairs={{0,2},{1,3},{2,0},{3,1},{64,66},{65,67},{66,64},{67,65},{128,130},... | collective-permute-start | bytes 147464 | tf_op jit(solution)/shard_map/ppermute | solution.py:51

commit v4 on v3

--- a/solution.py
+++ b/solution.py
@@ -164,21 +164,22 @@
     )(*blocks)
 
 
-def beside_kernel(*refs):
-    for k in range(3):
-        refs[3][:, 384 * k : 384 * (k + 1)] = refs[k][...]
+def beside_kernel(own, ahead, behind, top, bottom):
+    for k, ref in enumerate((own, ahead, behind)):
+        top[:, 384 * k : 384 * (k + 1)] = ref[0:256, :]
+        bottom[:, 384 * k : 384 * (k + 1)] = ref[256:512, :]
 
 
 def beside(*blocks):
     return pl.pallas_call(
-        beside_kernel, out_shape=shape((512, 1152)), name="beside", compiler_params=room(6)
+        beside_kernel, out_shape=[shape((256, 1152))] * 2, name="beside", compiler_params=room(6)
     )(*blocks)
 
 
 def halves_kernel(near_a, far_a, near_b, far_b, top, bottom):
-    top[:, 0:1152] = near_a[0:256, :]
+    top[:, 0:1152] = near_a[...]
     top[:, 1152:1536] = far_a[0:256, :]
-    bottom[:, 0:1152] = near_b[256:512, :]
+    bottom[:, 0:1152] = near_b[...]
     bottom[:, 1152:1536] = far_b[256:512, :]
 
 
@@ -189,9 +190,12 @@
 
 
 def act_first_kernel(table, *refs):
-    pieces, down_own, down_other, acc = refs[:6], refs[6], refs[7], refs[8]
+    pieces, down_own, down_other, acc = refs[:9], refs[9], refs[10], refs[11]
     for k, group in enumerate((0, 1, 3)):
-        rows = jnp.concatenate([pieces[2 * k][...], pieces[2 * k + 1][...]], axis=1)
+        top, bottom, far = pieces[3 * k : 3 * k + 3]
+        rows = jnp.concatenate(
+            [jnp.concatenate([top[...], bottom[...]], axis=0), far[...]], axis=1
+        )
         for side, down in enumerate((down_own, down_other)):
             columns = [
                 down[:, pl.ds(pl.multiple_of(table[4 * group + j] * 384, 384), 384)] for j in CHUNKS
@@ -208,7 +212,7 @@
 def act_first(table, pieces, down_own, down_other):
     return pl.pallas_call(
         act_first_kernel,
-        in_specs=[SM] + [VM] * 8,
+        in_specs=[SM] + [VM] * 11,
         out_specs=VM,
         out_shape=shape((512, 512), F32),
         name="act_first",
@@ -263,13 +267,15 @@
                 @pl.when(step == 4 // per * run + piece)
                 def _(total=total, run=run, group=group, chunk=chunk):
                     here = slice(384 * chunk, 384 * (chunk + 1))
-                    if group == 2:
-                        outs[0][here, :] = total[:, 0:256]
-                        outs[1][here, :] = total[:, 256:512]
-                    elif chunk == 3:
-                        outs[2 * run + 1][...] = total
+                    if group == 0 and chunk == 3:
+                        outs[1][...] = total
+                    elif group == 0:
+                        outs[0][here, :] = total
+                    elif group != 2 and chunk == 3:
+                        outs[3 * run + 2][...] = total
                     else:
-                        outs[2 * run][here, :] = total
+                        outs[3 * run][here, :] = total[:, 0:256]
+                        outs[3 * run + 1][here, :] = total[:, 256:512]
 
 
 def part(table, grads, weights, groups, per):
@@ -286,7 +292,12 @@
 
     dims = []
     for group in groups:
-        dims += [(1536, 256)] * 2 if group == 2 else [(1152, 512), (384, 512)]
+        if group == 2:
+            dims += [(1536, 256)] * 2
+        elif group == 0:
+            dims += [(1152, 512), (384, 512)]
+        else:
+            dims += [(1152, 256), (1152, 256), (384, 512)]
     return pl.pallas_call(
         functools.partial(part_kernel, groups, per),
         grid_spec=pltpu.PrefetchScalarGridSpec(
@@ -311,10 +322,8 @@
 def pairs_kernel(near_a, far_a, got_a, near_b, far_b, got_b, out_near_a, out_far_a, out_near_b, out_far_b):
     def some_rows(k, carry):
         here = pl.ds(pl.multiple_of(k * 128, 128), 128)
-        out_near_a[here, 0:256] = add(near_a[here, 0:256], got_a[here, :]).astype(BF)
-        out_near_a[here, 256:512] = near_a[here, 256:512]
-        out_near_b[here, 0:256] = near_b[here, 0:256]
-        out_near_b[here, 256:512] = add(near_b[here, 256:512], got_b[here, :]).astype(BF)
+        out_near_a[here, :] = add(near_a[here, :], got_a[here, :]).astype(BF)
+        out_near_b[here, :] = add(near_b[here, :], got_b[here, :]).astype(BF)
         return carry
 
     lax.fori_loop(0, 9, some_rows, 0)
@@ -327,7 +336,7 @@
 def add_pairs(*args):
     return pl.pallas_call(
         pairs_kernel,
-        out_shape=[shape((1152, 512)), shape((384, 512))] * 2,
+        out_shape=[shape((1152, 256)), shape((384, 512))] * 2,
         name="add_pairs",
         compiler_params=room(16),
     )(*args)
@@ -345,14 +354,14 @@
     )(*args)
 
 
-def near_kernel(mine, got1, got2, far_top, far_bottom, own, ahead, behind):
+def near_kernel(mine, top1, top2, bottom1, bottom2, far_top, far_bottom, own, ahead, behind):
     for k, out in enumerate((own, ahead, behind)):
 
         def some_rows(r, carry, k=k, out=out):
             to = pl.ds(pl.multiple_of(r * 128, 128), 128)
             here = pl.ds(pl.multiple_of(384 * k + r * 128, 128), 128)
-            total = add(mine[here, :], got1[here, :], got2[here, :])
-            top, bottom = total[:, 0:256], total[:, 256:512]
+            top = add(mine[here, 0:256], top1[here, :], top2[here, :])
+            bottom = add(mine[here, 256:512], bottom1[here, :], bottom2[here, :])
             if k == 1:
                 top = top + far_top[to, :].astype(F32)
             if k == 2:
@@ -444,23 +453,26 @@
     rows = pack(*received, near, across)
     ahead = shift_plane(rows, -1, True)
     behind = shift_plane(rows, 1, True)
-    near, sent_factor = lax.optimization_barrier((beside(rows, ahead, behind), sent_factor))
+    top, bottom = beside(rows, ahead, behind)
+    top, bottom, sent_factor = lax.optimization_barrier((top, bottom, sent_factor))
     factor_other = swap_core(sent_factor)
     far_top = shift_plane(ahead[:256], -1, True)
     far_bottom = shift_plane(behind[256:], 1, True)
     far = jnp.concatenate([far_top, far_bottom], axis=0)
 
-    behind_near = shift_plane(near, 1, False)
-    ahead_near = shift_plane(near, -1, False)
+    behind_bottom = shift_plane(bottom, 1, False)
+    ahead_top = shift_plane(top, -1, False)
     behind_far = shift_plane(far, 1, False)
     ahead_far = shift_plane(far, -1, False)
-    top, bottom = halves(ahead_near, ahead_far, behind_near, behind_far)
-    last_top = shift_plane(top, -1, False)
-    last_bottom = shift_plane(bottom, 1, False)
+    behind_top = shift_plane(top, 1, False)
+    ahead_bottom = shift_plane(bottom, -1, False)
+    top_on, bottom_on = halves(ahead_top, ahead_far, behind_bottom, behind_far)
+    last_top = shift_plane(top_on, -1, False)
+    last_bottom = shift_plane(bottom_on, 1, False)
 
     acc = act_first(
         table,
-        (near, far, ahead_near, ahead_far, behind_near, behind_far),
+        (top, bottom, far, ahead_top, ahead_bottom, ahead_far, behind_top, behind_bottom, behind_far),
         down_own,
         down_other,
     )
@@ -470,21 +482,31 @@
     far_top, far_bottom = part(table, grads, weights, (2,), 2)
     got_top = shift_plane(far_top, 1, False)
     got_bottom = shift_plane(far_bottom, -1, False)
-    ahead_near, ahead_far, behind_near, behind_far = part(table, grads, weights, (1, 3), 2)
+    ahead_top, ahead_bottom, ahead_far, behind_top, behind_bottom, behind_far = part(
+        table, grads, weights, (1, 3), 2
+    )
+    from_behind_bottom = shift_plane(ahead_bottom, 1, False)
+    from_ahead_top = shift_plane(behind_top, -1, False)
     own_near, own_far = part(table, grads, weights, (0,), 1)
     up_near, up_far, down_near, down_far = add_pairs(
-        ahead_near, ahead_far, got_top, behind_near, behind_far, got_bottom
+        ahead_top, ahead_far, got_top, behind_bottom, behind_far, got_bottom
     )
     from_behind_far = shift_plane(up_far, 1, False)
     from_ahead_far = shift_plane(down_far, -1, False)
-    from_behind_near = shift_plane(up_near, 1, False)
-    from_ahead_near = shift_plane(down_near, -1, False)
+    from_behind_top = shift_plane(up_near, 1, False)
+    from_ahead_bottom = shift_plane(down_near, -1, False)
 
     far_top, far_bottom = middle_far(own_far, from_behind_far, from_ahead_far)
     got_top = shift_plane(far_top, 1, True)
     got_bottom = shift_plane(far_bottom, -1, True)
     own, to_ahead, to_behind = middle_near(
-        own_near, from_behind_near, from_ahead_near, got_top, got_bottom
+        own_near,
+        from_behind_top,
+        from_ahead_top,
+        from_behind_bottom,
+        from_ahead_bottom,
+        got_top,
+        got_bottom,
     )
     from_behind = shift_plane(to_ahead, 1, True)
     from_ahead = shift_plane(to_behind, -1, True)

time: 216 us -> 215 us (level)
  waiting for transfers between devices: 88.8 us -> 77.2 us
  starting transfers between devices: 53.5 us -> 59.2 us
  local copies, waits for them, and re-layouts: 3.01 us -> 5.66 us
    ppermute x20 -> x24, waiting for transfers between devices: 69.7 us -> 57.8 us  [shift_plane(): return lax.ppermute(value, ('etp', 'tp'), pairs)]
    ppermute x20 -> x24, starting transfers between devices: 32.4 us -> 38 us  [shift_plane(): return lax.ppermute(value, ('etp', 'tp'), pairs)]
    unnamed x23, local copies, waits for them, and re-layouts: 2.92 us -> 5.57 us
  transfers between devices with their start and end apart: 34 -> 38, of which waited for: 19 -> 23; matrix products, arithmetic and copies ran while one was open for 0% -> 0% of each run, Pallas kernels for 8% -> 8%
where the time goes in v4:
time: 215 us; the launch traced here: 211 us
  waiting for transfers between devices  77.2 us (36%)
  starting transfers between devices  59.2 us (28%)
  blocking collectives  42.2 us (20%)
  Pallas kernels  23.9 us (11%)
  local copies, waits for them, and re-layouts  5.66 us (3%)
    ppermute x24, waiting for transfers between devices, shift_plane(): return lax.ppermute(value, ('etp', 'tp'), pairs)  57.8 us
    ppermute x24, starting transfers between devices, shift_plane(): return lax.ppermute(value, ('etp', 'tp'), pairs)  38 us
    all_to_all x1, blocking collectives, body(): lax.all_to_all(head_partial.reshape(16, 32, 1536), 'etp', 0, 0, tiled=True)  31.8 us
    ppermute x8, starting transfers between devices, shift_z(): return lax.ppermute(value, ('expert', 'tp'), pairs)  20.1 us
    ppermute x8, waiting for transfers between devices, shift_z(): return lax.ppermute(value, ('expert', 'tp'), pairs)  16.2 us
    pallas_call x3, Pallas kernels, part(): pl.pallas_call(functools.partial(part_kernel, groups, per), grid_spec=plt...  11.6 us
    all_gather x1, blocking collectives, body(): lax.all_gather(d_hidden, 'tp', axis=0, tiled=True)  10.3 us
    unnamed x23, local copies, waits for them, and re-layouts  5.57 us
  transfers between devices with their start and end apart: 38, of which 23 were waited for; matrix products, arithmetic and copies ran while one was open for 0% of the time, Pallas kernels for 8%

profile of v4, /device:TPU:2, one launch (start us, length us, event | category | flops | bytes accessed | tf_op | source)
XLA Modules:
  0.0 210.5 jit_solution(14984517481214697184)
XLA Ops:
  1.3 2.0 dispatch.1
  3.7 3.1 %collective-permute-done.2.other = bf16[192,384]{1,0:T(8,128)(2,1)S(1)} collective-permute-done((bf16[192,384]{1,0:T(8,128)(2,1)}, bf16[192,384]{1,0:T(8,128)(2,1)S(1)}, u32[]{:S(2)}, u32[]{:S(2)}) %collective-permute-start.2) | collective-permute-done | bytes 147488 | tf_op jit(solution)/shard_map/ppermute | solution.py:55
  6.8 0.9 copy-done.7
  7.7 0.8 copy-done.9
  8.5 2.0 collective-permute-start.3
  10.5 3.3 %collective-permute-start.4 = (bf16[128,384]{1,0:T(8,128)(2,1)S(1)}, bf16[128,384]{1,0:T(8,128)(2,1)S(1)}, u32[]{:S(2)}, u32[]{:S(2)}) collective-permute-start(bf16[128,384]{1,0:T(8,128)(2,1)S(1)} %get-tuple-element.46), channel_id=1, source_target_pairs={{0,128},{1,131},{2,130},{3,129},{64,192},{65,195},{66,194},{67,193... | collective-permute-start | bytes 294920 | tf_op jit(solution)/shard_map/ppermute | solution.py:51
  13.8 4.0 %collective-permute-start.5 = (bf16[128,384]{1,0:T(8,128)(2,1)S(1)}, bf16[128,384]{1,0:T(8,128)(2,1)S(1)}, u32[]{:S(2)}, u32[]{:S(2)}) collective-permute-start(bf16[128,384]{1,0:T(8,128)(2,1)S(1)} %get-tuple-element.47), channel_id=1, source_target_pairs={{0,192},{1,67},{2,194},{3,65},{64,2},{65,131},{66,0},{67,129},{128... | collective-permute-start | bytes 294920 | tf_op jit(solution)/shard_map/ppermute | solution.py:51
  18.4 7.8 %collective-permute-done.6.refs_4_ = bf16[64,384]{1,0:T(8,128)(2,1)S(1)} collective-permute-done((bf16[64,384]{1,0:T(8,128)(2,1)S(1)}, bf16[64,384]{1,0:T(8,128)(2,1)S(1)}, u32[]{:S(2)}, u32[]{:S(2)}) %collective-permute-start.6) | collective-permute-done | bytes 49184 | tf_op jit(solution)/shard_map/ppermute | solution.py:51
  26.3 0.6 collective-permute-start.7
  26.9 1.5 collective-permute-start.8
  28.9 5.2 %collective-permute-done.7.ahead = bf16[512,384]{1,0:T(8,128)(2,1)S(1)} collective-permute-done((bf16[512,384]{1,0:T(8,128)(2,1)S(1)}, bf16[512,384]{1,0:T(8,128)(2,1)S(1)}, u32[]{:S(2)}, u32[]{:S(2)}) %collective-permute-start.7) | collective-permute-done | bytes 393248 | tf_op jit(solution)/shard_map/ppermute | solution.py:41
  34.1 0.9 collective-permute-start.10
  35.4 0.9 collective-permute-start.11
  36.4 3.5 %collective-permute-done.10 = bf16[256,384]{1,0:T(8,128)(2,1)S(1)} collective-permute-done((bf16[256,384]{1,0:T(8,128)(2,1)S(1)}, bf16[256,384]{1,0:T(8,128)(2,1)S(1)}, u32[]{:S(2)}, u32[]{:S(2)}) %collective-permute-start.10) | collective-permute-done | bytes 196640 | tf_op jit(solution)/shard_map/ppermute | solution.py:41
  39.9 2.6 %collective-permute-done.11 = bf16[256,384]{1,0:T(8,128)(2,1)S(1)} collective-permute-done((bf16[256,384]{1,0:T(8,128)(2,1)S(1)}, bf16[256,384]{1,0:T(8,128)(2,1)S(1)}, u32[]{:S(2)}, u32[]{:S(2)}) %collective-permute-start.11) | collective-permute-done | bytes 196640 | tf_op jit(solution)/shard_map/ppermute | solution.py:41
  42.5 3.2 %collective-permute-start.12 = (bf16[512,384]{1,0:T(8,128)(2,1)S(1)}, bf16[512,384]{1,0:T(8,128)(2,1)S(1)}, u32[]{:S(2)}, u32[]{:S(2)}) collective-permute-start(bf16[512,384]{1,0:T(8,128)(2,1)S(1)} %constant_dynamic-update-slice_fusion.refs_2_), channel_id=1, source_target_pairs={{0,48},{1,13},{2,50},{3,15},{4,52},{5,1},{6,54},{7,3},{8,56},{9,5}... | collective-permute-start | bytes 1179656 | tf_op jit(solution)/shard_map/ppermute | solution.py:41
  45.7 1.0 copy-done.4
  46.7 1.0 copy-done.5
  48.3 1.9 factors.1
  50.4 0.6 collective-permute-done.12.far_a.refs_5_
  51.0 2.3 %collective-permute-start.13 = (bf16[256,1152]{1,0:T(8,128)(2,1)S(1)}, bf16[256,1152]{1,0:T(8,128)(2,1)S(1)}, u32[]{:S(2)}, u32[]{:S(2)}) collective-permute-start(bf16[256,1152]{1,0:T(8,128)(2,1)S(1)} %get-tuple-element.53.refs_1_), channel_id=1, source_target_pairs={{0,16},{1,5},{2,18},{3,7},{4,20},{5,9},{6,22},{7,11},{8,24},{9,13}... | collective-permute-start | bytes 1769480 | tf_op jit(solution)/shard_map/ppermute | solution.py:41
  53.2 1.4 collective-permute-done.14.far_b.refs_8_
  54.7 1.2 collective-permute-start.18
  55.9 6.7 %collective-permute-done.13.near_b.refs_7_ = bf16[256,1152]{1,0:T(8,128)(2,1)S(1)} collective-permute-done((bf16[256,1152]{1,0:T(8,128)(2,1)S(1)}, bf16[256,1152]{1,0:T(8,128)(2,1)S(1)}, u32[]{:S(2)}, u32[]{:S(2)}) %collective-permute-start.13) | collective-permute-done | bytes 589856 | tf_op jit(solution)/shard_map/ppermute | solution.py:41
  62.5 2.0 collective-permute-start.9
  64.5 0.6 collective-permute-start.19
  65.1 7.3 %collective-permute-done.9.near_a.refs_3_ = bf16[256,1152]{1,0:T(8,128)(2,1)S(1)} collective-permute-done((bf16[256,1152]{1,0:T(8,128)(2,1)S(1)}, bf16[256,1152]{1,0:T(8,128)(2,1)S(1)}, u32[]{:S(2)}, u32[]{:S(2)}) %collective-permute-start.9) | collective-permute-done | bytes 589856 | tf_op jit(solution)/shard_map/ppermute | solution.py:41
  72.5 3.1 %collective-permute-done.19.refs_6_ = bf16[256,1152]{1,0:T(8,128)(2,1)S(1)} collective-permute-done((bf16[256,1152]{1,0:T(8,128)(2,1)S(1)}, bf16[256,1152]{1,0:T(8,128)(2,1)S(1)}, u32[]{:S(2)}, u32[]{:S(2)}) %collective-permute-start.19) | collective-permute-done | bytes 589856 | tf_op jit(solution)/shard_map/ppermute | solution.py:41
  75.6 1.2 collective-permute-start.15
  76.8 0.8 collective-permute-start.16
  77.7 3.2 %act_first.1.refs_10_ = f32[512,512]{1,0:T(8,128)S(1)} custom-call(s32[34]{0:T(128)S(1)} %copy-done.10, bf16[256,1152]{1,0:T(8,128)(2,1)S(1)} %get-tuple-element.52.refs_0_, bf16[256,1152]{1,0:T(8,128)(2,1)S(1)} %get-tuple-element.53.refs_1_, bf16[512,384]{1,0:T(8,128)(2,1)S(1)} %constant_dynamic-update-slice_fusion.refs_2_, ...), custom_call_target="tpu_custom_call" | custom-call | tf_op jit(solution)/shard_map/act_first/pallas_call | solution.py:213
  80.9 6.8 %collective-permute-done.15.refs_0_ = bf16[256,1536]{1,0:T(8,128)(2,1)S(1)} collective-permute-done((bf16[256,1536]{1,0:T(8,128)(2,1)S(1)}, bf16[256,1536]{1,0:T(8,128)(2,1)S(1)}, u32[]{:S(2)}, u32[]{:S(2)}) %collective-permute-start.15) | collective-permute-done | bytes 786464 | tf_op jit(solution)/shard_map/ppermute | solution.py:41
  87.6 2.4 %collective-permute-done.16.refs_1_ = bf16[256,1536]{1,0:T(8,128)(2,1)S(1)} collective-permute-done((bf16[256,1536]{1,0:T(8,128)(2,1)S(1)}, bf16[256,1536]{1,0:T(8,128)(2,1)S(1)}, u32[]{:S(2)}, u32[]{:S(2)}) %collective-permute-start.16) | collective-permute-done | bytes 786464 | tf_op jit(solution)/shard_map/ppermute | solution.py:41
  90.0 1.7 act_last.1.refs_4_.refs_8_
  91.9 1.0 copy-done.2
  92.9 3.0 %shard_map.106 = (bf16[1536,256]{1,0:T(8,128)(2,1)S(1)}, bf16[1536,256]{1,0:T(8,128)(2,1)S(1)}) custom-call(s32[34]{0:T(128)S(1)} %copy-done.10, bf16[6144,256]{1,0:T(8,128)(2,1)S(1)} %bitcast.15, bf16[6144,256]{1,0:T(8,128)(2,1)S(1)} %bitcast.16, bf16[6144,256]{1,0:T(8,128)(2,1)S(1)} %collective-permute-done.refs_1_.refs_2_.refs_3_, ...), custom_call_target="tpu_custom_call" | custom-call | tf_op jit(solution)/shard_map/pallas_call | solution.py:301
  96.0 3.2 %collective-permute-start.22 = (bf16[1536,256]{1,0:T(8,128)(2,1)S(1)}, bf16[1536,256]{1,0:T(8,128)(2,1)S(1)}, u32[]{:S(2)}, u32[]{:S(2)}) collective-permute-start(bf16[1536,256]{1,0:T(8,128)(2,1)S(1)} %get-tuple-element.64), channel_id=1, source_target_pairs={{0,48},{1,13},{2,50},{3,15},{4,52},{5,1},{6,54},{7,3},{8,56},{9,5}... | collective-permute-start | bytes 2359304 | tf_op jit(solution)/shard_map/ppermute | solution.py:41
  99.2 5.5 %shard_map.105 = (bf16[1152,256]{1,0:T(8,128)(2,1)S(1)}, bf16[1152,256]{1,0:T(8,128)(2,1)S(1)}, bf16[384,512]{1,0:T(8,128)(2,1)S(1)}, bf16[1152,256]{1,0:T(8,128...) custom-call(s32[34]{0:T(128)S(1)} %copy-done.10, bf16[6144,256]{1,0:T(8,128)(2,1)S(1)} %bitcast.17, ...), custom_call_target="tpu_custom_call" | custom-call | tf_op jit(solution)/shard_map/pallas_call | solution.py:301
  104.8 4.4 %collective-permute-done.21.got_a = bf16[1536,256]{1,0:T(8,128)(2,1)S(1)} collective-permute-done((bf16[1536,256]{1,0:T(8,128)(2,1)S(1)}, bf16[1536,256]{1,0:T(8,128)(2,1)S(1)}, u32[]{:S(2)}, u32[]{:S(2)}) %collective-permute-start.21) | collective-permute-done | bytes 786464 | tf_op jit(solution)/shard_map/ppermute | solution.py:41
  109.7 3.3 %collective-permute-start.24 = (bf16[1152,256]{1,0:T(8,128)(2,1)S(1)}, bf16[1152,256]{1,0:T(8,128)(2,1)S(1)}, u32[]{:S(2)}, u32[]{:S(2)}) collective-permute-start(bf16[1152,256]{1,0:T(8,128)(2,1)S(1)} %get-tuple-element.66), channel_id=1, source_target_pairs={{0,48},{1,13},{2,50},{3,15},{4,52},{5,1},{6,54},{7,3},{8,56},{9,5}... | collective-permute-start | bytes 1769480 | tf_op jit(solution)/shard_map/ppermute | solution.py:41
  113.0 3.2 %collective-permute-start.28 = (bf16[384,512]{1,0:T(8,128)(2,1)S(1)}, bf16[384,512]{1,0:T(8,128)(2,1)S(1)}, u32[]{:S(2)}, u32[]{:S(2)}) collective-permute-start(bf16[384,512]{1,0:T(8,128)(2,1)S(1)} %get-tuple-element.71), channel_id=1, source_target_pairs={{0,48},{1,13},{2,50},{3,15},{4,52},{5,1},{6,54},{7,3},{8,56},{9,5}... | collective-permute-start | bytes 1179656 | tf_op jit(solution)/shard_map/ppermute | solution.py:41
  116.2 2.4 %collective-permute-done.27.got1 = bf16[384,512]{1,0:T(8,128)(2,1)S(1)} collective-permute-done((bf16[384,512]{1,0:T(8,128)(2,1)S(1)}, bf16[384,512]{1,0:T(8,128)(2,1)S(1)}, u32[]{:S(2)}, u32[]{:S(2)}) %collective-permute-start.27) | collective-permute-done | bytes 393248 | tf_op jit(solution)/shard_map/ppermute | solution.py:41
  118.7 2.0 collective-permute-start.26
  120.7 3.0 %shard_map.104 = (bf16[1152,512]{1,0:T(8,128)(2,1)S(1)}, bf16[384,512]{1,0:T(8,128)(2,1)S(1)}) custom-call(s32[34]{0:T(128)S(1)} %copy-done.10, bf16[6144,256]{1,0:T(8,128)(2,1)S(1)} %bitcast.19, bf16[6144,256]{1,0:T(8,128)(2,1)S(1)} %collective-permute-done.refs_1_.refs_2_.refs_3_, bf16[6144,256]{1,0:T(8,128)(2,1)S(1)} %bitcast.25, ...), custom_call_target="tpu_custom_call" | custom-call | tf_op jit(solution)/shard_map/pallas_call | solution.py:301
  123.7 0.9 collective-permute-done.28.got2
  124.9 5.7 %collective-permute-start.30 = (bf16[384,256]{1,0:T(8,128)(2,1)S(1)}, bf16[384,256]{1,0:T(8,128)(2,1)S(1)}, u32[]{:S(2)}, u32[]{:S(2)}) collective-permute-start(bf16[384,256]{1,0:T(8,128)(2,1)S(1)} %get-tuple-element.73), channel_id=1, source_target_pairs={{0,12},{1,49},{2,14},{3,51},{4,0},{5,53},{6,2},{7,55},{8,4},{9,57}... | collective-permute-start | bytes 589832 | tf_op jit(solution)/shard_map/ppermute | solution.py:41
  130.6 2.8 %collective-permute-done.23.top1 = bf16[1152,256]{1,0:T(8,128)(2,1)S(1)} collective-permute-done((bf16[1152,256]{1,0:T(8,128)(2,1)S(1)}, bf16[1152,256]{1,0:T(8,128)(2,1)S(1)}, u32[]{:S(2)}, u32[]{:S(2)}) %collective-permute-start.23) | collective-permute-done | bytes 589856 | tf_op jit(solution)/shard_map/ppermute | solution.py:41
  133.4 0.7 collective-permute-done.29.far_top
  134.7 2.7 %collective-permute-start.31 = (bf16[384,512]{1,0:T(8,128)(2,1)S(1)}, bf16[384,512]{1,0:T(8,128)(2,1)S(1)}, u32[]{:S(2)}, u32[]{:S(2)}) collective-permute-start(bf16[384,512]{1,0:T(8,128)(2,1)S(1)} %get-tuple-element.75), channel_id=1, source_target_pairs={{0,4},{1,17},{2,6},{3,19},{4,8},{5,21},{6,10},{7,23},{8,12},{9,25}... | collective-permute-start | bytes 1179656 | tf_op jit(solution)/shard_map/ppermute | solution.py:41
  137.4 2.4 %collective-permute-start.32 = (bf16[384,512]{1,0:T(8,128)(2,1)S(1)}, bf16[384,512]{1,0:T(8,128)(2,1)S(1)}, u32[]{:S(2)}, u32[]{:S(2)}) collective-permute-start(bf16[384,512]{1,0:T(8,128)(2,1)S(1)} %get-tuple-element.76), channel_id=1, source_target_pairs={{0,12},{1,49},{2,14},{3,51},{4,0},{5,53},{6,2},{7,55},{8,4},{9,57}... | collective-permute-start | bytes 1179656 | tf_op jit(solution)/shard_map/ppermute | solution.py:41
  139.7 5.7 %collective-permute-done.31.got1 = bf16[384,512]{1,0:T(8,128)(2,1)S(1)} collective-permute-done((bf16[384,512]{1,0:T(8,128)(2,1)S(1)}, bf16[384,512]{1,0:T(8,128)(2,1)S(1)}, u32[]{:S(2)}, u32[]{:S(2)}) %collective-permute-start.31) | collective-permute-done | bytes 393248 | tf_op jit(solution)/shard_map/ppermute | solution.py:41
  145.4 1.0 collective-permute-done.32.got2
  146.5 2.3 %collective-permute-start.33 = (bf16[128,384]{1,0:T(8,128)(2,1)S(1)}, bf16[128,384]{1,0:T(8,128)(2,1)S(1)}, u32[]{:S(2)}, u32[]{:S(2)}) collective-permute-start(bf16[128,384]{1,0:T(8,128)(2,1)S(1)} %get-tuple-element.77), channel_id=1, source_target_pairs={{0,194},{1,65},{2,192},{3,67},{64,0},{65,129},{66,2},{67,131},{128... | collective-permute-start | bytes 294920 | tf_op jit(solution)/shard_map/ppermute | solution.py:51
  148.8 1.5 collective-permute-start.34
  150.3 3.5 %collective-permute-start.35 = (bf16[128,384]{1,0:T(8,128)(2,1)S(1)}, bf16[128,384]{1,0:T(8,128)(2,1)S(1)}, u32[]{:S(2)}, u32[]{:S(2)}) collective-permute-start(bf16[128,384]{1,0:T(8,128)(2,1)S(1)} %get-tuple-element.79), channel_id=1, source_target_pairs={{0,66},{1,193},{2,64},{3,195},{64,130},{65,3},{66,128},{67,1},{128... | collective-permute-start | bytes 294920 | tf_op jit(solution)/shard_map/ppermute | solution.py:51
  153.9 1.6 collective-permute-done.34.from2
  155.5 1.6 collective-permute-done.35.from3
  157.3 2.9 %collective-permute-start.37 = (bf16[64,384]{1,0:T(8,128)(2,1)S(1)}, bf16[64,384]{1,0:T(8,128)(2,1)S(1)}, u32[]{:S(2)}, u32[]{:S(2)}) collective-permute-start(bf16[64,384]{1,0:T(8,128)(2,1)S(1)} %get-tuple-element.81), channel_id=1, source_target_pairs={{0,2},{1,3},{2,0},{3,1},{64,66},{65,67},{66,64},{67,65},{128,130},... | collective-permute-start | bytes 147464 | tf_op jit(solution)/shard_map/ppermute | solution.py:51
  160.2 5.2 %collective-permute-done.37.across = bf16[64,384]{1,0:T(8,128)(2,1)S(1)} collective-permute-done((bf16[64,384]{1,0:T(8,128)(2,1)S(1)}, bf16[64,384]{1,0:T(8,128)(2,1)S(1)}, u32[]{:S(2)}, u32[]{:S(2)}) %collective-permute-start.37) | collective-permute-done | bytes 49184 | tf_op jit(solution)/shard_map/ppermute | solution.py:51
  165.3 0.9 combine.1
  166.2 10.3 %all_gather.3.tokens = bf16[512,384]{1,0:T(8,128)(2,1)S(1)} all-gather(bf16[128,384]{1,0:T(8,128)(2,1)} %combine.1), channel_id=1, replica_groups=mesh['expert'=4,'etp'=16,'tp'=4] {'tp'}, dimensions={0}, use_global_device_ids=true | all-gather | bytes 491520 | tf_op jit(solution)/shard_map/all_gather | solution.py:523
  176.6 1.2 heads.1
  177.8 31.8 %all_to_all.5 = bf16[16,32,1536]{2,1,0:T(8,128)(2,1)S(1)} all-to-all(bf16[16,32,1536]{2,1,0:T(8,128)(2,1)S(1)} %bitcast.26), channel_id=1, replica_groups=mesh['expert'=4,'etp'=16,'tp'=4] {'etp'}, dimensions={0} | all-to-all | bytes 3145728 | tf_op jit(solution)/shard_map/all_to_all | solution.py:524
  209.6 0.9 reduce_sum.12
  (63 shorter events, 5.3 us)
Async XLA Ops:
  0.6 76.2 %collective-permute-start.17 = (bf16[256,6144]{1,0:T(8,128)(2,1)}, bf16[256,6144]{1,0:T(8,128)(2,1)S(1)}, u32[]{:S(2)}, u32[]{:S(2)}) collective-permute-start(bf16[256,6144]{1,0:T(8,128)(2,1)} %bitcast.8), channel_id=1, source_target_pairs={{0,1},{1,0},{2,3},{3,2},{4,5},{5,4},{6,7},{7,6},{8,9},{9,8},{10,11... | collective-permute-start | bytes 9437192 | tf_op jit(solution)/shard_map/ppermute | solution.py:55
  3.2 3.6 %collective-permute-start.2 = (bf16[192,384]{1,0:T(8,128)(2,1)}, bf16[192,384]{1,0:T(8,128)(2,1)S(1)}, u32[]{:S(2)}, u32[]{:S(2)}) collective-permute-start(bf16[192,384]{1,0:T(8,128)(2,1)} %get-tuple-element.43.far), channel_id=1, source_target_pairs={{0,1},{1,0},{2,3},{3,2},{4,5},{5,4},{6,7},{7,6},{8,9},{9,8},{10,11... | collective-permute-start | bytes 442376 | tf_op jit(solution)/shard_map/ppermute | solution.py:55
  6.8 0.9 copy-start.7
  7.7 0.8 copy-start.9
  8.5 17.7 %collective-permute-start.3 = (bf16[128,384]{1,0:T(8,128)(2,1)S(1)}, bf16[128,384]{1,0:T(8,128)(2,1)S(1)}, u32[]{:S(2)}, u32[]{:S(2)}) collective-permute-start(bf16[128,384]{1,0:T(8,128)(2,1)S(1)} %get-tuple-element.45), channel_id=1, source_target_pairs={{0,64},{1,195},{2,66},{3,193},{64,128},{65,1},{66,130},{67,3},{128... | collective-permute-start | bytes 294920 | tf_op jit(solution)/shard_map/ppermute | solution.py:51
  10.5 15.7 %collective-permute-start.4 = (bf16[128,384]{1,0:T(8,128)(2,1)S(1)}, bf16[128,384]{1,0:T(8,128)(2,1)S(1)}, u32[]{:S(2)}, u32[]{:S(2)}) collective-permute-start(bf16[128,384]{1,0:T(8,128)(2,1)S(1)} %get-tuple-element.46), channel_id=1, source_target_pairs={{0,128},{1,131},{2,130},{3,129},{64,192},{65,195},{66,194},{67,193... | collective-permute-start | bytes 294920 | tf_op jit(solution)/shard_map/ppermute | solution.py:51
  13.8 12.4 %collective-permute-start.5 = (bf16[128,384]{1,0:T(8,128)(2,1)S(1)}, bf16[128,384]{1,0:T(8,128)(2,1)S(1)}, u32[]{:S(2)}, u32[]{:S(2)}) collective-permute-start(bf16[128,384]{1,0:T(8,128)(2,1)S(1)} %get-tuple-element.47), channel_id=1, source_target_pairs={{0,192},{1,67},{2,194},{3,65},{64,2},{65,131},{66,0},{67,129},{128... | collective-permute-start | bytes 294920 | tf_op jit(solution)/shard_map/ppermute | solution.py:51
  17.8 8.4 %collective-permute-start.6 = (bf16[64,384]{1,0:T(8,128)(2,1)S(1)}, bf16[64,384]{1,0:T(8,128)(2,1)S(1)}, u32[]{:S(2)}, u32[]{:S(2)}) collective-permute-start(bf16[64,384]{1,0:T(8,128)(2,1)S(1)} %copy-done.9), channel_id=1, source_target_pairs={{0,2},{1,3},{2,0},{3,1},{64,66},{65,67},{66,64},{67,65},{128,130},... | collective-permute-start | bytes 147464 | tf_op jit(solution)/shard_map/ppermute | solution.py:51
  26.2 51.5 %copy-start = (bf16[1,256,6144]{2,1,0:T(8,128)(2,1)S(1)}, bf16[1,256,6144]{2,1,0:T(8,128)(2,1)}, u32[]{:S(2)}) copy-start(bf16[1,256,6144]{2,1,0:T(8,128)(2,1)} %param.16) | copy-start | bytes 9437188
  26.3 7.9 %collective-permute-start.7 = (bf16[512,384]{1,0:T(8,128)(2,1)S(1)}, bf16[512,384]{1,0:T(8,128)(2,1)S(1)}, u32[]{:S(2)}, u32[]{:S(2)}) collective-permute-start(bf16[512,384]{1,0:T(8,128)(2,1)S(1)} %pack.1.own), channel_id=1, source_target_pairs={{0,12},{1,49},{2,14},{3,51},{4,0},{5,53},{6,2},{7,55},{8,4},{9,57}... | collective-permute-start | bytes 1179656 | tf_op jit(solution)/shard_map/ppermute | solution.py:41
  26.9 8.5 %collective-permute-start.8 = (bf16[512,384]{1,0:T(8,128)(2,1)S(1)}, bf16[512,384]{1,0:T(8,128)(2,1)S(1)}, u32[]{:S(2)}, u32[]{:S(2)}) collective-permute-start(bf16[512,384]{1,0:T(8,128)(2,1)S(1)} %pack.1.own), channel_id=1, source_target_pairs={{0,4},{1,17},{2,6},{3,19},{4,8},{5,21},{6,10},{7,23},{8,12},{9,25}... | collective-permute-start | bytes 1179656 | tf_op jit(solution)/shard_map/ppermute | solution.py:41
  28.4 63.3 %collective-permute-start = (bf16[6144,256]{1,0:T(8,128)(2,1)}, bf16[6144,256]{1,0:T(8,128)(2,1)S(1)}, u32[]{:S(2)}, u32[]{:S(2)}) collective-permute-start(bf16[6144,256]{1,0:T(8,128)(2,1)} %bitcast.14), channel_id=1, source_target_pairs={{0,1},{1,0},{2,3},{3,2},{4,5},{5,4},{6,7},{7,6},{8,9},{9,8},{10,11... | collective-permute-start | bytes 9437192 | tf_op jit(solution)/shard_map/ppermute | solution.py:55
  28.4 63.4 %collective-permute-start.1 = (bf16[6144,256]{1,0:T(8,128)(2,1)}, bf16[6144,256]{1,0:T(8,128)(2,1)S(1)}, u32[]{:S(2)}, u32[]{:S(2)}) collective-permute-start(bf16[6144,256]{1,0:T(8,128)(2,1)} %bitcast.20), channel_id=1, source_target_pairs={{0,1},{1,0},{2,3},{3,2},{4,5},{5,4},{6,7},{7,6},{8,9},{9,8},{10,11... | collective-permute-start | bytes 9437192 | tf_op jit(solution)/shard_map/ppermute | solution.py:55
  34.1 5.7 %collective-permute-start.10 = (bf16[256,384]{1,0:T(8,128)(2,1)S(1)}, bf16[256,384]{1,0:T(8,128)(2,1)S(1)}, u32[]{:S(2)}, u32[]{:S(2)}) collective-permute-start(bf16[256,384]{1,0:T(8,128)(2,1)S(1)} %slice.20), channel_id=1, source_target_pairs={{0,12},{1,49},{2,14},{3,51},{4,0},{5,53},{6,2},{7,55},{8,4},{9,57}... | collective-permute-start | bytes 589832 | tf_op jit(solution)/shard_map/ppermute | solution.py:41
  35.4 7.1 %collective-permute-start.11 = (bf16[256,384]{1,0:T(8,128)(2,1)S(1)}, bf16[256,384]{1,0:T(8,128)(2,1)S(1)}, u32[]{:S(2)}, u32[]{:S(2)}) collective-permute-start(bf16[256,384]{1,0:T(8,128)(2,1)S(1)} %slice.21), channel_id=1, source_target_pairs={{0,4},{1,17},{2,6},{3,19},{4,8},{5,21},{6,10},{7,23},{8,12},{9,25}... | collective-permute-start | bytes 589832 | tf_op jit(solution)/shard_map/ppermute | solution.py:41
  42.5 8.4 %collective-permute-start.12 = (bf16[512,384]{1,0:T(8,128)(2,1)S(1)}, bf16[512,384]{1,0:T(8,128)(2,1)S(1)}, u32[]{:S(2)}, u32[]{:S(2)}) collective-permute-start(bf16[512,384]{1,0:T(8,128)(2,1)S(1)} %constant_dynamic-update-slice_fusion.refs_2_), channel_id=1, source_target_pairs={{0,48},{1,13},{2,50},{3,15},{4,52},{5,1},{6,54},{7,3},{8,56},{9,5}... | collective-permute-start | bytes 1179656 | tf_op jit(solution)/shard_map/ppermute | solution.py:41
  45.7 9.0 %collective-permute-start.14 = (bf16[512,384]{1,0:T(8,128)(2,1)S(1)}, bf16[512,384]{1,0:T(8,128)(2,1)S(1)}, u32[]{:S(2)}, u32[]{:S(2)}) collective-permute-start(bf16[512,384]{1,0:T(8,128)(2,1)S(1)} %constant_dynamic-update-slice_fusion.refs_2_), channel_id=1, source_target_pairs={{0,16},{1,5},{2,18},{3,7},{4,20},{5,9},{6,22},{7,11},{8,24},{9,13}... | collective-permute-start | bytes 1179656 | tf_op jit(solution)/shard_map/ppermute | solution.py:41
  45.7 1.0 copy-start.4
  46.7 1.0 copy-start.5
  47.8 0.6 copy-start.10
  51.0 11.6 %collective-permute-start.13 = (bf16[256,1152]{1,0:T(8,128)(2,1)S(1)}, bf16[256,1152]{1,0:T(8,128)(2,1)S(1)}, u32[]{:S(2)}, u32[]{:S(2)}) collective-permute-start(bf16[256,1152]{1,0:T(8,128)(2,1)S(1)} %get-tuple-element.53.refs_1_), channel_id=1, source_target_pairs={{0,16},{1,5},{2,18},{3,7},{4,20},{5,9},{6,22},{7,11},{8,24},{9,13}... | collective-permute-start | bytes 1769480 | tf_op jit(solution)/shard_map/ppermute | solution.py:41
  54.7 9.9 %collective-permute-start.18 = (bf16[256,1152]{1,0:T(8,128)(2,1)S(1)}, bf16[256,1152]{1,0:T(8,128)(2,1)S(1)}, u32[]{:S(2)}, u32[]{:S(2)}) collective-permute-start(bf16[256,1152]{1,0:T(8,128)(2,1)S(1)} %get-tuple-element.53.refs_1_), channel_id=1, source_target_pairs={{0,48},{1,13},{2,50},{3,15},{4,52},{5,1},{6,54},{7,3},{8,56},{9,5}... | collective-permute-start | bytes 1769480 | tf_op jit(solution)/shard_map/ppermute | solution.py:41
  62.5 9.9 %collective-permute-start.9 = (bf16[256,1152]{1,0:T(8,128)(2,1)S(1)}, bf16[256,1152]{1,0:T(8,128)(2,1)S(1)}, u32[]{:S(2)}, u32[]{:S(2)}) collective-permute-start(bf16[256,1152]{1,0:T(8,128)(2,1)S(1)} %get-tuple-element.52.refs_0_), channel_id=1, source_target_pairs={{0,48},{1,13},{2,50},{3,15},{4,52},{5,1},{6,54},{7,3},{8,56},{9,5}... | collective-permute-start | bytes 1769480 | tf_op jit(solution)/shard_map/ppermute | solution.py:41
  64.5 11.1 %collective-permute-start.19 = (bf16[256,1152]{1,0:T(8,128)(2,1)S(1)}, bf16[256,1152]{1,0:T(8,128)(2,1)S(1)}, u32[]{:S(2)}, u32[]{:S(2)}) collective-permute-start(bf16[256,1152]{1,0:T(8,128)(2,1)S(1)} %get-tuple-element.52.refs_0_), channel_id=1, source_target_pairs={{0,16},{1,5},{2,18},{3,7},{4,20},{5,9},{6,22},{7,11},{8,24},{9,13}... | collective-permute-start | bytes 1769480 | tf_op jit(solution)/shard_map/ppermute | solution.py:41
  72.4 8.5 %collective-permute-start.20 = (f32[512,512]{1,0:T(8,128)S(1)}, f32[512,512]{1,0:T(8,128)S(1)}, u32[]{:S(2)}, u32[]{:S(2)}) collective-permute-start(f32[512,512]{1,0:T(8,128)S(1)} %get-tuple-element.57), channel_id=1, source_target_pairs={{0,1},{1,0},{2,3},{3,2},{4,5},{5,4},{6,7},{7,6},{8,9},{9,8},{10,11... | collective-permute-start | bytes 3145736 | tf_op jit(solution)/shard_map/ppermute | solution.py:55
  75.6 12.0 %collective-permute-start.15 = (bf16[256,1536]{1,0:T(8,128)(2,1)S(1)}, bf16[256,1536]{1,0:T(8,128)(2,1)S(1)}, u32[]{:S(2)}, u32[]{:S(2)}) collective-permute-start(bf16[256,1536]{1,0:T(8,128)(2,1)S(1)} %get-tuple-element.54), channel_id=1, source_target_pairs={{0,48},{1,13},{2,50},{3,15},{4,52},{5,1},{6,54},{7,3},{8,56},{9,5}... | collective-permute-start | bytes 2359304 | tf_op jit(solution)/shard_map/ppermute | solution.py:41
  76.8 13.2 %collective-permute-start.16 = (bf16[256,1536]{1,0:T(8,128)(2,1)S(1)}, bf16[256,1536]{1,0:T(8,128)(2,1)S(1)}, u32[]{:S(2)}, u32[]{:S(2)}) collective-permute-start(bf16[256,1536]{1,0:T(8,128)(2,1)S(1)} %get-tuple-element.55), channel_id=1, source_target_pairs={{0,16},{1,5},{2,18},{3,7},{4,20},{5,9},{6,22},{7,11},{8,24},{9,13}... | collective-permute-start | bytes 2359304 | tf_op jit(solution)/shard_map/ppermute | solution.py:41
  90.0 1.9 copy-start.1
  90.0 2.8 %copy-start.2 = (bf16[1,6144,256]{2,1,0:T(8,128)(2,1)S(1)}, bf16[1,6144,256]{2,1,0:T(8,128)(2,1)}, u32[]{:S(2)}) copy-start(bf16[1,6144,256]{2,1,0:T(8,128)(2,1)} %param.15) | copy-start | bytes 9437188
  95.9 13.3 %collective-permute-start.21 = (bf16[1536,256]{1,0:T(8,128)(2,1)S(1)}, bf16[1536,256]{1,0:T(8,128)(2,1)S(1)}, u32[]{:S(2)}, u32[]{:S(2)}) collective-permute-start(bf16[1536,256]{1,0:T(8,128)(2,1)S(1)} %get-tuple-element.61), channel_id=1, source_target_pairs={{0,16},{1,5},{2,18},{3,7},{4,20},{5,9},{6,22},{7,11},{8,24},{9,13}... | collective-permute-start | bytes 2359304 | tf_op jit(solution)/shard_map/ppermute | solution.py:41
  96.0 13.2 %collective-permute-start.22 = (bf16[1536,256]{1,0:T(8,128)(2,1)S(1)}, bf16[1536,256]{1,0:T(8,128)(2,1)S(1)}, u32[]{:S(2)}, u32[]{:S(2)}) collective-permute-start(bf16[1536,256]{1,0:T(8,128)(2,1)S(1)} %get-tuple-element.64), channel_id=1, source_target_pairs={{0,48},{1,13},{2,50},{3,15},{4,52},{5,1},{6,54},{7,3},{8,56},{9,5}... | collective-permute-start | bytes 2359304 | tf_op jit(solution)/shard_map/ppermute | solution.py:41
  109.6 9.1 %collective-permute-start.27 = (bf16[384,512]{1,0:T(8,128)(2,1)S(1)}, bf16[384,512]{1,0:T(8,128)(2,1)S(1)}, u32[]{:S(2)}, u32[]{:S(2)}) collective-permute-start(bf16[384,512]{1,0:T(8,128)(2,1)S(1)} %get-tuple-element.70), channel_id=1, source_target_pairs={{0,16},{1,5},{2,18},{3,7},{4,20},{5,9},{6,22},{7,11},{8,24},{9,13}... | collective-permute-start | bytes 1179656 | tf_op jit(solution)/shard_map/ppermute | solution.py:41
  109.7 15.2 %collective-permute-start.24 = (bf16[1152,256]{1,0:T(8,128)(2,1)S(1)}, bf16[1152,256]{1,0:T(8,128)(2,1)S(1)}, u32[]{:S(2)}, u32[]{:S(2)}) collective-permute-start(bf16[1152,256]{1,0:T(8,128)(2,1)S(1)} %get-tuple-element.66), channel_id=1, source_target_pairs={{0,48},{1,13},{2,50},{3,15},{4,52},{5,1},{6,54},{7,3},{8,56},{9,5}... | collective-permute-start | bytes 1769480 | tf_op jit(solution)/shard_map/ppermute | solution.py:41
  113.0 17.6 %collective-permute-start.25 = (bf16[1152,256]{1,0:T(8,128)(2,1)S(1)}, bf16[1152,256]{1,0:T(8,128)(2,1)S(1)}, u32[]{:S(2)}, u32[]{:S(2)}) collective-permute-start(bf16[1152,256]{1,0:T(8,128)(2,1)S(1)} %get-tuple-element.67), channel_id=1, source_target_pairs={{0,16},{1,5},{2,18},{3,7},{4,20},{5,9},{6,22},{7,11},{8,24},{9,13}... | collective-permute-start | bytes 1769480 | tf_op jit(solution)/shard_map/ppermute | solution.py:41
  113.0 11.6 %collective-permute-start.28 = (bf16[384,512]{1,0:T(8,128)(2,1)S(1)}, bf16[384,512]{1,0:T(8,128)(2,1)S(1)}, u32[]{:S(2)}, u32[]{:S(2)}) collective-permute-start(bf16[384,512]{1,0:T(8,128)(2,1)S(1)} %get-tuple-element.71), channel_id=1, source_target_pairs={{0,48},{1,13},{2,50},{3,15},{4,52},{5,1},{6,54},{7,3},{8,56},{9,5}... | collective-permute-start | bytes 1179656 | tf_op jit(solution)/shard_map/ppermute | solution.py:41
  116.2 17.2 %collective-permute-start.23 = (bf16[1152,256]{1,0:T(8,128)(2,1)S(1)}, bf16[1152,256]{1,0:T(8,128)(2,1)S(1)}, u32[]{:S(2)}, u32[]{:S(2)}) collective-permute-start(bf16[1152,256]{1,0:T(8,128)(2,1)S(1)} %get-tuple-element.65), channel_id=1, source_target_pairs={{0,16},{1,5},{2,18},{3,7},{4,20},{5,9},{6,22},{7,11},{8,24},{9,13}... | collective-permute-start | bytes 1769480 | tf_op jit(solution)/shard_map/ppermute | solution.py:41
  118.7 14.7 %collective-permute-start.26 = (bf16[1152,256]{1,0:T(8,128)(2,1)S(1)}, bf16[1152,256]{1,0:T(8,128)(2,1)S(1)}, u32[]{:S(2)}, u32[]{:S(2)}) collective-permute-start(bf16[1152,256]{1,0:T(8,128)(2,1)S(1)} %get-tuple-element.68), channel_id=1, source_target_pairs={{0,48},{1,13},{2,50},{3,15},{4,52},{5,1},{6,54},{7,3},{8,56},{9,5}... | collective-permute-start | bytes 1769480 | tf_op jit(solution)/shard_map/ppermute | solution.py:41
  124.8 40.6 %copy-start.6 = (bf16[128,384]{1,0:T(8,128)(2,1)S(1)}, bf16[128,384]{1,0:T(8,128)(2,1)}, u32[]{:S(2)}) copy-start(bf16[128,384]{1,0:T(8,128)(2,1)} %grads.3) | copy-start | bytes 294916
  124.8 40.6 %copy-start.8 = (bf16[256,128]{1,0:T(8,128)(2,1)S(1)}, bf16[256,128]{1,0:T(8,128)(2,1)}, u32[]{:S(2)}) copy-start(bf16[256,128]{1,0:T(8,128)(2,1)} %get-tuple-element.42.sel) | copy-start | bytes 196612
  124.8 9.3 %collective-permute-start.29 = (bf16[384,256]{1,0:T(8,128)(2,1)S(1)}, bf16[384,256]{1,0:T(8,128)(2,1)S(1)}, u32[]{:S(2)}, u32[]{:S(2)}) collective-permute-start(bf16[384,256]{1,0:T(8,128)(2,1)S(1)} %get-tuple-element.72), channel_id=1, source_target_pairs={{0,4},{1,17},{2,6},{3,19},{4,8},{5,21},{6,10},{7,23},{8,12},{9,25}... | collective-permute-start | bytes 589832 | tf_op jit(solution)/shard_map/ppermute | solution.py:41
  124.9 9.2 %collective-permute-start.30 = (bf16[384,256]{1,0:T(8,128)(2,1)S(1)}, bf16[384,256]{1,0:T(8,128)(2,1)S(1)}, u32[]{:S(2)}, u32[]{:S(2)}) collective-permute-start(bf16[384,256]{1,0:T(8,128)(2,1)S(1)} %get-tuple-element.73), channel_id=1, source_target_pairs={{0,12},{1,49},{2,14},{3,51},{4,0},{5,53},{6,2},{7,55},{8,4},{9,57}... | collective-permute-start | bytes 589832 | tf_op jit(solution)/shard_map/ppermute | solution.py:41
  134.1 42.5 %copy-start.3 = (bf16[1536,384]{1,0:T(8,128)(2,1)S(1)}, bf16[1536,384]{1,0:T(8,128)(2,1)}, u32[]{:S(2)}) copy-start(bf16[1536,384]{1,0:T(8,128)(2,1)} %weights.1) | copy-start | bytes 3538948
  134.7 10.7 %collective-permute-start.31 = (bf16[384,512]{1,0:T(8,128)(2,1)S(1)}, bf16[384,512]{1,0:T(8,128)(2,1)S(1)}, u32[]{:S(2)}, u32[]{:S(2)}) collective-permute-start(bf16[384,512]{1,0:T(8,128)(2,1)S(1)} %get-tuple-element.75), channel_id=1, source_target_pairs={{0,4},{1,17},{2,6},{3,19},{4,8},{5,21},{6,10},{7,23},{8,12},{9,25}... | collective-permute-start | bytes 1179656 | tf_op jit(solution)/shard_map/ppermute | solution.py:41
  137.4 9.0 %collective-permute-start.32 = (bf16[384,512]{1,0:T(8,128)(2,1)S(1)}, bf16[384,512]{1,0:T(8,128)(2,1)S(1)}, u32[]{:S(2)}, u32[]{:S(2)}) collective-permute-start(bf16[384,512]{1,0:T(8,128)(2,1)S(1)} %get-tuple-element.76), channel_id=1, source_target_pairs={{0,12},{1,49},{2,14},{3,51},{4,0},{5,53},{6,2},{7,55},{8,4},{9,57}... | collective-permute-start | bytes 1179656 | tf_op jit(solution)/shard_map/ppermute | solution.py:41
  146.5 7.3 %collective-permute-start.33 = (bf16[128,384]{1,0:T(8,128)(2,1)S(1)}, bf16[128,384]{1,0:T(8,128)(2,1)S(1)}, u32[]{:S(2)}, u32[]{:S(2)}) collective-permute-start(bf16[128,384]{1,0:T(8,128)(2,1)S(1)} %get-tuple-element.77), channel_id=1, source_target_pairs={{0,194},{1,65},{2,192},{3,67},{64,0},{65,129},{66,2},{67,131},{128... | collective-permute-start | bytes 294920 | tf_op jit(solution)/shard_map/ppermute | solution.py:51
  148.8 6.7 %collective-permute-start.34 = (bf16[128,384]{1,0:T(8,128)(2,1)S(1)}, bf16[128,384]{1,0:T(8,128)(2,1)S(1)}, u32[]{:S(2)}, u32[]{:S(2)}) collective-permute-start(bf16[128,384]{1,0:T(8,128)(2,1)S(1)} %get-tuple-element.78), channel_id=1, source_target_pairs={{0,130},{1,129},{2,128},{3,131},{64,194},{65,193},{66,192},{67,195... | collective-permute-start | bytes 294920 | tf_op jit(solution)/shard_map/ppermute | solution.py:51
  150.3 6.8 %collective-permute-start.35 = (bf16[128,384]{1,0:T(8,128)(2,1)S(1)}, bf16[128,384]{1,0:T(8,128)(2,1)S(1)}, u32[]{:S(2)}, u32[]{:S(2)}) collective-permute-start(bf16[128,384]{1,0:T(8,128)(2,1)S(1)} %get-tuple-element.79), channel_id=1, source_target_pairs={{0,66},{1,193},{2,64},{3,195},{64,130},{65,3},{66,128},{67,1},{128... | collective-permute-start | bytes 294920 | tf_op jit(solution)/shard_map/ppermute | solution.py:51
  157.2 8.2 %collective-permute-start.36 = (bf16[192,384]{1,0:T(8,128)(2,1)S(1)}, bf16[192,384]{1,0:T(8,128)(2,1)S(1)}, u32[]{:S(2)}, u32[]{:S(2)}) collective-permute-start(bf16[192,384]{1,0:T(8,128)(2,1)S(1)} %pad_maximum_fusion), channel_id=1, source_target_pairs={{0,1},{1,0},{2,3},{3,2},{4,5},{5,4},{6,7},{7,6},{8,9},{9,8},{10,11... | collective-permute-start | bytes 442376 | tf_op jit(solution)/shard_map/ppermute | solution.py:55
  157.3 8.1 %collective-permute-start.37 = (bf16[64,384]{1,0:T(8,128)(2,1)S(1)}, bf16[64,384]{1,0:T(8,128)(2,1)S(1)}, u32[]{:S(2)}, u32[]{:S(2)}) collective-permute-start(bf16[64,384]{1,0:T(8,128)(2,1)S(1)} %get-tuple-element.81), channel_id=1, source_target_pairs={{0,2},{1,3},{2,0},{3,1},{64,66},{65,67},{66,64},{67,65},{128,130},... | collective-permute-start | bytes 147464 | tf_op jit(solution)/shard_map/ppermute | solution.py:51
